TPU v7x, 128 devices: a whole 4x4x4 slice. The times are simulated.
128 devices in a mesh: ax: 8 (over x, core), az: 16 (over z, y).
Axes of the slice: x: 4, y: 4, z: 4, core: 2. Of those that a mesh axis runs over, the one named last changes fastest.
Arguments:
- particles: float32 [32, 256, 128, 128], P('ax', 'az'), may hold values from -8 to 8, as said below
- counts: int32 [32, 256], P('ax', 'az'), may hold values from 48 to 128
- pair_codes: int32 [32, 256, 6], P('ax', 'az'), may hold values from 0 to 8, as said below
- contact: int32 [32, 256], P('ax', 'az'), may hold values from 0 to 511
- twist_state: float32 [512, 3], P(('ax', 'az')), may hold values from -4 to 4
- leaving_slot: int32 [32768], P(('ax', 'az')), may hold values from 0 to 8191, as said below
- leaving_dest: int32 [32768, 1], P(('ax', 'az')), may hold values from 0 to 127; in each aligned block of 256 rows (0 to 255, 256 to 511, ...) at most 4 rows name the same one
- arrival_slot: int32 [65536], P(('ax', 'az')), may hold values from 0 to 8191, as said below
Outputs:
- particles_out: float32 [32, 256, 128, 128], P('ax', 'az')
- density: float32 [32, 256, 128], P('ax', 'az')
Inputs may be any that keep to these rules, and one draw needn't show every extreme that they name: `particles`: rows 0 to 2 lie in [0, 1), row 6 in [0.02, 0.06], row 7 in [0.2, 2]. `pair_codes`: each cell's list holds 6 different codes; the first is 4, the cell itself. `leaving_slot`: the 256 slots of one device are different. `leaving_dest`: devices in mesh order, ax slowest; at most 4 of one device's 256 rows name the same device. `arrival_slot`: the 512 entries of one receiving device are different slots.
All inputs are finite; a program needn't handle non-finite values.
Results may differ from a plain program's by a relative error of at most 0.0003.
Values sent between devices are 32-bit elements; how exact they have to be, the bound alone decides.
No kernel may reach another device: no remote copies, remote signals or barrier semaphores. Data moves between devices by JAX's collectives and lax.ppermute only.
A program may use at most 192 MiB of HBM per device.

v0:
```python
import jax
import jax.numpy as jnp
from jax import lax
from jax.sharding import Mesh
from jax.sharding import PartitionSpec as P

AX = ("ax_0", "ax_1")
AX_AZ = ("ax_0", "ax_1", "az_0", "az_1")
AZ = ("az_0", "az_1")


sound_square = 1.0
wall_gain = 4.0
mix_gain = 2.0
time_step = 0.05


def extended(x, sides, width):
    for axis, dim in sides:
        devices, length = (lax.axis_size(axis), x.shape[dim])
        up = [(i, (i + 1) % devices) for i in range(devices)]
        down = [(j, i) for i, j in up]
        last = lax.slice_in_dim(x, length - width, length, axis=dim)
        leading = lax.slice_in_dim(x, 0, width, axis=dim)
        before = lax.ppermute(last, axis, up)
        after = lax.ppermute(leading, axis, down)
        x = jnp.concatenate([before, x, after], axis=dim)
    return x


def in_blocks(x, dim, devices):
    before, after = (x.shape[:dim], x.shape[dim + 1 :])
    return jnp.moveaxis(x.reshape(*before, devices, -1, *after), dim, 0)


def in_order(tiles, dim):
    dims = list(tiles.shape[1:])
    dims[dim] *= tiles.shape[0]
    return jnp.moveaxis(tiles, 0, dim).reshape(dims)


def exchange_both(x, axis, axes, splits, concats):
    sizes = [lax.axis_size(a) for a in axes]
    tiles = in_blocks(x, splits[0], sizes[0])
    tiles = jnp.moveaxis(in_blocks(tiles, splits[1] + 1, sizes[1]), 0, 1)
    inside = tiles.shape[2:]
    tiles = tiles.reshape(-1, *inside)
    tiles = lax.all_to_all(tiles, axis, split_axis=0, concat_axis=0, tiled=True)
    tiles = in_order(tiles.reshape(*sizes, *inside), concats[0] + 1)
    return in_order(tiles, concats[1])


def stacked_from(x, axes, sequence):
    tiles = x
    for k in sequence:
        tiles = lax.all_gather(tiles, axes[k])
    done = sequence[::-1]
    back = [done.index(k) for k in range(len(axes))]
    tiles = tiles.transpose(*back, *range(len(axes), tiles.ndim))
    return tiles.reshape(-1, *x.shape)


def gathered_by_axis(x, axes, sequence, dim):
    return in_order(stacked_from(x, axes, sequence), dim)


def shifts(code_list):
    return ((code_list // 3 - 1).astype(jnp.float32), (code_list % 3 - 1).astype(jnp.float32))


def neighbor_index(code_list, margin, row_width):
    first_row = lax.broadcasted_iota(jnp.int32, code_list.shape, 0)
    second_col = lax.broadcasted_iota(jnp.int32, code_list.shape, 1)
    return (
        (first_row + margin + code_list // 3 - 1) * row_width
        + second_col
        + margin
        + code_list % 3
        - 1
    )


def geometry(center, partner, shift_a, shift_z):
    diff_a = partner[..., 0, None, :] + shift_a[..., None, None] - center[..., 0, :, None]
    diff_z = partner[..., 1, None, :] + shift_z[..., None, None] - center[..., 1, :, None]
    diff_y = partner[..., 2, None, :] - center[..., 2, :, None]
    nearness = jnp.maximum(1.0 - (diff_a * diff_a + diff_z * diff_z + diff_y * diff_y), 0.0)
    return ((diff_a, diff_z, diff_y), nearness)


def density_term(nearness, partner):
    return jnp.sum(nearness * nearness * nearness * partner[..., 6, None, :], axis=-1)


def pressure_terms(density, mass):
    living = mass > 0.0
    guarded = jnp.where(living, density, 1.0)
    press_ratio = jnp.where(living, sound_square * (density - 1.0) / (guarded * guarded), 0.0)
    inverse = jnp.where(living, 1.0 / guarded, 0.0)
    return (press_ratio, inverse)


def force_terms(center, partner, offsets, nearness, press_center, press_partner, inverse_partner):
    partner_mass = partner[..., 6, None, :]
    square = nearness * nearness
    repulse = (
        partner_mass * (press_center[..., :, None] + press_partner[..., None, :]) * 6.0 * square
    )
    friction = (
        partner_mass
        * inverse_partner[..., None, :]
        * (center[..., 7, :, None] + partner[..., 7, None, :])
        * square
    )
    acceleration = -jnp.stack(
        [jnp.sum(repulse * component, axis=-1) for component in offsets], axis=-2
    )
    acceleration = (
        acceleration
        + jnp.einsum(
            "...ij,...cj->...ci", friction, partner[..., 3:6, :], precision=lax.Precision.HIGHEST
        )
        - center[..., 3:6, :] * jnp.sum(friction, axis=-1)[..., None, :]
    )
    mixing = mix_gain * partner_mass * inverse_partner[..., None, :] * square
    mixing_rate = (
        jnp.einsum(
            "...ij,...cj->...ci", mixing, partner[..., 8:, :], precision=lax.Precision.HIGHEST
        )
        - center[..., 8:, :] * jnp.sum(mixing, axis=-1)[..., None, :]
    )
    return (acceleration, mixing_rate)


def advance(center, acceleration, mixing_rate, surface):
    living = (center[..., 6, :] > 0.0).astype(jnp.float32)[..., None, :]
    wall_weight = jnp.maximum(1.0 - 3.0 * center[..., 2, :], 0.0)[..., None, :]
    wall_pull = wall_gain * wall_weight * (surface[..., :, None] - center[..., 3:6, :])
    velocity = center[..., 3:6, :] + time_step * (acceleration + wall_pull) * living
    position = center[..., 0:3, :] + time_step * velocity
    species = center[..., 8:, :] + time_step * mixing_rate * living
    return jnp.concatenate([position, velocity, center[..., 6:8, :], species], axis=-2)


def clear_ends(padded, layers):
    axial = lax.axis_index(AX)
    row_iota = lax.broadcasted_iota(jnp.int32, (padded.shape[0],) + (1,) * (padded.ndim - 1), 0)
    low_edge = jnp.logical_and(axial == 0, row_iota < layers)
    high_edge = jnp.logical_and(
        axial == lax.axis_size(AX) - 1, row_iota >= padded.shape[0] - layers
    )
    return jnp.where(jnp.logical_or(low_edge, high_edge), jnp.zeros_like(padded), padded)


def finish(current, partners, partner_press, shift_a, shift_z, press_center, surface):
    grid_rows, grid_cols, fields, block_size = current.shape
    acceleration = jnp.zeros((grid_rows, grid_cols, 3, block_size), jnp.float32)
    mixing_rate = jnp.zeros((grid_rows, grid_cols, fields - 8, block_size), jnp.float32)
    for member in range(len(partners)):
        offsets, nearness = geometry(
            current, partners[member], shift_a[:, :, member], shift_z[:, :, member]
        )
        accel_part, mixing_part = force_terms(
            current,
            partners[member],
            offsets,
            nearness,
            press_center,
            partner_press[member][:, :, 0, :],
            partner_press[member][:, :, 1, :],
        )
        acceleration = acceleration + accel_part
        mixing_rate = mixing_rate + mixing_part
    return advance(current, acceleration, mixing_rate, surface)


def rim_step(current, pair_codes, surface):
    grid_rows, grid_cols, fields, block_size = current.shape
    padded = clear_ends(extended(current, ((AX, 0), (AZ, 1)), 1), 1)
    flat_cells = padded.reshape(-1, fields, block_size)
    partner_index = neighbor_index(pair_codes, 1, grid_cols + 2)
    shift_a, shift_z = shifts(pair_codes)
    partners = [flat_cells[partner_index[:, :, member]] for member in range(pair_codes.shape[2])]
    density = jnp.zeros((grid_rows, grid_cols, block_size), jnp.float32)
    for member in range(pair_codes.shape[2]):
        nearness = geometry(
            current, partners[member], shift_a[:, :, member], shift_z[:, :, member]
        )[1]
        density = density + density_term(nearness, partners[member])
    press_ratio, inverse = pressure_terms(density, current[:, :, 6, :])
    rim_values = extended(jnp.stack([press_ratio, inverse], axis=2), ((AX, 0), (AZ, 1)), 1)
    flat_pressure = clear_ends(rim_values, 1).reshape(-1, 2, block_size)
    pressure_rows = [
        flat_pressure[partner_index[:, :, member]] for member in range(pair_codes.shape[2])
    ]
    advanced = finish(current, partners, pressure_rows, shift_a, shift_z, press_ratio, surface)
    living = (current[:, :, 6, :] > 0.0).astype(jnp.float32)
    return (advanced, density * living)


def migrate(current, leaving_slot, leaving_dest, arrival_slot):
    grid_rows, grid_cols, fields, block_size = current.shape
    cell_count = grid_rows * grid_cols
    cells = current.reshape(cell_count, fields, block_size)
    ranks_total = lax.axis_size(AX) * lax.axis_size(AZ)
    capacity = arrival_slot.shape[0] // ranks_total
    source_cell = leaving_slot // block_size
    source_pos = leaving_slot % block_size
    moving = cells[source_cell, :, source_pos]
    dest_rank = leaving_dest[:, 0]
    onehot = (dest_rank[:, None] == lax.broadcasted_iota(jnp.int32, (1, ranks_total), 1)).astype(
        jnp.int32
    )
    before = jnp.cumsum(onehot, axis=0) - onehot
    dest_order = jnp.sum(before * onehot, axis=1)
    buffer_row = dest_rank * capacity + dest_order
    outgoing = jnp.zeros((ranks_total * capacity, fields), jnp.float32).at[buffer_row].set(moving)
    present = jnp.zeros((ranks_total * capacity,), jnp.int32).at[buffer_row].set(1)
    axial_count = lax.axis_size(AX)
    sector_count = lax.axis_size(AZ)
    incoming, arrived = (
        exchange_both(
            outgoing.reshape(axial_count, sector_count, capacity, fields),
            AX_AZ,
            (AX, AZ),
            (0, 1),
            (0, 1),
        ),
        exchange_both(
            present.reshape(axial_count, sector_count, capacity), AX_AZ, (AX, AZ), (0, 1), (0, 1)
        ),
    )
    target = jnp.where(arrived.reshape(-1) > 0, arrival_slot, cell_count * block_size)
    cells = cells.at[source_cell, :, source_pos].set(0.0)
    cells = cells.at[target // block_size, :, target % block_size].set(
        incoming.reshape(-1, fields), mode="drop"
    )
    return cells.reshape(grid_rows, grid_cols, fields, block_size)


def local(
    particles, counts, pair_codes, contact, twist_state, leaving_slot, leaving_dest, arrival_slot
):
    grid_rows, grid_cols, fields, block_size = particles.shape
    slot_iota = lax.broadcasted_iota(jnp.int32, (grid_rows, grid_cols, block_size), 2)
    keep_mask = (slot_iota < counts[:, :, None]).astype(jnp.float32)
    current = particles * keep_mask[:, :, None, :]
    segments = gathered_by_axis(twist_state, AX_AZ, (0, 2, 3, 1), 0)
    surface = segments[contact]
    density = jnp.zeros((grid_rows, grid_cols, block_size), jnp.float32)
    for repeat in range(2):
        if repeat == 1:
            current = migrate(current, leaving_slot, leaving_dest, arrival_slot)
        current, density = rim_step(current, pair_codes, surface)
    return (current, density)


def solution(mesh):
    finer = Mesh(mesh.devices.reshape(4, 2, 4, 4), ("ax_0", "ax_1", "az_0", "az_1"))
    return jax.shard_map(
        local,
        mesh=finer,
        in_specs=(
            P(AX, AZ, None, None),
            P(AX, AZ),
            P(AX, AZ, None),
            P(AX, AZ),
            P(AX_AZ, None),
            P(AX_AZ),
            P(AX_AZ, None),
            P(AX_AZ),
        ),
        out_specs=(P(AX, AZ, None, None), P(AX, AZ, None)),
        check_vma=False,
    )
```

profile of v0, /device:TPU:1, one launch (start us, length us, event | category | flops | bytes accessed | tf_op | source)
XLA Modules:
  0.0 874.1 jit_solution(12806782325444402581)
XLA Ops:
  12.6 10.6 %all-to-all-start = ((s32[128,1,1,4]{3,2,1,0:T(1,128)}), s32[128,1,1,4]{3,2,1,0:T(1,128)S(1)}, u32[]{:S(2)}, u32[]{:S(2)}) async-start(s32[128,1,1,4]{3,2,1,0:T(1,128)} %bitcast.117), calls=%async_computation | async-start | bytes 131072 | tf_op jit(solution)/shard_map/all_to_all | solution.py:48
  35.7 7.0 collective-permute-done.2
  100.6 11.5 %fusion.3 = (f32[4,16,128]{2,1,0:T(8,128)S(1)}, f32[4,16,128]{2,1,0:T(8,128)S(1)}, f32[4,16,128]{2,1,0:T(8,128)S(1)}, f32[4,16,128]{2,1,0:T(8,128)S(1)}) fusion(f32[4,16,128]{2,1,0:T(8,128)S(1)} %bitcast.598, f32[4,16,128]{2,1,0:T(8,128)S(1)} %bitcast.550, f32[4,16,128]{2,1,0:T(8,128)S(1)} %bitcast.554, f32[4,16,128]{2,1,0:T(8,128)S(1)} %bitcast.546, ...), kind=kLoop, calls=%fused_computation.157 | loop fusion | flops 58687488 | bytes 753664 | tf_op jit(solution)/shard_map/reduce_sum | solution.py:92
  115.8 8.1 all-gather.4
  123.9 9.2 %all-gather.1 = f32[16,4,3]{2,1,0:T(4,128)S(1)} all-gather(f32[4,4,3]{2,1,0:T(4,128)S(1)} %all-gather.4), channel_id=3, replica_groups=mesh['ax_0'=4,'ax_1'=2,'az_0'=4,'az_1'=4] {'az_0'}, dimensions={0}, use_global_device_ids=true | all-gather | bytes 960 | tf_op jit(solution)/shard_map/all_gather | solution.py:56
  133.3 9.3 %all-gather.2 = f32[16,4,4,3]{2,1,3,0:T(4,128)S(1)} all-gather(f32[4,4,4,3]{2,1,3,0:T(4,128)S(1)} %copy.53), channel_id=4, replica_groups=mesh['ax_0'=4,'ax_1'=2,'az_0'=4,'az_1'=4] {'az_1'}, dimensions={0}, use_global_device_ids=true | all-gather | bytes 3840 | tf_op jit(solution)/shard_map/all_gather | solution.py:56
  143.6 11.0 %all-gather.3 = f32[8,4,4,4,3]{3,2,4,1,0:T(4,128)S(1)} all-gather(f32[4,4,4,4,3]{3,2,4,1,0:T(4,128)S(1)} %bitcast.492), channel_id=5, replica_groups=mesh['ax_0'=4,'ax_1'=2,'az_0'=4,'az_1'=4] {'ax_1'}, dimensions={0}, use_global_device_ids=true | all-gather | bytes 9216 | tf_op jit(solution)/shard_map/all_gather | solution.py:56
  174.1 12.1 %fusion.130 = f32[4,16,120,128]{3,2,1,0:T(8,128)S(1)} fusion(f32[4,16,128,128]{3,2,1,0:T(8,128)} %bitcast.304, f32[4,16,128]{2,1,0:T(8,128)S(1)} %bitcast.736, f32[4,16,128]{2,1,0:T(8,128)S(1)} %bitcast.364, f32[4,16,128]{2,1,0:T(8,128)S(1)} %bitcast.607, f32[4,16,128]{2,1,0:T(8,128)S(1)} %bitcast.384, f32[4,16,128]{2,1,0:T(8,128)S(1)} %bitcast.611, ...), kind=kOutput, calls=%fused_computation.286 | convolution fusion | flops 1522532352 | bytes 8093696 | tf_op jit(solution)/shard_map/...ij,...cj->...ci/dot_general | solution.py:127
  186.2 13.1 %fusion.128 = f32[4,16,120,128]{3,2,1,0:T(8,128)S(1)} fusion(f32[4,16,128,128]{3,2,1,0:T(8,128)S(1)} %bitcast.332, f32[4,16,128]{2,1,0:T(8,128)S(1)} %bitcast.754, f32[4,16,128]{2,1,0:T(8,128)S(1)} %bitcast.551, f32[4,16,128]{2,1,0:T(8,128)S(1)} %bitcast.555, f32[4,16,128]{2,1,0:T(8,128)S(1)} %bitcast.547, f32[4,16,128]{2,1,0:T(8,128)S(1)} %bitcast.365, ...), kind=kOutput, calls=%fused_computation.284 | convolution fusion | flops 1522532352 | bytes 8093696 | tf_op jit(solution)/shard_map/...ij,...cj->...ci/dot_general | solution.py:127
  199.3 13.1 %fusion.126 = f32[4,16,120,128]{3,2,1,0:T(8,128)S(1)} fusion(f32[4,16,128,128]{3,2,1,0:T(8,128)S(1)} %bitcast.324, f32[4,16,128]{2,1,0:T(8,128)S(1)} %bitcast.748, f32[4,16,128]{2,1,0:T(8,128)S(1)} %bitcast.635, f32[4,16,128]{2,1,0:T(8,128)S(1)} %bitcast.639, f32[4,16,128]{2,1,0:T(8,128)S(1)} %bitcast.631, f32[4,16,128]{2,1,0:T(8,128)S(1)} %bitcast.366, ...), kind=kOutput, calls=%fused_computation.282 | convolution fusion | flops 1522532352 | bytes 8093696 | tf_op jit(solution)/shard_map/...ij,...cj->...ci/dot_general | solution.py:127
  212.5 11.5 %fusion.124 = f32[4,16,120,128]{3,2,1,0:T(8,128)} fusion(f32[4,16,128,128]{3,2,1,0:T(8,128)S(1)} %bitcast.316, f32[4,16,128]{2,1,0:T(8,128)S(1)} %bitcast.742, f32[4,16,128]{2,1,0:T(8,128)S(1)} %bitcast.539, f32[4,16,128]{2,1,0:T(8,128)S(1)} %bitcast.543, f32[4,16,128]{2,1,0:T(8,128)S(1)} %bitcast.535, f32[4,16,128]{2,1,0:T(8,128)S(1)} %bitcast.367, ...), kind=kOutput, calls=%fused_computation.280 | convolution fusion | flops 1522532352 | bytes 8093696 | tf_op jit(solution)/shard_map/...ij,...cj->...ci/dot_general | solution.py:127
  224.0 11.5 %fusion.122 = f32[4,16,120,128]{3,2,1,0:T(8,128)} fusion(f32[4,16,128,128]{3,2,1,0:T(8,128)S(1)} %bitcast.312, f32[4,16,128]{2,1,0:T(8,128)S(1)} %bitcast.730, f32[4,16,128]{2,1,0:T(8,128)S(1)} %bitcast.525, f32[4,16,128]{2,1,0:T(8,128)S(1)} %bitcast.529, f32[4,16,128]{2,1,0:T(8,128)S(1)} %bitcast.521, f32[4,16,128]{2,1,0:T(8,128)S(1)} %bitcast.368, ...), kind=kOutput, calls=%fused_computation.278 | convolution fusion | flops 1522532352 | bytes 8093696 | tf_op jit(solution)/shard_map/...ij,...cj->...ci/dot_general | solution.py:127
  235.5 13.1 %fusion.146 = (f32[4,16,128]{2,1,0:T(8,128)S(1)}, f32[4,16,128]{2,1,0:T(8,128)S(1)}, f32[4,16,128]{2,1,0:T(8,128)S(1)}, f32[4,16,128]{2,1,0:T(8,128)S(1)}, f32[4,16,128]{2,1,0:T(8,128)S(1)}) fusion(f32[4,16,128]{2,1,0:T(8,128)S(1)} %bitcast.724, f32[4,16,128]{2,1,0:T(8,128)S(1)} %bitcast.722, f32[4,16,128]{2,1,0:T(8,128)S(1)} %bitcast.462, ...), kind=kLoop, calls=%fused_computation.304 | loop fusion | flops 28270592 | bytes 589824 | tf_op jit(solution)/shard_map/reduce_sum | solution.py:123
  248.6 13.2 %fusion.148 = (f32[4,16,128]{2,1,0:T(8,128)S(1)}, f32[4,16,128]{2,1,0:T(8,128)S(1)}, f32[4,16,128]{2,1,0:T(8,128)S(1)}, f32[4,16,128]{2,1,0:T(8,128)S(1)}, f32[4,16,128]{2,1,0:T(8,128)S(1)}) fusion(f32[4,16,128]{2,1,0:T(8,128)S(1)} %bitcast.716, f32[4,16,128]{2,1,0:T(8,128)S(1)} %bitcast.714, f32[4,16,128]{2,1,0:T(8,128)S(1)} %bitcast.463, ...), kind=kLoop, calls=%fused_computation.306 | loop fusion | flops 28270592 | bytes 589824 | tf_op jit(solution)/shard_map/reduce_sum | solution.py:123
  261.8 13.2 %fusion.150 = (f32[4,16,128]{2,1,0:T(8,128)S(1)}, f32[4,16,128]{2,1,0:T(8,128)S(1)}, f32[4,16,128]{2,1,0:T(8,128)S(1)}, f32[4,16,128]{2,1,0:T(8,128)S(1)}, f32[4,16,128]{2,1,0:T(8,128)S(1)}) fusion(f32[4,16,128]{2,1,0:T(8,128)S(1)} %bitcast.708, f32[4,16,128]{2,1,0:T(8,128)S(1)} %bitcast.706, f32[4,16,128]{2,1,0:T(8,128)S(1)} %bitcast.464, ...), kind=kLoop, calls=%fused_computation.308 | loop fusion | flops 28270592 | bytes 589824 | tf_op jit(solution)/shard_map/reduce_sum | solution.py:123
  275.0 13.2 %fusion.152 = (f32[4,16,128]{2,1,0:T(8,128)S(1)}, f32[4,16,128]{2,1,0:T(8,128)S(1)}, f32[4,16,128]{2,1,0:T(8,128)S(1)}, f32[4,16,128]{2,1,0:T(8,128)S(1)}, f32[4,16,128]{2,1,0:T(8,128)S(1)}) fusion(f32[4,16,128]{2,1,0:T(8,128)S(1)} %bitcast.700, f32[4,16,128]{2,1,0:T(8,128)S(1)} %bitcast.698, f32[4,16,128]{2,1,0:T(8,128)S(1)} %bitcast.465, ...), kind=kLoop, calls=%fused_computation.310 | loop fusion | flops 28270592 | bytes 589824 | tf_op jit(solution)/shard_map/reduce_sum | solution.py:123
  288.1 13.2 %fusion.144 = (f32[4,16,128]{2,1,0:T(8,128)S(1)}, f32[4,16,128]{2,1,0:T(8,128)S(1)}, f32[4,16,128]{2,1,0:T(8,128)S(1)}, f32[4,16,128]{2,1,0:T(8,128)S(1)}, f32[4,16,128]{2,1,0:T(8,128)S(1)}) fusion(f32[4,16,128]{2,1,0:T(8,128)S(1)} %bitcast.682, f32[4,16,128]{2,1,0:T(8,128)S(1)} %bitcast.466, f32[4,16,128]{2,1,0:T(8,128)S(1)} %bitcast.680, ...), kind=kLoop, calls=%fused_computation.302 | loop fusion | flops 28270592 | bytes 589824 | tf_op jit(solution)/shard_map/reduce_sum | solution.py:123
  301.3 12.9 %fusion.457 = f32[4,16,3,128]{3,2,1,0:T(4,128)S(1)} fusion(f32[4,16,128]{2,1,0:T(8,128)S(1)} %bitcast.725, f32[4,16,128]{2,1,0:T(8,128)S(1)} %bitcast.723, f32[4,16,128]{2,1,0:T(8,128)S(1)} %bitcast.467, f32[4,16,128]{2,1,0:T(8,128)S(1)} %bitcast.553, f32[4,16,128]{2,1,0:T(8,128)S(1)} %bitcast.557, f32[4,16,128]{2,1,0:T(8,128)S(1)} %bitcast.549, ...), kind=kOutput, calls=%fused_computation.588 | convolution fusion | flops 52576256 | bytes 786432 | tf_op jit(solution)/shard_map/...ij,...cj->...ci/dot_general | solution.py:120
  314.2 12.9 %fusion.458 = f32[4,16,3,128]{3,2,1,0:T(4,128)S(1)} fusion(f32[4,16,128]{2,1,0:T(8,128)S(1)} %bitcast.717, f32[4,16,128]{2,1,0:T(8,128)S(1)} %bitcast.715, f32[4,16,128]{2,1,0:T(8,128)S(1)} %bitcast.468, f32[4,16,128]{2,1,0:T(8,128)S(1)} %bitcast.637, f32[4,16,128]{2,1,0:T(8,128)S(1)} %bitcast.641, f32[4,16,128]{2,1,0:T(8,128)S(1)} %bitcast.633, ...), kind=kOutput, calls=%fused_computation.589 | convolution fusion | flops 52576256 | bytes 786432 | tf_op jit(solution)/shard_map/...ij,...cj->...ci/dot_general | solution.py:120
  327.1 12.9 %fusion.459 = f32[4,16,3,128]{3,2,1,0:T(4,128)S(1)} fusion(f32[4,16,128]{2,1,0:T(8,128)S(1)} %bitcast.709, f32[4,16,128]{2,1,0:T(8,128)S(1)} %bitcast.707, f32[4,16,128]{2,1,0:T(8,128)S(1)} %bitcast.469, f32[4,16,128]{2,1,0:T(8,128)S(1)} %bitcast.541, f32[4,16,128]{2,1,0:T(8,128)S(1)} %bitcast.545, f32[4,16,128]{2,1,0:T(8,128)S(1)} %bitcast.537, ...), kind=kOutput, calls=%fused_computation.590 | convolution fusion | flops 52576256 | bytes 786432 | tf_op jit(solution)/shard_map/...ij,...cj->...ci/dot_general | solution.py:120
  340.1 13.3 %fusion.460 = f32[4,16,3,128]{3,2,1,0:T(4,128)S(1)} fusion(f32[4,16,128]{2,1,0:T(8,128)S(1)} %bitcast.701, f32[4,16,128]{2,1,0:T(8,128)S(1)} %bitcast.699, f32[4,16,128]{2,1,0:T(8,128)S(1)} %bitcast.470, f32[4,16,128]{2,1,0:T(8,128)S(1)} %bitcast.527, f32[4,16,128]{2,1,0:T(8,128)S(1)} %bitcast.531, f32[4,16,128]{2,1,0:T(8,128)S(1)} %bitcast.523, ...), kind=kOutput, calls=%fused_computation.591 | convolution fusion | flops 52576256 | bytes 786432 | tf_op jit(solution)/shard_map/...ij,...cj->...ci/dot_general | solution.py:120
  353.4 13.2 %fusion.154 = (f32[4,16,128]{2,1,0:T(8,128)S(1)}, f32[4,16,128]{2,1,0:T(8,128)S(1)}, f32[4,16,128]{2,1,0:T(8,128)S(1)}, f32[4,16,128]{2,1,0:T(8,128)S(1)}, f32[4,16,128]{2,1,0:T(8,128)S(1)}) fusion(f32[4,16,128]{2,1,0:T(8,128)S(1)} %bitcast.690, f32[4,16,128]{2,1,0:T(8,128)S(1)} %bitcast.688, f32[4,16,128]{2,1,0:T(8,128)S(1)} %bitcast.471, ...), kind=kLoop, calls=%fused_computation.312 | loop fusion | flops 28270592 | bytes 589824 | tf_op jit(solution)/shard_map/reduce_sum | solution.py:123
  366.6 12.9 %fusion.461 = f32[4,16,3,128]{3,2,1,0:T(4,128)S(1)} fusion(f32[4,16,128]{2,1,0:T(8,128)S(1)} %bitcast.691, f32[4,16,128]{2,1,0:T(8,128)S(1)} %bitcast.689, f32[4,16,128]{2,1,0:T(8,128)S(1)} %bitcast.472, f32[4,16,128]{2,1,0:T(8,128)S(1)} %bitcast.500, f32[4,16,128]{2,1,0:T(8,128)S(1)} %bitcast.504, f32[4,16,128]{2,1,0:T(8,128)S(1)} %bitcast.496, ...), kind=kOutput, calls=%fused_computation.592 | convolution fusion | flops 52576256 | bytes 786432 | tf_op jit(solution)/shard_map/...ij,...cj->...ci/dot_general | solution.py:120
  379.5 12.3 %slice_add_fusion.1 = (f32[4,16,3,128]{3,2,1,0:T(4,128)S(1)}, f32[4,16,3,128]{3,2,1,0:T(4,128)S(1)}) fusion(f32[4,16,128,128]{3,2,1,0:T(8,128)S(1)} %copy-done.1, f32[4,16,128]{2,1,0:T(8,128)S(1)} %bitcast.762, f32[4,16,3]{2,1,0:T(8,128)S(1)} %bitcast.760, f32[4,16,128]{2,1,0:T(8,128)S(1)} %bitcast.766, f32[4,16,3,128]{3,2,1,0:T(4,128)S(1)} %fusion.461, ...), kind=kOutput, calls=%fused_computation.630 | convolution fusion | flops 52871168 | bytes 1508096 | tf_op jit(solution)/shard_map/...ij,...cj->...ci/dot_general | solution.py:120
  391.8 13.6 %multiply_add_fusion.1 = f32[4,16,120,128]{3,2,1,0:T(8,128)S(1)} fusion(f32[4,16,120,128]{3,2,1,0:T(8,128)} %fusion.122, f32[4,16,120,128]{3,2,1,0:T(8,128)S(1)} %copy-done.25, f32[4,16,120,128]{3,2,1,0:T(8,128)S(1)} %fusion.126, f32[4,16,120,128]{3,2,1,0:T(8,128)S(1)} %fusion.128, f32[4,16,120,128]{3,2,1,0:T(8,128)S(1)} %fusion.130, ...), kind=kOutput, calls=%fused_computation.289 | convolution fusion | flops 1541210112 | bytes 31916032 | tf_op jit(solution)/shard_map/...ij,...cj->...ci/dot_general | solution.py:127
  417.4 9.7 %all-to-all-start.1 = ((f32[128,1,1,4,128]{4,3,2,1,0:T(4,128)}), f32[128,1,1,4,128]{4,3,2,1,0:T(4,128)S(1)}, u32[]{:S(2)}, u32[]{:S(2)}) async-start(f32[128,1,1,4,128]{4,3,2,1,0:T(4,128)} %bitcast.125), calls=%async_computation.1 | async-start | bytes 524288 | tf_op jit(solution)/shard_map/all_to_all | solution.py:48
  427.2 25.9 %scatter_fusion = f32[64,128,128]{1,2,0:T(8,128)} fusion(f32[64,128,128]{1,2,0:T(8,128)} %copy.58, s32[256]{0:T(256)S(1)} %bitcast.292, f32[256,128]{1,0:T(8,128)S(1)} %broadcast.395), kind=kCustom, calls=%fused_computation.26 | custom fusion | bytes 395264 | tf_op jit(solution)/shard_map/scatter | solution.py:234
  453.1 57.5 %scatter_fusion.1 = f32[64,128,128]{1,2,0:T(8,128)} fusion(f32[64,128,128]{1,2,0:T(8,128)} %scatter_fusion, s32[512]{0:T(512)S(1)} %bitcast.291, f32[512,128]{1,0:T(8,128)S(1)} %bitcast.486), kind=kCustom, calls=%fused_computation.29 | custom fusion | bytes 790528 | tf_op jit(solution)/shard_map/scatter | solution.py:235
  519.9 11.7 %collective-permute-done.8 = f32[1,16,128,128]{3,2,1,0:T(8,128)S(1)} collective-permute-done((f32[1,16,128,128]{3,2,1,0:T(8,128)S(1)}, f32[1,16,128,128]{3,2,1,0:T(8,128)S(1)}, u32[]{:S(2)}, u32[]{:S(2)}) %collective-permute-start.8) | collective-permute-done | bytes 1048608 | tf_op jit(solution)/shard_map/ppermute | solution.py:25
  603.5 11.5 %fusion.15 = (f32[4,16,128]{2,1,0:T(8,128)S(1)}, f32[4,16,128]{2,1,0:T(8,128)S(1)}, f32[4,16,128]{2,1,0:T(8,128)S(1)}, f32[4,16,128]{2,1,0:T(8,128)S(1)}) fusion(f32[4,16,128]{2,1,0:T(8,128)S(1)} %bitcast.604, f32[4,16,128]{2,1,0:T(8,128)S(1)} %bitcast.586, f32[4,16,128]{2,1,0:T(8,128)S(1)} %bitcast.590, f32[4,16,128]{2,1,0:T(8,128)S(1)} %bitcast.582, ...), kind=kLoop, calls=%fused_computation.169 | loop fusion | flops 58687488 | bytes 753664 | tf_op jit(solution)/shard_map/reduce_sum | solution.py:92
  639.7 12.3 %fusion.118 = f32[4,16,120,128]{3,2,1,0:T(8,128)S(1)} fusion(f32[4,16,128,128]{3,2,1,0:T(8,128)} %bitcast.308, f32[4,16,128]{2,1,0:T(8,128)S(1)} %bitcast.739, f32[4,16,128]{2,1,0:T(8,128)S(1)} %bitcast.424, f32[4,16,128]{2,1,0:T(8,128)S(1)} %bitcast.619, f32[4,16,128]{2,1,0:T(8,128)S(1)} %bitcast.444, f32[4,16,128]{2,1,0:T(8,128)S(1)} %bitcast.623, ...), kind=kOutput, calls=%fused_computation.274 | convolution fusion | flops 1522532352 | bytes 8093696 | tf_op jit(solution)/shard_map/...ij,...cj->...ci/dot_general | solution.py:127
  652.0 13.1 %fusion.116 = f32[4,16,120,128]{3,2,1,0:T(8,128)S(1)} fusion(f32[4,16,128,128]{3,2,1,0:T(8,128)S(1)} %bitcast.340, f32[4,16,128]{2,1,0:T(8,128)S(1)} %bitcast.757, f32[4,16,128]{2,1,0:T(8,128)S(1)} %bitcast.587, f32[4,16,128]{2,1,0:T(8,128)S(1)} %bitcast.591, f32[4,16,128]{2,1,0:T(8,128)S(1)} %bitcast.583, f32[4,16,128]{2,1,0:T(8,128)S(1)} %bitcast.425, ...), kind=kOutput, calls=%fused_computation.272 | convolution fusion | flops 1522532352 | bytes 8093696 | tf_op jit(solution)/shard_map/...ij,...cj->...ci/dot_general | solution.py:127
  665.1 13.1 %fusion.114 = f32[4,16,120,128]{3,2,1,0:T(8,128)S(1)} fusion(f32[4,16,128,128]{3,2,1,0:T(8,128)S(1)} %bitcast.336, f32[4,16,128]{2,1,0:T(8,128)S(1)} %bitcast.751, f32[4,16,128]{2,1,0:T(8,128)S(1)} %bitcast.649, f32[4,16,128]{2,1,0:T(8,128)S(1)} %bitcast.653, f32[4,16,128]{2,1,0:T(8,128)S(1)} %bitcast.645, f32[4,16,128]{2,1,0:T(8,128)S(1)} %bitcast.426, ...), kind=kOutput, calls=%fused_computation.270 | convolution fusion | flops 1522532352 | bytes 8093696 | tf_op jit(solution)/shard_map/...ij,...cj->...ci/dot_general | solution.py:127
  678.2 11.5 %fusion.112 = f32[4,16,120,128]{3,2,1,0:T(8,128)} fusion(f32[4,16,128,128]{3,2,1,0:T(8,128)S(1)} %bitcast.328, f32[4,16,128]{2,1,0:T(8,128)S(1)} %bitcast.745, f32[4,16,128]{2,1,0:T(8,128)S(1)} %bitcast.563, f32[4,16,128]{2,1,0:T(8,128)S(1)} %bitcast.567, f32[4,16,128]{2,1,0:T(8,128)S(1)} %bitcast.559, f32[4,16,128]{2,1,0:T(8,128)S(1)} %bitcast.427, ...), kind=kOutput, calls=%fused_computation.268 | convolution fusion | flops 1522532352 | bytes 8093696 | tf_op jit(solution)/shard_map/...ij,...cj->...ci/dot_general | solution.py:127
  689.8 11.5 %fusion.110 = f32[4,16,120,128]{3,2,1,0:T(8,128)} fusion(f32[4,16,128,128]{3,2,1,0:T(8,128)S(1)} %bitcast.320, f32[4,16,128]{2,1,0:T(8,128)S(1)} %bitcast.733, f32[4,16,128]{2,1,0:T(8,128)S(1)} %bitcast.575, f32[4,16,128]{2,1,0:T(8,128)S(1)} %bitcast.579, f32[4,16,128]{2,1,0:T(8,128)S(1)} %bitcast.571, f32[4,16,128]{2,1,0:T(8,128)S(1)} %bitcast.428, ...), kind=kOutput, calls=%fused_computation.266 | convolution fusion | flops 1522532352 | bytes 8093696 | tf_op jit(solution)/shard_map/...ij,...cj->...ci/dot_general | solution.py:127
  701.3 13.1 %fusion.158 = (f32[4,16,128]{2,1,0:T(8,128)S(1)}, f32[4,16,128]{2,1,0:T(8,128)S(1)}, f32[4,16,128]{2,1,0:T(8,128)S(1)}, f32[4,16,128]{2,1,0:T(8,128)S(1)}, f32[4,16,128]{2,1,0:T(8,128)S(1)}) fusion(f32[4,16,128]{2,1,0:T(8,128)S(1)} %bitcast.728, f32[4,16,128]{2,1,0:T(8,128)S(1)} %bitcast.726, f32[4,16,128]{2,1,0:T(8,128)S(1)} %bitcast.474, ...), kind=kLoop, calls=%fused_computation.316 | loop fusion | flops 28270592 | bytes 589824 | tf_op jit(solution)/shard_map/reduce_sum | solution.py:123
  714.4 13.2 %fusion.160 = (f32[4,16,128]{2,1,0:T(8,128)S(1)}, f32[4,16,128]{2,1,0:T(8,128)S(1)}, f32[4,16,128]{2,1,0:T(8,128)S(1)}, f32[4,16,128]{2,1,0:T(8,128)S(1)}, f32[4,16,128]{2,1,0:T(8,128)S(1)}) fusion(f32[4,16,128]{2,1,0:T(8,128)S(1)} %bitcast.720, f32[4,16,128]{2,1,0:T(8,128)S(1)} %bitcast.718, f32[4,16,128]{2,1,0:T(8,128)S(1)} %bitcast.475, ...), kind=kLoop, calls=%fused_computation.318 | loop fusion | flops 28270592 | bytes 589824 | tf_op jit(solution)/shard_map/reduce_sum | solution.py:123
  727.6 13.2 %fusion.162 = (f32[4,16,128]{2,1,0:T(8,128)S(1)}, f32[4,16,128]{2,1,0:T(8,128)S(1)}, f32[4,16,128]{2,1,0:T(8,128)S(1)}, f32[4,16,128]{2,1,0:T(8,128)S(1)}, f32[4,16,128]{2,1,0:T(8,128)S(1)}) fusion(f32[4,16,128]{2,1,0:T(8,128)S(1)} %bitcast.712, f32[4,16,128]{2,1,0:T(8,128)S(1)} %bitcast.710, f32[4,16,128]{2,1,0:T(8,128)S(1)} %bitcast.476, ...), kind=kLoop, calls=%fused_computation.320 | loop fusion | flops 28270592 | bytes 589824 | tf_op jit(solution)/shard_map/reduce_sum | solution.py:123
  740.7 13.2 %fusion.164 = (f32[4,16,128]{2,1,0:T(8,128)S(1)}, f32[4,16,128]{2,1,0:T(8,128)S(1)}, f32[4,16,128]{2,1,0:T(8,128)S(1)}, f32[4,16,128]{2,1,0:T(8,128)S(1)}, f32[4,16,128]{2,1,0:T(8,128)S(1)}) fusion(f32[4,16,128]{2,1,0:T(8,128)S(1)} %bitcast.704, f32[4,16,128]{2,1,0:T(8,128)S(1)} %bitcast.702, f32[4,16,128]{2,1,0:T(8,128)S(1)} %bitcast.477, ...), kind=kLoop, calls=%fused_computation.322 | loop fusion | flops 28270592 | bytes 589824 | tf_op jit(solution)/shard_map/reduce_sum | solution.py:123
  753.9 13.2 %fusion.156 = (f32[4,16,128]{2,1,0:T(8,128)S(1)}, f32[4,16,128]{2,1,0:T(8,128)S(1)}, f32[4,16,128]{2,1,0:T(8,128)S(1)}, f32[4,16,128]{2,1,0:T(8,128)S(1)}, f32[4,16,128]{2,1,0:T(8,128)S(1)}) fusion(f32[4,16,128]{2,1,0:T(8,128)S(1)} %bitcast.686, f32[4,16,128]{2,1,0:T(8,128)S(1)} %bitcast.478, f32[4,16,128]{2,1,0:T(8,128)S(1)} %bitcast.684, ...), kind=kLoop, calls=%fused_computation.314 | loop fusion | flops 28270592 | bytes 589824 | tf_op jit(solution)/shard_map/reduce_sum | solution.py:123
  767.1 12.9 %fusion.471 = f32[4,16,3,128]{3,2,1,0:T(4,128)S(1)} fusion(f32[4,16,128]{2,1,0:T(8,128)S(1)} %bitcast.729, f32[4,16,128]{2,1,0:T(8,128)S(1)} %bitcast.727, f32[4,16,128]{2,1,0:T(8,128)S(1)} %bitcast.479, f32[4,16,128]{2,1,0:T(8,128)S(1)} %bitcast.589, f32[4,16,128]{2,1,0:T(8,128)S(1)} %bitcast.593, f32[4,16,128]{2,1,0:T(8,128)S(1)} %bitcast.585, ...), kind=kOutput, calls=%fused_computation.602 | convolution fusion | flops 52576256 | bytes 786432 | tf_op jit(solution)/shard_map/...ij,...cj->...ci/dot_general | solution.py:120
  780.0 12.9 %fusion.472 = f32[4,16,3,128]{3,2,1,0:T(4,128)S(1)} fusion(f32[4,16,128]{2,1,0:T(8,128)S(1)} %bitcast.721, f32[4,16,128]{2,1,0:T(8,128)S(1)} %bitcast.719, f32[4,16,128]{2,1,0:T(8,128)S(1)} %bitcast.480, f32[4,16,128]{2,1,0:T(8,128)S(1)} %bitcast.651, f32[4,16,128]{2,1,0:T(8,128)S(1)} %bitcast.655, f32[4,16,128]{2,1,0:T(8,128)S(1)} %bitcast.647, ...), kind=kOutput, calls=%fused_computation.603 | convolution fusion | flops 52576256 | bytes 786432 | tf_op jit(solution)/shard_map/...ij,...cj->...ci/dot_general | solution.py:120
  792.9 12.9 %fusion.473 = f32[4,16,3,128]{3,2,1,0:T(4,128)S(1)} fusion(f32[4,16,128]{2,1,0:T(8,128)S(1)} %bitcast.713, f32[4,16,128]{2,1,0:T(8,128)S(1)} %bitcast.711, f32[4,16,128]{2,1,0:T(8,128)S(1)} %bitcast.481, f32[4,16,128]{2,1,0:T(8,128)S(1)} %bitcast.565, f32[4,16,128]{2,1,0:T(8,128)S(1)} %bitcast.569, f32[4,16,128]{2,1,0:T(8,128)S(1)} %bitcast.561, ...), kind=kOutput, calls=%fused_computation.604 | convolution fusion | flops 52576256 | bytes 786432 | tf_op jit(solution)/shard_map/...ij,...cj->...ci/dot_general | solution.py:120
  805.9 13.2 %fusion.474 = f32[4,16,3,128]{3,2,1,0:T(4,128)S(1)} fusion(f32[4,16,128]{2,1,0:T(8,128)S(1)} %bitcast.705, f32[4,16,128]{2,1,0:T(8,128)S(1)} %bitcast.703, f32[4,16,128]{2,1,0:T(8,128)S(1)} %bitcast.482, f32[4,16,128]{2,1,0:T(8,128)S(1)} %bitcast.577, f32[4,16,128]{2,1,0:T(8,128)S(1)} %bitcast.581, f32[4,16,128]{2,1,0:T(8,128)S(1)} %bitcast.573, ...), kind=kOutput, calls=%fused_computation.605 | convolution fusion | flops 52576256 | bytes 786432 | tf_op jit(solution)/shard_map/...ij,...cj->...ci/dot_general | solution.py:120
  819.0 13.2 %fusion.166 = (f32[4,16,128]{2,1,0:T(8,128)S(1)}, f32[4,16,128]{2,1,0:T(8,128)S(1)}, f32[4,16,128]{2,1,0:T(8,128)S(1)}, f32[4,16,128]{2,1,0:T(8,128)S(1)}, f32[4,16,128]{2,1,0:T(8,128)S(1)}) fusion(f32[4,16,128]{2,1,0:T(8,128)S(1)} %bitcast.695, f32[4,16,128]{2,1,0:T(8,128)S(1)} %bitcast.693, f32[4,16,128]{2,1,0:T(8,128)S(1)} %bitcast.483, ...), kind=kLoop, calls=%fused_computation.324 | loop fusion | flops 28270592 | bytes 589824 | tf_op jit(solution)/shard_map/reduce_sum | solution.py:123
  832.2 12.9 %fusion.475 = f32[4,16,3,128]{3,2,1,0:T(4,128)S(1)} fusion(f32[4,16,128]{2,1,0:T(8,128)S(1)} %bitcast.696, f32[4,16,128]{2,1,0:T(8,128)S(1)} %bitcast.694, f32[4,16,128]{2,1,0:T(8,128)S(1)} %bitcast.484, f32[4,16,128]{2,1,0:T(8,128)S(1)} %bitcast.512, f32[4,16,128]{2,1,0:T(8,128)S(1)} %bitcast.516, f32[4,16,128]{2,1,0:T(8,128)S(1)} %bitcast.508, ...), kind=kOutput, calls=%fused_computation.606 | convolution fusion | flops 52576256 | bytes 786432 | tf_op jit(solution)/shard_map/...ij,...cj->...ci/dot_general | solution.py:120
  845.1 12.3 %slice_add_fusion = (f32[4,16,3,128]{3,2,1,0:T(4,128)S(1)}, f32[4,16,3,128]{3,2,1,0:T(4,128)S(1)}) fusion(f32[4,16,128,128]{3,2,1,0:T(8,128)S(1)} %bitcast.289, f32[4,16,128]{2,1,0:T(8,128)S(1)} %bitcast.764, f32[4,16,3]{2,1,0:T(8,128)S(1)} %bitcast.761, f32[4,16,128]{2,1,0:T(8,128)S(1)} %bitcast.767, f32[4,16,3,128]{3,2,1,0:T(4,128)S(1)} %fusion.475, ...), kind=kOutput, calls=%fused_computation.623 | convolution fusion | flops 52871168 | bytes 1508096 | tf_op jit(solution)/shard_map/...ij,...cj->...ci/dot_general | solution.py:120
  857.5 13.6 %multiply_add_fusion = f32[4,16,120,128]{3,2,1,0:T(8,128)S(1)} fusion(f32[4,16,120,128]{3,2,1,0:T(8,128)} %fusion.110, f32[4,16,120,128]{3,2,1,0:T(8,128)S(1)} %copy-done.26, f32[4,16,120,128]{3,2,1,0:T(8,128)S(1)} %fusion.114, f32[4,16,120,128]{3,2,1,0:T(8,128)S(1)} %fusion.116, f32[4,16,120,128]{3,2,1,0:T(8,128)S(1)} %fusion.118, ...), kind=kOutput, calls=%fused_computation.288 | convolution fusion | flops 1541210112 | bytes 31916032 | tf_op jit(solution)/shard_map/...ij,...cj->...ci/dot_general | solution.py:127
  (219 shorter events, 226.7 us)
Async XLA Ops:
  4.1 2.0 copy-start
  6.1 3.8 copy-start.15
  6.1 17.2 %copy-start.14 = (s32[4,16,6]{1,0,2:T(4,128)S(1)}, s32[4,16,6]{1,0,2:T(4,128)}, u32[]{:S(2)}) copy-start(s32[4,16,6]{1,0,2:T(4,128)} %param.10) | copy-start | bytes 4612
  6.1 17.6 %copy-start.23 = (s32[256]{0:T(256)S(1)}, s32[256]{0:T(256)}, u32[]{:S(2)}) copy-start(s32[256]{0:T(256)} %param.13) | copy-start | bytes 3076
  6.1 17.8 %copy-start.21 = (s32[4,16]{1,0:T(4,128)S(1)}, s32[4,16]{1,0:T(4,128)}, u32[]{:S(2)}) copy-start(s32[4,16]{1,0:T(4,128)} %param.11) | copy-start | bytes 772
  7.3 18.8 %collective-permute-start = (f32[1,16,128,128]{3,2,1,0:T(8,128)}, f32[1,16,128,128]{3,2,1,0:T(8,128)S(1)}, u32[]{:S(2)}, u32[]{:S(2)}) collective-permute-start(f32[1,16,128,128]{3,2,1,0:T(8,128)} %get-tuple-element.225), channel_id=1, source_target_pairs={{0,16},{16,32},{32,48},{48,64},{64,80},{80,96},{96,112},{112,0},{1... | collective-permute-start | bytes 3145736 | tf_op jit(solution)/shard_map/ppermute | solution.py:25
  9.9 16.2 %collective-permute-start.1 = (f32[1,16,128,128]{3,2,1,0:T(8,128)S(1)}, f32[1,16,128,128]{3,2,1,0:T(8,128)S(1)}, u32[]{:S(2)}, u32[]{:S(2)}) collective-permute-start(f32[1,16,128,128]{3,2,1,0:T(8,128)S(1)} %get-tuple-element.226), channel_id=1, source_target_pairs={{16,0},{32,16},{48,32},{64,48},{80,64},{96,80},{112,96},{0,112},{1... | collective-permute-start | bytes 3145736 | tf_op jit(solution)/shard_map/ppermute | solution.py:26
  10.5 12.8 %copy-start.24 = (s32[256,1]{0,1:T(1,128)}, s32[256,1]{0,1:T(1,128)S(1)}, u32[]{:S(2)}) copy-start(s32[256,1]{0,1:T(1,128)S(1)} %compare_select_fusion) | copy-start | bytes 3076
  12.6 144.2 %all-to-all-start = ((s32[128,1,1,4]{3,2,1,0:T(1,128)}), s32[128,1,1,4]{3,2,1,0:T(1,128)S(1)}, u32[]{:S(2)}, u32[]{:S(2)}) async-start(s32[128,1,1,4]{3,2,1,0:T(1,128)} %bitcast.117), calls=%async_computation | async-start | bytes 131072 | tf_op jit(solution)/shard_map/all_to_all | solution.py:48
  26.1 7.7 copy-start.18
  27.9 14.7 %collective-permute-start.2 = (f32[6,1,128,128]{3,2,1,0:T(8,128)}, f32[6,1,128,128]{3,2,1,0:T(8,128)S(1)}, u32[]{:S(2)}, u32[]{:S(2)}) collective-permute-start(f32[6,1,128,128]{3,2,1,0:T(8,128)} %get-tuple-element.117), channel_id=1, source_target_pairs={{0,1},{1,2},{2,3},{3,4},{4,5},{5,6},{6,7},{7,8},{8,9},{9,10},{10,1... | collective-permute-start | bytes 1179656 | tf_op jit(solution)/shard_map/ppermute | solution.py:25
  29.3 13.4 %collective-permute-start.3 = (f32[6,1,128,128]{3,2,1,0:T(8,128)S(1)}, f32[6,1,128,128]{3,2,1,0:T(8,128)S(1)}, u32[]{:S(2)}, u32[]{:S(2)}) collective-permute-start(f32[6,1,128,128]{3,2,1,0:T(8,128)S(1)} %get-tuple-element.118), channel_id=1, source_target_pairs={{1,0},{2,1},{3,2},{4,3},{5,4},{6,5},{7,6},{8,7},{9,8},{10,9},{11,1... | collective-permute-start | bytes 1179656 | tf_op jit(solution)/shard_map/ppermute | solution.py:26
  33.7 11.7 %copy-start.16 = (pred[108]{0:T(512)(128)(4,1)}, pred[108]{0:T(512)(128)(4,1)S(1)}, u32[]{:S(2)}) copy-start(pred[108]{0:T(512)(128)(4,1)S(1)} %broadcast_in_dim.51) | copy-start | bytes 328
  78.1 37.7 %copy-start.20 = (s32[64]{0:T(128)S(1)}, s32[64]{0:T(128)}, u32[]{:S(2)}) copy-start(s32[64]{0:T(128)} %reshape.457) | copy-start | bytes 772
  78.1 37.7 %copy-start.19 = (f32[4,3]{1,0:T(4,128)S(1)}, f32[4,3]{1,0:T(4,128)}, u32[]{:S(2)}) copy-start(f32[4,3]{1,0:T(4,128)} %param.12) | copy-start | bytes 148
  84.0 79.0 %copy-start.17 = (pred[108]{0:T(512)(128)(4,1)S(1)}, pred[108]{0:T(512)(128)(4,1)}, u32[]{:S(2)}) copy-start(pred[108]{0:T(512)(128)(4,1)} %copy-done.16) | copy-start | bytes 328
  113.6 43.3 %collective-permute-start.4 = (f32[1,16,2,128]{3,2,1,0:T(2,128)S(1)}, f32[1,16,2,128]{3,2,1,0:T(2,128)S(1)}, u32[]{:S(2)}, u32[]{:S(2)}) collective-permute-start(f32[1,16,2,128]{3,2,1,0:T(2,128)S(1)} %get-tuple-element.245), channel_id=1, source_target_pairs={{0,16},{16,32},{32,48},{48,64},{64,80},{80,96},{96,112},{112,0},{1... | collective-permute-start | bytes 49160 | tf_op jit(solution)/shard_map/ppermute | solution.py:25
  115.8 41.1 %collective-permute-start.5 = (f32[1,16,2,128]{3,2,1,0:T(2,128)S(1)}, f32[1,16,2,128]{3,2,1,0:T(2,128)S(1)}, u32[]{:S(2)}, u32[]{:S(2)}) collective-permute-start(f32[1,16,2,128]{3,2,1,0:T(2,128)S(1)} %get-tuple-element.246), channel_id=1, source_target_pairs={{16,0},{32,16},{48,32},{64,48},{80,64},{96,80},{112,96},{0,112},{1... | collective-permute-start | bytes 49160 | tf_op jit(solution)/shard_map/ppermute | solution.py:26
  157.0 5.9 collective-permute-start.6
  158.1 4.8 collective-permute-start.7
  174.1 12.1 %copy-start.11 = (f32[64,128,128]{2,1,0:T(8,128)S(1)}, f32[64,128,128]{2,1,0:T(8,128)}, u32[]{:S(2)}) copy-start(f32[64,128,128]{2,1,0:T(8,128)} %gather_fusion.1) | copy-start | bytes 12582916
  186.2 13.1 %copy-start.9 = (f32[64,128,128]{2,1,0:T(8,128)S(1)}, f32[64,128,128]{2,1,0:T(8,128)}, u32[]{:S(2)}) copy-start(f32[64,128,128]{2,1,0:T(8,128)} %gather_fusion.2) | copy-start | bytes 12582916
  199.3 13.1 %copy-start.7 = (f32[64,128,128]{2,1,0:T(8,128)S(1)}, f32[64,128,128]{2,1,0:T(8,128)}, u32[]{:S(2)}) copy-start(f32[64,128,128]{2,1,0:T(8,128)} %gather_fusion.3) | copy-start | bytes 12582916
  212.5 11.5 %copy-start.6 = (f32[64,128,128]{2,1,0:T(8,128)S(1)}, f32[64,128,128]{2,1,0:T(8,128)}, u32[]{:S(2)}) copy-start(f32[64,128,128]{2,1,0:T(8,128)} %gather_fusion.4) | copy-start | bytes 12582916
  224.0 77.3 %copy-start.1 = (f32[4,16,128,128]{3,2,1,0:T(8,128)S(1)}, f32[4,16,128,128]{3,2,1,0:T(8,128)}, u32[]{:S(2)}) copy-start(f32[4,16,128,128]{3,2,1,0:T(8,128)} %copy-done) | copy-start | bytes 12582916
  340.1 26.5 %copy-start.4 = (f32[64,128,128]{2,1,0:T(8,128)S(1)}, f32[64,128,128]{2,1,0:T(8,128)}, u32[]{:S(2)}) copy-start(f32[64,128,128]{2,1,0:T(8,128)} %gather_fusion.5) | copy-start | bytes 12582916
  379.5 12.3 %copy-start.25 = (f32[4,16,120,128]{3,2,1,0:T(8,128)S(1)}, f32[4,16,120,128]{3,2,1,0:T(8,128)}, u32[]{:S(2)}) copy-start(f32[4,16,120,128]{3,2,1,0:T(8,128)} %fusion.124) | copy-start | bytes 11796484
  408.0 19.1 %copy-start.22 = (s32[512]{0:T(512)S(1)}, s32[512]{0:T(512)}, u32[]{:S(2)}) copy-start(s32[512]{0:T(512)} %param.15) | copy-start | bytes 6148
  417.4 35.7 %all-to-all-start.1 = ((f32[128,1,1,4,128]{4,3,2,1,0:T(4,128)}), f32[128,1,1,4,128]{4,3,2,1,0:T(4,128)S(1)}, u32[]{:S(2)}, u32[]{:S(2)}) async-start(f32[128,1,1,4,128]{4,3,2,1,0:T(4,128)} %bitcast.125), calls=%async_computation.1 | async-start | bytes 524288 | tf_op jit(solution)/shard_map/all_to_all | solution.py:48
  516.2 18.1 %copy-start.2 = (f32[64,128,128]{2,1,0:T(8,128)S(1)}, f32[64,128,128]{2,1,0:T(8,128)}, u32[]{:S(2)}) copy-start(f32[64,128,128]{2,1,0:T(8,128)} %copy.65) | copy-start | bytes 12582916
  518.0 13.6 %collective-permute-start.8 = (f32[1,16,128,128]{3,2,1,0:T(8,128)S(1)}, f32[1,16,128,128]{3,2,1,0:T(8,128)S(1)}, u32[]{:S(2)}, u32[]{:S(2)}) collective-permute-start(f32[1,16,128,128]{3,2,1,0:T(8,128)S(1)} %get-tuple-element.185), channel_id=1, source_target_pairs={{0,16},{16,32},{32,48},{48,64},{64,80},{80,96},{96,112},{112,0},{1... | collective-permute-start | bytes 3145736 | tf_op jit(solution)/shard_map/ppermute | solution.py:25
  519.9 14.4 %collective-permute-start.9 = (f32[1,16,128,128]{3,2,1,0:T(8,128)S(1)}, f32[1,16,128,128]{3,2,1,0:T(8,128)S(1)}, u32[]{:S(2)}, u32[]{:S(2)}) collective-permute-start(f32[1,16,128,128]{3,2,1,0:T(8,128)S(1)} %get-tuple-element.186), channel_id=1, source_target_pairs={{16,0},{32,16},{48,32},{64,48},{80,64},{96,80},{112,96},{0,112},{1... | collective-permute-start | bytes 3145736 | tf_op jit(solution)/shard_map/ppermute | solution.py:26
  534.4 10.9 %collective-permute-start.10 = (f32[6,1,128,128]{3,2,1,0:T(8,128)S(1)}, f32[6,1,128,128]{3,2,1,0:T(8,128)S(1)}, u32[]{:S(2)}, u32[]{:S(2)}) collective-permute-start(f32[6,1,128,128]{3,2,1,0:T(8,128)S(1)} %get-tuple-element.115), channel_id=1, source_target_pairs={{0,1},{1,2},{2,3},{3,4},{4,5},{5,6},{6,7},{7,8},{8,9},{9,10},{10,1... | collective-permute-start | bytes 1179656 | tf_op jit(solution)/shard_map/ppermute | solution.py:25
  538.3 8.9 %collective-permute-start.11 = (f32[6,1,128,128]{3,2,1,0:T(8,128)S(1)}, f32[6,1,128,128]{3,2,1,0:T(8,128)S(1)}, u32[]{:S(2)}, u32[]{:S(2)}) collective-permute-start(f32[6,1,128,128]{3,2,1,0:T(8,128)S(1)} %get-tuple-element.116), channel_id=1, source_target_pairs={{1,0},{2,1},{3,2},{4,3},{5,4},{6,5},{7,6},{8,7},{9,8},{10,9},{11,1... | collective-permute-start | bytes 1179656 | tf_op jit(solution)/shard_map/ppermute | solution.py:26
  617.1 3.7 collective-permute-start.12
  618.8 3.2 collective-permute-start.13
  621.9 6.5 collective-permute-start.14
  622.0 6.5 collective-permute-start.15
  639.7 12.3 %copy-start.13 = (f32[64,128,128]{2,1,0:T(8,128)S(1)}, f32[64,128,128]{2,1,0:T(8,128)}, u32[]{:S(2)}) copy-start(f32[64,128,128]{2,1,0:T(8,128)} %gather_fusion.14) | copy-start | bytes 12582916
  652.0 13.1 %copy-start.12 = (f32[64,128,128]{2,1,0:T(8,128)S(1)}, f32[64,128,128]{2,1,0:T(8,128)}, u32[]{:S(2)}) copy-start(f32[64,128,128]{2,1,0:T(8,128)} %gather_fusion.15) | copy-start | bytes 12582916
  665.1 13.1 %copy-start.10 = (f32[64,128,128]{2,1,0:T(8,128)S(1)}, f32[64,128,128]{2,1,0:T(8,128)}, u32[]{:S(2)}) copy-start(f32[64,128,128]{2,1,0:T(8,128)} %gather_fusion.16) | copy-start | bytes 12582916
  678.2 11.5 %copy-start.8 = (f32[64,128,128]{2,1,0:T(8,128)S(1)}, f32[64,128,128]{2,1,0:T(8,128)}, u32[]{:S(2)}) copy-start(f32[64,128,128]{2,1,0:T(8,128)} %gather_fusion.17) | copy-start | bytes 12582916
  689.8 77.3 %copy-start.3 = (f32[64,128,128]{2,1,0:T(8,128)S(1)}, f32[64,128,128]{2,1,0:T(8,128)}, u32[]{:S(2)}) copy-start(f32[64,128,128]{2,1,0:T(8,128)} %copy.65) | copy-start | bytes 12582916
  805.8 26.3 %copy-start.5 = (f32[64,128,128]{2,1,0:T(8,128)S(1)}, f32[64,128,128]{2,1,0:T(8,128)}, u32[]{:S(2)}) copy-start(f32[64,128,128]{2,1,0:T(8,128)} %gather_fusion.18) | copy-start | bytes 12582916
  845.1 12.3 %copy-start.26 = (f32[4,16,120,128]{3,2,1,0:T(8,128)S(1)}, f32[4,16,120,128]{3,2,1,0:T(8,128)}, u32[]{:S(2)}) copy-start(f32[4,16,120,128]{3,2,1,0:T(8,128)} %fusion.112) | copy-start | bytes 11796484
where the time goes:
time: 889 us; the launch traced here: 874 us
  matrix products  304 us (34%)
  other arithmetic  256 us (29%)
  local copies, waits for them, and re-layouts  191 us (21%)
  starting transfers between devices  51.4 us (6%)
  blocking collectives  37.7 us (4%)
  waiting for transfers between devices  31.2 us (4%)
    reduce_sum x12, other arithmetic, force_terms(): jnp.sum(friction, axis=-1)[..., None, :]  158 us
    dot_general x12, matrix products, force_terms(): jnp.einsum('...ij,...cj->...ci', friction, partner[..., 3:6, :], precisio...  154 us
    dot_general x12, matrix products, force_terms(): jnp.einsum('...ij,...cj->...ci', mixing, partner[..., 8:, :], precision=l...  150 us
    gather x12, local copies, waits for them, and re-layouts, rim_step(): flat_cells[partner_index[:, :, member]]  70.4 us
    scatter x2, local copies, waits for them, and re-layouts, migrate(): cells.at[target // block_size, :, target % block_size]  63.1 us
    all_gather x4, blocking collectives, stacked_from(): tiles = lax.all_gather(tiles, axes[k])  37.7 us
    reduce_sum x4, other arithmetic, density_term(): jnp.sum(nearness * nearness * nearness * partner[..., 6, None, :], axis=-1)  36.1 us
    scatter x1, local copies, waits for them, and re-layouts, migrate(): cells = cells.at[source_cell, :, source_pos].set(0.0)  25.9 us
  transfers between devices with their start and end apart: 18, of which 8 were waited for; matrix products, arithmetic and copies ran while one was open for 13% of the time, Pallas kernels for 0%

commit v1 on v0

v1 whole, which is shorter than its diff:
```python
import functools

import jax
import jax.numpy as jnp
from jax import lax
from jax.experimental import pallas as pl
from jax.experimental.pallas import tpu as pltpu
from jax.sharding import PartitionSpec as P

AXES = ("ax", "az")
F32, BF16, I32 = jnp.float32, jnp.bfloat16, jnp.int32

wall_gain = 4.0
time_step = 0.05
MIB = 1 << 20


def rows_of(x, n):
    return jnp.broadcast_to(x, (n,) + x.shape[1:])


def sub_iota(shape):
    return lax.broadcasted_iota(I32, shape, 0)


def halves(x):
    hi = x.astype(BF16)
    return hi, (x - hi.astype(F32)).astype(BF16)


def thirds(x):
    hi = x.astype(BF16).astype(F32)
    rest = x - hi
    mid = rest.astype(BF16).astype(F32)
    return hi, mid, rest - mid


def step_kernel(rows, cols, tab, surf, *refs):
    (cells, a_low, a_high, z_low, z_high, c_ll, c_lh, c_hl, c_hh, out, dens, side_t, side_s, feat, squares, mass, root, rho, ratio, inverse) = refs
    width = cols + 4
    sub8 = sub_iota((8, 128))
    eye = (sub_iota((128, 128)) == lax.broadcasted_iota(I32, (128, 128), 1)).astype(F32).astype(BF16)
    zero_b = jnp.zeros((64, 128), BF16)
    row_mid, col_mid = (rows + 3) / 2.0, (cols + 3) / 2.0

    def shifted(g, r, c):
        off_r = r.astype(F32) - row_mid
        off_c = c.astype(F32) - col_mid
        return jnp.where(sub8 == 0, g + off_r, jnp.where(sub8 == 1, g + off_c, g))

    def geometry(g, r, c, center):
        x = jnp.where(sub8 < 3, shifted(g, r, c), 0.0)
        norm = rows_of(jnp.sum(x * x, axis=0, keepdims=True), 8)
        m = rows_of(g[6:7], 8)
        cube = jnp.exp2(jnp.log2(jnp.maximum(m, 1e-30)) * (1.0 / 3.0))
        cube = cube - (cube - m / (cube * cube)) * (1.0 / 3.0)
        cube = jnp.where(m > 0.0, cube, 0.0)
        u = jnp.where(sub8 < 3, x, jnp.where(sub8 == 3, -norm, jnp.where(sub8 == 4, 1.0, 0.0))) * cube
        uh, um, ul = thirds(u)
        zero = jnp.zeros_like(u)
        t_rows = jnp.concatenate([uh, um, ul, uh, um, uh, zero, zero], axis=0).astype(BF16)
        index = r * width + c
        mass[pl.ds(index, 1), :] = g[6:7]
        root[pl.ds(index, 1), :] = cube[0:1]
        if center:
            w = jnp.where(sub8 < 3, x + x, jnp.where(sub8 == 3, 1.0, jnp.where(sub8 == 4, 1.0 - norm, 0.0)))
            wh, wm, wl = thirds(w)
            side_s[index] = jnp.concatenate([wh, wh, wh, wm, wm, wl, zero, zero], axis=0).astype(BF16)
        return t_rows

    def turned(items):
        for k in range(0, len(items), 2):
            pair = items[k : k + 2]
            blocks = []
            for g, r, c, center in pair:
                blocks += [geometry(g, r, c, center), zero_b]
            if len(pair) == 1:
                blocks += [zero_b, zero_b]
            t = lax.dot_general(eye, jnp.concatenate(blocks, axis=0), (((1,), (1,)), ((), ())), preferred_element_type=F32)
            for n, (g, r, c, center) in enumerate(pair):
                side_t[r * width + c] = t[:, n * 128 : (n + 1) * 128].astype(BF16)

    def loop(n, body):
        def step(i, carry):
            body(i)
            return carry

        lax.fori_loop(0, n, step, 0)

    unroll = 4

    def local_geo(i):
        items = []
        for k in range(unroll):
            n = i * unroll + k
            items.append((cells[n, 0:8, :], n // cols + 2, n % cols + 2, True))
        turned(items)

    loop(rows * cols // unroll, local_geo)

    def a_geo(ref, first, second, i):
        items = []
        for k in range(2):
            n = i * 2 + k
            items.append((ref[n, 0:8, :], jnp.int32(first), n + 2, True))
            items.append((ref[n, 128:136, :], jnp.int32(second), n + 2, False))
        turned(items)

    loop(cols // 2, functools.partial(a_geo, a_low, 1, 0))
    loop(cols // 2, functools.partial(a_geo, a_high, rows + 2, rows + 3))

    def z_geo(ref, first, second, i):
        turned([(ref[i, 0:8, :], i + 2, jnp.int32(first), True), (ref[i, 128:136, :], i + 2, jnp.int32(second), False)])

    loop(rows, functools.partial(z_geo, z_low, 1, 0))
    loop(rows, functools.partial(z_geo, z_high, cols + 2, cols + 3))
    corners = ((c_ll, 1, 0, 1, 0), (c_lh, 1, 0, cols + 2, cols + 3), (c_hl, rows + 2, rows + 3, 1, 0), (c_hh, rows + 2, rows + 3, cols + 2, cols + 3))
    for ref, r1, r0, k1, k0 in corners:
        r1, r0, k1, k0 = jnp.int32(r1), jnp.int32(r0), jnp.int32(k1), jnp.int32(k0)
        turned([(ref[0, 0:8, :], r1, k1, True), (ref[0, 128:136, :], r0, k1, False), (ref[0, 136:144, :], r1, k0, False), (ref[0, 144:152, :], r0, k0, False)])

    zero_w = jnp.zeros((64, 128), BF16)
    zero_h = jnp.zeros((128, 128), BF16)

    def density(n, keep):
        base = n * 8
        center = tab[base]
        b = jnp.concatenate([side_s[center], zero_w], axis=0)
        rhs = jnp.concatenate([jnp.concatenate([b, zero_h], axis=1), jnp.concatenate([zero_h, b], axis=1)], axis=0)
        total = jnp.zeros((8, 128), F32)
        for j in range(3):
            lhs = jnp.concatenate([side_t[tab[base + 1 + 2 * j]], side_t[tab[base + 2 + 2 * j]]], axis=1)
            y = jnp.maximum(jnp.dot(lhs, rhs, preferred_element_type=F32), 0.0)
            square = y * y
            cubes = square * y
            for h in range(2):
                lanes = slice(h * 128, (h + 1) * 128)
                total = total + jnp.sum(cubes[:, lanes].reshape(16, 8, 128), axis=0)
                if keep:
                    squares[n, j * 256 + h * 128 : j * 256 + (h + 1) * 128, :] = square[:, lanes].astype(BF16)
        rho[pl.ds(center, 1), :] = jnp.sum(total, axis=0, keepdims=True)

    own = rows * cols
    ring = 2 * (rows + 2) + 2 * cols

    def own_density(i):
        for k in range(2):
            density(i * 2 + k, True)

    loop(own // 2, own_density)

    def ring_density(i):
        for k in range(2):
            density(own + i * 2 + k, False)

    loop(ring // 2, ring_density)

    living = mass[...] > 0.0
    guarded = jnp.where(living, rho[...], 1.0)
    ratio[...] = jnp.where(living, (guarded - 1.0) / (guarded * guarded), 0.0)
    inverse[...] = jnp.where(living, 1.0 / guarded, 0.0)

    def row8(ref, index):
        return rows_of(ref[pl.ds(index, 1), :], 8)

    def positions(g, r, c):
        x = shifted(g, r, c)
        return jnp.where((sub8 == 0) | (sub8 == 4), 1.0, jnp.where(sub8 < 4, pltpu.roll(x, 1, 0), pltpu.roll(x, 5, 0)))

    def features(load, r, c):
        index = r * width + c
        g = load(0)
        cube = row8(root, index)
        scale = cube * row8(inverse, index)
        nu = rows_of(g[7:8], 8)
        first = jnp.where(sub8 < 3, pltpu.roll(g, 5, 0) * nu, jnp.where(sub8 == 6, 1.0, g)) * scale
        press = positions(g, r, c) * jnp.where(sub8 < 4, cube, cube * row8(ratio, index))
        hi, lo = halves(press)
        feat[index, 128:144, :] = jnp.concatenate([hi.astype(F32), lo.astype(F32)], axis=0).astype(BF16)
        feat[index, 0:16, :] = jnp.concatenate([first, load(1) * scale], axis=0).astype(BF16)
        for k in range(1, 8):
            feat[index, 16 * k : 16 * k + 16, :] = jnp.concatenate([load(2 * k) * scale, load(2 * k + 1) * scale], axis=0).astype(BF16)

    def loader(ref, n):
        return lambda k: ref[n, 8 * k : 8 * k + 8, :]

    def local_feat(i):
        for k in range(2):
            n = i * 2 + k
            features(loader(cells, n), n // cols + 2, n % cols + 2)

    loop(own // 2, local_feat)

    def a_feat(i):
        features(loader(a_low, i), jnp.int32(1), i + 2)
        features(loader(a_high, i), jnp.int32(rows + 2), i + 2)

    loop(cols, a_feat)

    def z_feat(i):
        features(loader(z_low, i), i + 2, jnp.int32(1))
        features(loader(z_high, i), i + 2, jnp.int32(cols + 2))

    loop(rows, z_feat)
    for ref, r1, r0, k1, k0 in corners:
        features(loader(ref, 0), jnp.int32(r1), jnp.int32(k1))

    def force(n):
        r, c = n // cols + 2, n % cols + 2
        index = r * width + c
        base = n * 8
        lhs = jnp.concatenate([feat[tab[base + 1 + j]] for j in range(6)], axis=1)
        sums = jnp.dot(lhs, squares[n], preferred_element_type=F32)
        g = cells[n, 0:8, :]
        m, nu = rows_of(g[6:7], 8), rows_of(g[7:8], 8)
        alive = jnp.where(m > 0.0, time_step, 0.0)
        first = sums[0:8]
        press = sums[128:136] + sums[136:144]
        press = press - positions(g, r, c) * jnp.where(sub8 < 4, rows_of(press[0:1], 8), rows_of(press[4:5], 8))
        press = press * jnp.where(sub8 < 4, row8(ratio, index), 1.0)
        press = press + pltpu.roll(press, 4, 0)
        weight, friction = rows_of(first[6:7], 8), rows_of(first[7:8], 8)
        surface = jnp.where(sub8 == 3, surf[n * 4], jnp.where(sub8 == 4, surf[n * 4 + 1], surf[n * 4 + 2]))
        wall = wall_gain * jnp.maximum(1.0 - 3.0 * rows_of(g[2:3], 8), 0.0)
        accel = nu * (first - g * weight) + pltpu.roll(first, 3, 0) - g * friction + wall * (surface - g)
        accel = accel - 6.0 * pltpu.roll(press, 2, 0)
        velocity = g + accel * alive
        position = g + time_step * pltpu.roll(velocity, 5, 0)
        out[n, 0:8, :] = jnp.where(sub8 < 3, position, jnp.where(sub8 < 6, velocity, g))
        gain = 2.0 * alive
        stay = 1.0 - gain * weight
        for k in range(1, 16):
            out[n, 8 * k : 8 * k + 8, :] = cells[n, 8 * k : 8 * k + 8, :] * stay + gain * sums[8 * k : 8 * k + 8]
        dens[pl.ds(n, 1), :] = jnp.where(m > 0.0, row8(rho, index), 0.0)[0:1]

    def forces(i):
        for k in range(2):
            force(i * 2 + k)

    loop(own // 2, forces)


def step_call(rows, cols, table, surface, cells, halo):
    own = rows * cols
    patch = (rows + 4) * (cols + 4)
    smem = pl.BlockSpec(memory_space=pltpu.SMEM)
    vmem = pl.BlockSpec(memory_space=pltpu.VMEM)
    return pl.pallas_call(
        functools.partial(step_kernel, rows, cols),
        out_shape=(jax.ShapeDtypeStruct((own, 128, 128), F32), jax.ShapeDtypeStruct((own, 128), F32)),
        in_specs=[smem, smem] + [vmem] * 9,
        out_specs=(vmem, vmem),
        scratch_shapes=[
            pltpu.VMEM((patch, 128, 128), BF16),
            pltpu.VMEM((patch, 64, 128), BF16),
            pltpu.VMEM((patch, 144, 128), BF16),
            pltpu.VMEM((own, 768, 128), BF16),
            pltpu.VMEM((patch, 128), F32),
            pltpu.VMEM((patch, 128), F32),
            pltpu.VMEM((patch, 128), F32),
            pltpu.VMEM((patch, 128), F32),
            pltpu.VMEM((patch, 128), F32),
        ],
        compiler_params=pltpu.CompilerParams(vmem_limit_bytes=60 * MIB),
    )(table, surface, cells, *halo)


def extract_kernel(state, slots, buffer_row, out, kept, moved):
    cells, leaving, slots_out = state.shape[0], slots.shape[0], out.shape[0]
    offset = jnp.broadcast_to(slots[...], (leaving, 128)) - lax.broadcasted_iota(I32, (leaving, 128), 1)
    moved[...] = jnp.zeros_like(moved)

    def body(c, carry):
        hit = jnp.where(offset == c * 128, 1.0, 0.0)
        gone = jnp.sum(hit, axis=0, keepdims=True)
        hi, lo = halves(state[c])
        moved[...] += lax.dot_general(hit.astype(BF16), jnp.concatenate([hi, lo], axis=0), (((1,), (1,)), ((), ())), preferred_element_type=F32)
        kept[c] = state[c] * (1.0 - gone)
        return carry

    lax.fori_loop(0, cells, body, 0)
    place = jnp.where(jnp.broadcast_to(buffer_row[...], (slots_out, leaving)) == sub_iota((slots_out, leaving)), 1.0, 0.0).astype(BF16)
    right = jnp.concatenate([moved[...].astype(BF16), jnp.ones((leaving, 128), BF16)], axis=1)
    sums = jnp.dot(place, right, preferred_element_type=F32)
    lane = lax.broadcasted_iota(I32, (slots_out, 128), 1)
    out[...] = jnp.where((lane == 6) & (sums[:, 256:384] < 0.5), -1.0, sums[:, 0:128] + sums[:, 128:256])


def extract(state, slots, buffer_row, places):
    vmem = pl.BlockSpec(memory_space=pltpu.VMEM)
    return pl.pallas_call(
        extract_kernel,
        out_shape=(jax.ShapeDtypeStruct((places, 128), F32), jax.ShapeDtypeStruct(state.shape, F32)),
        in_specs=[vmem] * 3,
        out_specs=(vmem, vmem),
        scratch_shapes=[pltpu.VMEM((slots.shape[0], 256), F32)],
        compiler_params=pltpu.CompilerParams(vmem_limit_bytes=40 * MIB),
    )(state, slots, buffer_row)


def insert_kernel(state, incoming, slots, out):
    cells, places = state.shape[0], slots.shape[0]
    data = incoming[...]
    absent = jnp.broadcast_to(data[:, 6:7], (places, 128)) < 0.0
    offset = jnp.broadcast_to(slots[...], (places, 128)) - lax.broadcasted_iota(I32, (places, 128), 1)
    offset = jnp.where(absent, -1, offset)
    hi, lo = halves(jnp.transpose(data))
    left = jnp.concatenate([hi, lo, jnp.ones((16, places), BF16)], axis=0)

    def body(i, carry):
        hits = [jnp.where(offset == (2 * i + k) * 128, 1.0, 0.0).astype(BF16) for k in range(2)]
        sums = jnp.dot(left, jnp.concatenate(hits, axis=1), preferred_element_type=F32)
        for k in range(2):
            part = sums[:, 128 * k : 128 * (k + 1)]
            out[2 * i + k] = state[2 * i + k] * (1.0 - part[256:257]) + (part[0:128] + part[128:256])
        return carry

    lax.fori_loop(0, cells // 2, body, 0)


def insert(state, incoming, slots):
    vmem = pl.BlockSpec(memory_space=pltpu.VMEM)
    return pl.pallas_call(
        insert_kernel,
        out_shape=jax.ShapeDtypeStruct(state.shape, F32),
        in_specs=[vmem] * 3,
        out_specs=vmem,
        compiler_params=pltpu.CompilerParams(vmem_limit_bytes=40 * MIB),
    )(state, incoming, slots)


def moves(n_ax, n_az, da, dz):
    pairs = []
    for a in range(n_ax):
        for z in range(n_az):
            if 0 <= a + da < n_ax:
                pairs.append((a * n_az + z, (a + da) * n_az + (z + dz) % n_az))
    return pairs


def rim(state, rows, cols, n_ax, n_az):
    grid = state.reshape(rows, cols, 128, 128)

    def ax_part(first, second):
        return jnp.concatenate([grid[first], grid[second, :, 0:8]], axis=1)

    def az_part(first, second):
        return jnp.concatenate([grid[:, first], grid[:, second, 0:8]], axis=1)

    def corner(r1, r0, k1, k0):
        return jnp.concatenate([grid[r1, k1], grid[r0, k1, 0:8], grid[r1, k0, 0:8], grid[r0, k0, 0:8]], axis=0)[None]

    lo, hi = (0, 1), (-1, -2)
    sent = [
        (ax_part(*hi), 1, 0),
        (ax_part(*lo), -1, 0),
        (az_part(*hi), 0, 1),
        (az_part(*lo), 0, -1),
        (corner(*hi, *hi), 1, 1),
        (corner(*hi, *lo), 1, -1),
        (corner(*lo, *hi), -1, 1),
        (corner(*lo, *lo), -1, -1),
    ]
    return [lax.ppermute(x, AXES, moves(n_ax, n_az, da, dz)) for x, da, dz in sent]


def border(rows, cols):
    cells = [(r, c) for r in range(rows) for c in range(cols) if r in (0, rows - 1) or c in (0, cols - 1)]
    return cells, {cell: n for n, cell in enumerate(cells)}


def local(particles, counts, pair_codes, contact, twist_state, leaving_slot, leaving_dest, arrival_slot):
    rows, cols, fields, block = particles.shape
    n_ax, n_az = lax.axis_size("ax"), lax.axis_size("az")
    ranks = n_ax * n_az
    own = rows * cols
    ax, az = lax.axis_index("ax"), lax.axis_index("az")

    keep = lax.broadcasted_iota(I32, (own, block), 1) < counts.reshape(own, 1)
    state = jnp.where(keep[:, None, :], particles.reshape(own, fields, block), 0.0)
    halo = rim(state, rows, cols, n_ax, n_az)

    listed, place = border(rows, cols)
    partners = pair_codes.shape[2]
    rim_codes = jnp.stack([pair_codes[r, c] for r, c in listed]).astype(F32)
    segments = twist_state.shape[0]
    used = segments * 3 + len(listed) * partners
    padded = -(-used // 128) * 128
    packed = jnp.concatenate([twist_state.reshape(-1), rim_codes.reshape(-1), jnp.zeros((padded - used,), F32)])
    everyone = lax.all_gather(packed.reshape(-1, 128), AXES).reshape(ranks, padded)
    twist = everyone[:, : segments * 3].reshape(ranks * segments, 3)
    surface = jnp.pad(twist[contact.reshape(own)], ((0, 0), (0, 1))).reshape(-1)
    codes = everyone[:, segments * 3 : used].reshape(ranks * len(listed), partners)

    ring = [(r, c) for r in range(-1, rows + 1) for c in range(-1, cols + 1) if not (0 <= r < rows and 0 <= c < cols)]
    side_a = jnp.array([-1 if r < 0 else (1 if r >= rows else 0) for r, c in ring], I32)
    side_z = jnp.array([-1 if c < 0 else (1 if c >= cols else 0) for r, c in ring], I32)
    number = jnp.array([place[(r % rows, c % cols)] for r, c in ring], I32)
    device = jnp.clip(ax + side_a, 0, n_ax - 1) * n_az + (az + side_z) % n_az
    ring_codes = codes[device * len(listed) + number].astype(I32)

    width = cols + 4
    centers = jnp.array([(r + 2) * width + c + 2 for r in range(rows) for c in range(cols)] + [(r + 2) * width + c + 2 for r, c in ring], I32)
    all_codes = jnp.concatenate([pair_codes.reshape(own, partners), ring_codes], axis=0)
    linked = centers[:, None] + (all_codes // 3 - 1) * width + all_codes % 3 - 1
    table = jnp.concatenate([centers[:, None], linked, jnp.zeros((centers.shape[0], 1), I32)], axis=1).reshape(-1)

    dest = leaving_dest[:, 0]
    leaving = dest.shape[0]
    same = dest[:, None] == dest[None, :]
    earlier = lax.broadcasted_iota(I32, (leaving, leaving), 0) > lax.broadcasted_iota(I32, (leaving, leaving), 1)
    order = jnp.sum((same & earlier).astype(I32), axis=1)
    capacity = arrival_slot.shape[0] // ranks
    buffer_row = (dest * capacity + order).reshape(1, leaving)

    state, _ = step_call(rows, cols, table, surface, state, halo)
    outgoing, state = extract(state, leaving_slot.reshape(-1, 1), buffer_row, ranks * capacity)
    incoming = lax.all_to_all(outgoing.reshape(ranks, capacity, fields), AXES, 0, 0, tiled=True)
    state = insert(state, incoming.reshape(-1, fields), arrival_slot.reshape(-1, 1))
    halo = rim(state, rows, cols, n_ax, n_az)
    state, density = step_call(rows, cols, table, surface, state, halo)
    return state.reshape(particles.shape), density.reshape(rows, cols, block)


def solution(mesh):
    both = P("ax", "az")
    flat = P(AXES)
    return jax.shard_map(
        local,
        mesh=mesh,
        in_specs=(P("ax", "az", None, None), both, P("ax", "az", None), both, P(AXES, None), flat, P(AXES, None), flat),
        out_specs=(P("ax", "az", None, None), P("ax", "az", None)),
        check_vma=False,
    )
```

time: 889 us -> 288 us (0.32); the launches traced: 874 us -> 287 us
  matrix products: 304 us -> 0 us
  other arithmetic: 256 us -> 16.8 us
  local copies, waits for them, and re-layouts: 191 us -> 25.1 us
  Pallas kernels: 0 us -> 104 us
  blocking collectives: 37.7 us -> 54.2 us
    dot_general x24 -> x0, matrix products: 304 us -> none  [the longest x12 154 us: force_terms(): jnp.einsum('...ij,...cj->...ci', friction, partner[..., 3:6, :], precisio...]
    reduce_sum x17 -> x1, other arithmetic: 194 us -> 0.93 us  [local(): order = jnp.sum((same & earlier).astype(I32), axis=1)]
    pallas_call x0 -> x4, Pallas kernels: none -> 104 us  [the longest x2 81.5 us: step_call(): pl.pallas_call(functools.partial(step_kernel, rows, cols), out_shape=(jax...]
    scatter x5 -> x0, local copies, waits for them, and re-layouts: 94.2 us -> none  [the longest x2 63.1 us: migrate(): cells.at[target // block_size, :, target % block_size]]
    gather x25 -> x3, local copies, waits for them, and re-layouts: 78.9 us -> 2.59 us  [the longest x2 1.99 us: local(): ring_codes = codes[device * len(listed) + number].astype(I32)]
    mul x16 -> x0, other arithmetic: 20.2 us -> none  [the longest x10 11.7 us: force_terms(): partner_mass * inverse_partner[..., None, :]]
    all_gather x4 -> x1, blocking collectives: 37.7 us -> 54.2 us  [local(): lax.all_gather(packed.reshape(-1, 128), AXES).reshape(ranks, padded)]
    all_to_all x2 -> x1, starting transfers between devices: 20.4 us -> 4.35 us  [local(): lax.all_to_all(outgoing.reshape(ranks, capacity, fields), AXES, 0, 0, til...]
  transfers between devices with their start and end apart: 18 -> 17, of which waited for: 8 -> 6; matrix products, arithmetic and copies ran while one was open for 13% -> 9% of each run, Pallas kernels for 0% -> 0%
where the time goes in v1:
time: 288 us; the launch traced here: 287 us
  Pallas kernels  104 us (36%)
  blocking collectives  54.2 us (19%)
  starting transfers between devices  48.8 us (17%)
  waiting for transfers between devices  36.8 us (13%)
  local copies, waits for them, and re-layouts  25.1 us (9%)
  other arithmetic  16.8 us (6%)
    pallas_call x2, Pallas kernels, step_call(): pl.pallas_call(functools.partial(step_kernel, rows, cols), out_shape=(jax...  81.5 us
    all_gather x1, blocking collectives, local(): lax.all_gather(packed.reshape(-1, 128), AXES).reshape(ranks, padded)  54.2 us
    ppermute x16, starting transfers between devices, rim(): lax.ppermute(x, AXES, moves(n_ax, n_az, da, dz))  44.4 us
    ppermute x16, waiting for transfers between devices, rim(): lax.ppermute(x, AXES, moves(n_ax, n_az, da, dz))  25.6 us
    pallas_call x1, Pallas kernels, extract(): pl.pallas_call(extract_kernel, out_shape=(jax.ShapeDtypeStruct((places, 1...  13.7 us
    all_to_all x1, waiting for transfers between devices, local(): lax.all_to_all(outgoing.reshape(ranks, capacity, fields), AXES, 0, 0, til...  11.3 us
    unnamed x61, local copies, waits for them, and re-layouts  10.4 us
    pallas_call x1, Pallas kernels, insert(): pl.pallas_call(insert_kernel, out_shape=jax.ShapeDtypeStruct(state.shape,...  8.37 us
  transfers between devices with their start and end apart: 17, of which 6 were waited for; matrix products, arithmetic and copies ran while one was open for 9% of the time, Pallas kernels for 0%

profile of v1, /device:TPU:1, one launch (start us, length us, event | category | flops | bytes accessed | tf_op | source)
XLA Modules:
  0.0 286.6 jit_solution(4404602057182063371)
XLA Ops:
  0.6 0.8 iota_compare_fusion.1
  1.4 2.8 broadcast_select_fusion
  6.1 5.5 %collective-permute-start.4 = (f32[1,152,128]{2,1,0:T(8,128)}, f32[1,152,128]{2,1,0:T(8,128)}, u32[]{:S(2)}, u32[]{:S(2)}) collective-permute-start(f32[1,152,128]{2,1,0:T(8,128)} %maximum_bitcast_fusion), channel_id=1, source_target_pairs={{0,17},{1,18},{2,19},{3,20},{4,21},{5,22},{6,23},{7,24},{8,25},{9,... | collective-permute-start | bytes 233480 | tf_op jit(solution)/shard_map/ppermute | solution.py:364
  12.2 6.8 %collective-permute-start.5 = (f32[1,152,128]{2,1,0:T(8,128)}, f32[1,152,128]{2,1,0:T(8,128)}, u32[]{:S(2)}, u32[]{:S(2)}) collective-permute-start(f32[1,152,128]{2,1,0:T(8,128)} %maximum_bitcast_fusion.1), channel_id=1, source_target_pairs={{0,31},{1,16},{2,17},{3,18},{4,19},{5,20},{6,21},{7,22},{8,23},{9,... | collective-permute-start | bytes 233480 | tf_op jit(solution)/shard_map/ppermute | solution.py:364
  19.0 0.7 slice_bitcast_fusion.2
  21.3 2.7 bitcast_select_fusion.refs_0_
  24.3 1.3 pad_maximum_fusion
  25.6 2.0 collective-permute-start
  27.6 1.1 pad_maximum_fusion.1
  28.7 2.4 collective-permute-start.1
  32.8 54.2 %all_gather.3 = f32[128,2,128]{2,1,0:T(2,128)S(1)} all-gather(f32[1,2,128]{2,1,0:T(2,128)S(1)} %maximum_bitcast_fusion.8), channel_id=1, replica_groups=mesh['ax'=8,'az'=16] {'ax','az'}, dimensions={0}, use_global_device_ids=true | all-gather | bytes 132096 | tf_op jit(solution)/shard_map/all_gather | solution.py:390
  87.7 1.7 slice.352
  89.3 1.7 reshape.142
  91.7 1.2 gather_fusion
  92.9 0.8 copy.137
  93.8 0.8 reshape.145
  94.5 0.9 convert_reduce_fusion
  96.2 0.8 fusion.5
  96.9 0.7 add_add_fusion
  97.7 1.0 pad_maximum_fusion.5
  98.7 3.4 %collective-permute-start.3 = (f32[4,136,128]{2,1,0:T(8,128)S(1)}, f32[4,136,128]{2,1,0:T(8,128)S(1)}, u32[]{:S(2)}, u32[]{:S(2)}) collective-permute-start(f32[4,136,128]{2,1,0:T(8,128)S(1)} %pad_maximum_fusion.5), channel_id=1, source_target_pairs={{0,15},{1,0},{2,1},{3,2},{4,3},{5,4},{6,5},{7,6},{8,7},{9,8},{10,9... | collective-permute-start | bytes 835592 | tf_op jit(solution)/shard_map/ppermute | solution.py:364
  102.1 0.9 maximum_bitcast_fusion.2
  103.0 0.8 slice.353
  104.7 1.9 collective-permute-start.6
  106.7 8.0 %collective-permute-done.6.refs_7_ = f32[1,152,128]{2,1,0:T(8,128)S(1)} collective-permute-done((f32[1,152,128]{2,1,0:T(8,128)S(1)}, f32[1,152,128]{2,1,0:T(8,128)S(1)}, u32[]{:S(2)}, u32[]{:S(2)}) %collective-permute-start.6) | collective-permute-done | bytes 77856 | tf_op jit(solution)/shard_map/ppermute | solution.py:364
  114.7 1.9 collective-permute-start.7
  117.8 0.8 copy.139.slots
  118.7 2.6 collective-permute-done.7.refs_8_
  122.4 40.8 %shard_map.131 = (f32[64,128,128]{2,1,0:T(8,128)}, f32[64,128]{1,0:T(8,128)}) custom-call(s32[864]{0:T(1024)} %reshape.143.tab, f32[256]{0:T(256)} %reshape.146.surf, f32[64,128,128]{2,1,0:T(8,128)} %copy-done.4, f32[16,136,128]{2,1,0:T(8,128)} %copy-done.6, f32[16,136,128]{2,1,0:T(8,128)} %collective-permute-done.1.refs_2_, ...), custom_call_target="tpu_custom_call" | custom-call | tf_op jit(solution)/shard_map/pallas_call | solution.py:248
  163.2 2.2 copy-done.1
  165.4 13.7 %shard_map.132 = (f32[512,128]{1,0:T(8,128)}, f32[64,128,128]{2,1,0:T(8,128)S(1)}) custom-call(f32[64,128,128]{2,1,0:T(8,128)S(1)} %copy-done.1, s32[256,1]{1,0:T(8,128)S(1)} %copy.139.slots, s32[1,256]{1,0:T(1,128)S(1)} %bitcast_add_fusion.buffer_row), custom_call_target="tpu_custom_call" | custom-call | tf_op jit(solution)/shard_map/pallas_call | solution.py:291
  179.1 2.0 copy-done.2
  181.1 4.4 %all-to-all-start = ((f32[128,4,128]{2,1,0:T(4,128)}), f32[128,4,128]{2,1,0:T(4,128)S(1)}, u32[]{:S(2)}, u32[]{:S(2)}) async-start(f32[128,4,128]{2,1,0:T(4,128)} %bitcast.33), calls=%async_computation | async-start | bytes 524288 | tf_op jit(solution)/shard_map/all_to_all | solution.py:418
  185.6 11.3 %all-to-all-done = f32[128,4,128]{2,1,0:T(4,128)S(1)} async-done(((f32[128,4,128]{2,1,0:T(4,128)}), f32[128,4,128]{2,1,0:T(4,128)S(1)}, u32[]{:S(2)}, u32[]{:S(2)}) %all-to-all-start) | async-done | bytes 262176 | tf_op jit(solution)/shard_map/all_to_all | solution.py:418
  196.9 2.2 copy-done.3
  199.1 8.4 %shard_map.133.refs_0_ = f32[64,128,128]{2,1,0:T(8,128)S(1)} custom-call(f32[64,128,128]{2,1,0:T(8,128)S(1)} %copy-done.3, f32[512,128]{1,0:T(8,128)S(1)} %bitcast.205, s32[512,1]{1,0:T(8,128)S(1)} %copy.140.slots), custom_call_target="tpu_custom_call" | custom-call | tf_op jit(solution)/shard_map/pallas_call | solution.py:323
  207.7 3.1 %collective-permute-start.15 = (f32[1,152,128]{2,1,0:T(8,128)S(1)}, f32[1,152,128]{2,1,0:T(8,128)S(1)}, u32[]{:S(2)}, u32[]{:S(2)}) collective-permute-start(f32[1,152,128]{2,1,0:T(8,128)S(1)} %maximum_bitcast_fusion.7), channel_id=1, source_target_pairs={{16,15},{17,0},{18,1},{19,2},{20,3},{21,4},{22,5},{23,6},{24,7},{2... | collective-permute-start | bytes 233480 | tf_op jit(solution)/shard_map/ppermute | solution.py:364
  211.0 1.9 collective-permute-start.9
  213.0 3.6 %collective-permute-start.8 = (f32[16,136,128]{2,1,0:T(8,128)S(1)}, f32[16,136,128]{2,1,0:T(8,128)S(1)}, u32[]{:S(2)}, u32[]{:S(2)}) collective-permute-start(f32[16,136,128]{2,1,0:T(8,128)S(1)} %pad_maximum_fusion.2), channel_id=1, source_target_pairs={{0,16},{1,17},{2,18},{3,19},{4,20},{5,21},{6,22},{7,23},{8,24},{9,... | collective-permute-start | bytes 3342344 | tf_op jit(solution)/shard_map/ppermute | solution.py:364
  216.6 1.9 collective-permute-start.14
  218.7 3.6 %collective-permute-start.11 = (f32[4,136,128]{2,1,0:T(8,128)S(1)}, f32[4,136,128]{2,1,0:T(8,128)S(1)}, u32[]{:S(2)}, u32[]{:S(2)}) collective-permute-start(f32[4,136,128]{2,1,0:T(8,128)S(1)} %pad_maximum_fusion.7), channel_id=1, source_target_pairs={{0,15},{1,0},{2,1},{3,2},{4,3},{5,4},{6,5},{7,6},{8,7},{9,8},{10,9... | collective-permute-start | bytes 835592 | tf_op jit(solution)/shard_map/ppermute | solution.py:364
  222.4 6.5 %collective-permute-done.14.refs_7_ = f32[1,152,128]{2,1,0:T(8,128)S(1)} collective-permute-done((f32[1,152,128]{2,1,0:T(8,128)S(1)}, f32[1,152,128]{2,1,0:T(8,128)S(1)}, u32[]{:S(2)}, u32[]{:S(2)}) %collective-permute-start.14) | collective-permute-done | bytes 77856 | tf_op jit(solution)/shard_map/ppermute | solution.py:364
  228.8 3.2 %collective-permute-start.13 = (f32[1,152,128]{2,1,0:T(8,128)S(1)}, f32[1,152,128]{2,1,0:T(8,128)S(1)}, u32[]{:S(2)}, u32[]{:S(2)}) collective-permute-start(f32[1,152,128]{2,1,0:T(8,128)S(1)} %maximum_bitcast_fusion.5), channel_id=1, source_target_pairs={{0,31},{1,16},{2,17},{3,18},{4,19},{5,20},{6,21},{7,22},{8,23},{9,... | collective-permute-start | bytes 233480 | tf_op jit(solution)/shard_map/ppermute | solution.py:364
  232.1 2.4 collective-permute-done.13.refs_6_
  234.5 3.0 %collective-permute-start.12 = (f32[1,152,128]{2,1,0:T(8,128)S(1)}, f32[1,152,128]{2,1,0:T(8,128)S(1)}, u32[]{:S(2)}, u32[]{:S(2)}) collective-permute-start(f32[1,152,128]{2,1,0:T(8,128)S(1)} %maximum_bitcast_fusion.4), channel_id=1, source_target_pairs={{0,17},{1,18},{2,19},{3,20},{4,21},{5,22},{6,23},{7,24},{8,25},{9,... | collective-permute-start | bytes 233480 | tf_op jit(solution)/shard_map/ppermute | solution.py:364
  237.5 6.0 %collective-permute-done.12.refs_5_ = f32[1,152,128]{2,1,0:T(8,128)S(1)} collective-permute-done((f32[1,152,128]{2,1,0:T(8,128)S(1)}, f32[1,152,128]{2,1,0:T(8,128)S(1)}, u32[]{:S(2)}, u32[]{:S(2)}) %collective-permute-start.12) | collective-permute-done | bytes 77856 | tf_op jit(solution)/shard_map/ppermute | solution.py:364
  244.8 1.0 copy-done.8
  245.8 40.8 %shard_map.134 = (f32[64,128,128]{2,1,0:T(8,128)}, f32[64,128]{1,0:T(8,128)}) custom-call(s32[864]{0:T(1024)} %reshape.143.tab, f32[256]{0:T(256)} %reshape.146.surf, f32[64,128,128]{2,1,0:T(8,128)} %copy-done, f32[16,136,128]{2,1,0:T(8,128)} %copy-done.8, f32[16,136,128]{2,1,0:T(8,128)} %copy-done.7, f32[4,136,128]{2,1,0:T(8,128)} %copy-done.11, ...), custom_call_target="tpu_custom_call" | custom-call | tf_op jit(solution)/shard_map/pallas_call | solution.py:248
  (119 shorter events, 13.1 us)
Async XLA Ops:
  1.4 19.7 %copy-start.18 = (s32[4,16]{1,0:T(4,128)S(1)}, s32[4,16]{1,0:T(4,128)}, u32[]{:S(2)}) copy-start(s32[4,16]{1,0:T(4,128)} %param.13) | copy-start | bytes 772
  6.1 92.6 %collective-permute-start.4 = (f32[1,152,128]{2,1,0:T(8,128)}, f32[1,152,128]{2,1,0:T(8,128)}, u32[]{:S(2)}, u32[]{:S(2)}) collective-permute-start(f32[1,152,128]{2,1,0:T(8,128)} %maximum_bitcast_fusion), channel_id=1, source_target_pairs={{0,17},{1,18},{2,19},{3,20},{4,21},{5,22},{6,23},{7,24},{8,25},{9,... | collective-permute-start | bytes 233480 | tf_op jit(solution)/shard_map/ppermute | solution.py:364
  12.2 92.5 %collective-permute-start.5 = (f32[1,152,128]{2,1,0:T(8,128)}, f32[1,152,128]{2,1,0:T(8,128)}, u32[]{:S(2)}, u32[]{:S(2)}) collective-permute-start(f32[1,152,128]{2,1,0:T(8,128)} %maximum_bitcast_fusion.1), channel_id=1, source_target_pairs={{0,31},{1,16},{2,17},{3,18},{4,19},{5,20},{6,21},{7,22},{8,23},{9,... | collective-permute-start | bytes 233480 | tf_op jit(solution)/shard_map/ppermute | solution.py:364
  21.1 100.2 %collective-permute-start.2 = (f32[4,136,128]{2,1,0:T(8,128)}, f32[4,136,128]{2,1,0:T(8,128)}, u32[]{:S(2)}, u32[]{:S(2)}) collective-permute-start(f32[4,136,128]{2,1,0:T(8,128)} %pad_maximum_fusion.4), channel_id=1, source_target_pairs={{0,1},{1,2},{2,3},{3,4},{4,5},{5,6},{6,7},{7,8},{8,9},{9,10},{10,1... | collective-permute-start | bytes 835592 | tf_op jit(solution)/shard_map/ppermute | solution.py:364
  24.1 4.6 %copy-start.4 = (f32[64,128,128]{2,1,0:T(8,128)}, f32[64,128,128]{2,1,0:T(8,128)S(1)}, u32[]{:S(2)}) copy-start(f32[64,128,128]{2,1,0:T(8,128)S(1)} %bitcast_select_fusion.refs_0_) | copy-start | bytes 12582916
  24.1 7.1 %copy-start.5 = (s32[4,16,6]{1,0,2:T(4,128)S(1)}, s32[4,16,6]{1,0,2:T(4,128)}, u32[]{:S(2)}) copy-start(s32[4,16,6]{1,0,2:T(4,128)} %param.14) | copy-start | bytes 4612
  24.1 8.6 %copy-start.20 = (f32[4,3]{1,0:T(4,128)S(1)}, f32[4,3]{1,0:T(4,128)}, u32[]{:S(2)}) copy-start(f32[4,3]{1,0:T(4,128)} %param.16) | copy-start | bytes 148
  25.6 95.7 %collective-permute-start = (f32[16,136,128]{2,1,0:T(8,128)}, f32[16,136,128]{2,1,0:T(8,128)S(1)}, u32[]{:S(2)}, u32[]{:S(2)}) collective-permute-start(f32[16,136,128]{2,1,0:T(8,128)} %pad_maximum_fusion), channel_id=1, source_target_pairs={{0,16},{1,17},{2,18},{3,19},{4,20},{5,21},{6,22},{7,23},{8,24},{9,... | collective-permute-start | bytes 3342344 | tf_op jit(solution)/shard_map/ppermute | solution.py:364
  28.7 92.6 %collective-permute-start.1 = (f32[16,136,128]{2,1,0:T(8,128)}, f32[16,136,128]{2,1,0:T(8,128)}, u32[]{:S(2)}, u32[]{:S(2)}) collective-permute-start(f32[16,136,128]{2,1,0:T(8,128)} %pad_maximum_fusion.1), channel_id=1, source_target_pairs={{16,0},{17,1},{18,2},{19,3},{20,4},{21,5},{22,6},{23,7},{24,8},{25... | collective-permute-start | bytes 3342344 | tf_op jit(solution)/shard_map/ppermute | solution.py:364
  98.7 22.6 %collective-permute-start.3 = (f32[4,136,128]{2,1,0:T(8,128)S(1)}, f32[4,136,128]{2,1,0:T(8,128)S(1)}, u32[]{:S(2)}, u32[]{:S(2)}) collective-permute-start(f32[4,136,128]{2,1,0:T(8,128)S(1)} %pad_maximum_fusion.5), channel_id=1, source_target_pairs={{0,15},{1,0},{2,1},{3,2},{4,3},{5,4},{6,5},{7,6},{8,7},{9,8},{10,9... | collective-permute-start | bytes 835592 | tf_op jit(solution)/shard_map/ppermute | solution.py:364
  104.7 9.9 %collective-permute-start.6 = (f32[1,152,128]{2,1,0:T(8,128)S(1)}, f32[1,152,128]{2,1,0:T(8,128)S(1)}, u32[]{:S(2)}, u32[]{:S(2)}) collective-permute-start(f32[1,152,128]{2,1,0:T(8,128)S(1)} %maximum_bitcast_fusion.2), channel_id=1, source_target_pairs={{16,1},{17,2},{18,3},{19,4},{20,5},{21,6},{22,7},{23,8},{24,9},{25... | collective-permute-start | bytes 233480 | tf_op jit(solution)/shard_map/ppermute | solution.py:364
  114.7 6.7 %copy-start.14 = (f32[1,152,128]{2,1,0:T(8,128)}, f32[1,152,128]{2,1,0:T(8,128)S(1)}, u32[]{:S(2)}) copy-start(f32[1,152,128]{2,1,0:T(8,128)S(1)} %collective-permute-done.6.refs_7_) | copy-start | bytes 233476
  114.7 6.6 %collective-permute-start.7 = (f32[1,152,128]{2,1,0:T(8,128)S(1)}, f32[1,152,128]{2,1,0:T(8,128)S(1)}, u32[]{:S(2)}, u32[]{:S(2)}) collective-permute-start(f32[1,152,128]{2,1,0:T(8,128)S(1)} %maximum_bitcast_fusion.3), channel_id=1, source_target_pairs={{16,15},{17,0},{18,1},{19,2},{20,3},{21,4},{22,5},{23,6},{24,7},{2... | collective-permute-start | bytes 233480 | tf_op jit(solution)/shard_map/ppermute | solution.py:364
  121.3 0.6 copy-start.16
  121.3 0.7 copy-start.9
  121.3 1.1 copy-start.6
  163.2 2.2 copy-start.1
  165.4 20.1 %copy-start.19 = (s32[512]{0:T(512)S(1)}, s32[512]{0:T(512)}, u32[]{:S(2)}) copy-start(s32[512]{0:T(512)} %param.19) | copy-start | bytes 6148
  179.1 2.0 copy-start.2
  181.1 15.8 %all-to-all-start = ((f32[128,4,128]{2,1,0:T(4,128)}), f32[128,4,128]{2,1,0:T(4,128)S(1)}, u32[]{:S(2)}, u32[]{:S(2)}) async-start(f32[128,4,128]{2,1,0:T(4,128)} %bitcast.33), calls=%async_computation | async-start | bytes 524288 | tf_op jit(solution)/shard_map/all_to_all | solution.py:418
  196.9 2.2 copy-start.3
  207.5 11.1 %copy-start = (f32[64,128,128]{2,1,0:T(8,128)}, f32[64,128,128]{2,1,0:T(8,128)S(1)}, u32[]{:S(2)}) copy-start(f32[64,128,128]{2,1,0:T(8,128)S(1)} %shard_map.133.refs_0_) | copy-start | bytes 12582916
  207.7 14.5 %collective-permute-start.15 = (f32[1,152,128]{2,1,0:T(8,128)S(1)}, f32[1,152,128]{2,1,0:T(8,128)S(1)}, u32[]{:S(2)}, u32[]{:S(2)}) collective-permute-start(f32[1,152,128]{2,1,0:T(8,128)S(1)} %maximum_bitcast_fusion.7), channel_id=1, source_target_pairs={{16,15},{17,0},{18,1},{19,2},{20,3},{21,4},{22,5},{23,6},{24,7},{2... | collective-permute-start | bytes 233480 | tf_op jit(solution)/shard_map/ppermute | solution.py:364
  211.0 32.6 %collective-permute-start.9 = (f32[16,136,128]{2,1,0:T(8,128)S(1)}, f32[16,136,128]{2,1,0:T(8,128)S(1)}, u32[]{:S(2)}, u32[]{:S(2)}) collective-permute-start(f32[16,136,128]{2,1,0:T(8,128)S(1)} %pad_maximum_fusion.3), channel_id=1, source_target_pairs={{16,0},{17,1},{18,2},{19,3},{20,4},{21,5},{22,6},{23,7},{24,8},{25... | collective-permute-start | bytes 3342344 | tf_op jit(solution)/shard_map/ppermute | solution.py:364
  213.0 30.6 %collective-permute-start.8 = (f32[16,136,128]{2,1,0:T(8,128)S(1)}, f32[16,136,128]{2,1,0:T(8,128)S(1)}, u32[]{:S(2)}, u32[]{:S(2)}) collective-permute-start(f32[16,136,128]{2,1,0:T(8,128)S(1)} %pad_maximum_fusion.2), channel_id=1, source_target_pairs={{0,16},{1,17},{2,18},{3,19},{4,20},{5,21},{6,22},{7,23},{8,24},{9,... | collective-permute-start | bytes 3342344 | tf_op jit(solution)/shard_map/ppermute | solution.py:364
  216.6 12.2 %collective-permute-start.14 = (f32[1,152,128]{2,1,0:T(8,128)S(1)}, f32[1,152,128]{2,1,0:T(8,128)S(1)}, u32[]{:S(2)}, u32[]{:S(2)}) collective-permute-start(f32[1,152,128]{2,1,0:T(8,128)S(1)} %maximum_bitcast_fusion.6), channel_id=1, source_target_pairs={{16,1},{17,2},{18,3},{19,4},{20,5},{21,6},{22,7},{23,8},{24,9},{25... | collective-permute-start | bytes 233480 | tf_op jit(solution)/shard_map/ppermute | solution.py:364
  218.7 24.9 %collective-permute-start.11 = (f32[4,136,128]{2,1,0:T(8,128)S(1)}, f32[4,136,128]{2,1,0:T(8,128)S(1)}, u32[]{:S(2)}, u32[]{:S(2)}) collective-permute-start(f32[4,136,128]{2,1,0:T(8,128)S(1)} %pad_maximum_fusion.7), channel_id=1, source_target_pairs={{0,15},{1,0},{2,1},{3,2},{4,3},{5,4},{6,5},{7,6},{8,7},{9,8},{10,9... | collective-permute-start | bytes 835592 | tf_op jit(solution)/shard_map/ppermute | solution.py:364
  222.3 21.4 %copy-start.12 = (f32[1,152,128]{2,1,0:T(8,128)}, f32[1,152,128]{2,1,0:T(8,128)S(1)}, u32[]{:S(2)}) copy-start(f32[1,152,128]{2,1,0:T(8,128)S(1)} %collective-permute-done.15.refs_8_) | copy-start | bytes 233476
  222.3 21.3 %collective-permute-start.10 = (f32[4,136,128]{2,1,0:T(8,128)S(1)}, f32[4,136,128]{2,1,0:T(8,128)S(1)}, u32[]{:S(2)}, u32[]{:S(2)}) collective-permute-start(f32[4,136,128]{2,1,0:T(8,128)S(1)} %pad_maximum_fusion.6), channel_id=1, source_target_pairs={{0,1},{1,2},{2,3},{3,4},{4,5},{5,6},{6,7},{7,8},{8,9},{9,10},{10,1... | collective-permute-start | bytes 835592 | tf_op jit(solution)/shard_map/ppermute | solution.py:364
  228.8 14.8 %copy-start.13 = (f32[1,152,128]{2,1,0:T(8,128)}, f32[1,152,128]{2,1,0:T(8,128)S(1)}, u32[]{:S(2)}) copy-start(f32[1,152,128]{2,1,0:T(8,128)S(1)} %collective-permute-done.14.refs_7_) | copy-start | bytes 233476
  228.8 5.7 %collective-permute-start.13 = (f32[1,152,128]{2,1,0:T(8,128)S(1)}, f32[1,152,128]{2,1,0:T(8,128)S(1)}, u32[]{:S(2)}, u32[]{:S(2)}) collective-permute-start(f32[1,152,128]{2,1,0:T(8,128)S(1)} %maximum_bitcast_fusion.5), channel_id=1, source_target_pairs={{0,31},{1,16},{2,17},{3,18},{4,19},{5,20},{6,21},{7,22},{8,23},{9,... | collective-permute-start | bytes 233480 | tf_op jit(solution)/shard_map/ppermute | solution.py:364
  234.5 9.1 %copy-start.15 = (f32[1,152,128]{2,1,0:T(8,128)}, f32[1,152,128]{2,1,0:T(8,128)S(1)}, u32[]{:S(2)}) copy-start(f32[1,152,128]{2,1,0:T(8,128)S(1)} %collective-permute-done.13.refs_6_) | copy-start | bytes 233476
  234.5 9.0 %collective-permute-start.12 = (f32[1,152,128]{2,1,0:T(8,128)S(1)}, f32[1,152,128]{2,1,0:T(8,128)S(1)}, u32[]{:S(2)}, u32[]{:S(2)}) collective-permute-start(f32[1,152,128]{2,1,0:T(8,128)S(1)} %maximum_bitcast_fusion.4), channel_id=1, source_target_pairs={{0,17},{1,18},{2,19},{3,20},{4,21},{5,22},{6,23},{7,24},{8,25},{9,... | collective-permute-start | bytes 233480 | tf_op jit(solution)/shard_map/ppermute | solution.py:364
  243.6 0.6 copy-start.17
  243.6 0.7 copy-start.10
  243.6 0.8 copy-start.11
  243.6 1.2 copy-start.7
  244.8 1.0 copy-start.8

commit v2 on v1

v2 whole, which is shorter than its diff:
```python
import functools

import jax
import jax.numpy as jnp
from jax import lax
from jax.experimental import pallas as pl
from jax.experimental.pallas import tpu as pltpu
from jax.sharding import PartitionSpec as P

AXES = ("ax", "az")
F32, BF16, I32 = jnp.float32, jnp.bfloat16, jnp.int32

wall_gain = 4.0
time_step = 0.05
MIB = 1 << 20


def rows_of(x, n):
    return jnp.broadcast_to(x, (n,) + x.shape[1:])


def sub_iota(shape):
    return lax.broadcasted_iota(I32, shape, 0)


def halves(x):
    hi = x.astype(BF16)
    return hi, (x - hi.astype(F32)).astype(BF16)


def thirds(x):
    hi = x.astype(BF16).astype(F32)
    rest = x - hi
    mid = rest.astype(BF16).astype(F32)
    return hi, mid, rest - mid


def loop(n, body):
    def step(i, carry):
        body(i)
        return carry

    lax.fori_loop(0, n, step, 0)


ROWS_K = 32
CODE_ROW = 135


def step_kernel(rows, cols, leaving, codes, surf, *refs):
    (cells, a_low, a_high, z_low, z_high, corner_low, corner_high) = refs[:7]
    if leaving:
        slots, buffer_row, out, sent, gathered = refs[7:12]
        scratch = refs[12:]
    else:
        out, dens = refs[7:9]
        scratch = refs[9:]
    side_t, side_s, feat, squares, row_t, row_s, mass, root, rho, ratio, inverse, ring_codes, semaphore = scratch
    width = cols + 4
    own = rows * cols
    sub8 = sub_iota((8, 128))
    eye = (sub_iota((128, 128)) == lax.broadcasted_iota(I32, (128, 128), 1)).astype(F32).astype(BF16)
    row_mid, col_mid = (rows + 3) / 2.0, (cols + 3) / 2.0

    parts = ((a_low, 0, cols), (a_high, cols, cols), (z_low, 2 * cols, rows), (z_high, 2 * cols + rows, rows), (corner_low, 2 * cols + 2 * rows, 2), (corner_high, 2 * cols + 2 * rows + 2, 2))
    copies = [pltpu.make_async_copy(ref.at[:, CODE_ROW, :], ring_codes.at[pl.ds(first, n), :], semaphore.at[k]) for k, (ref, first, n) in enumerate(parts)]
    for copy in copies:
        copy.start()

    def geometry(ref, cell, height, row, n, index, apart, r, c, center):
        flat = ref.reshape(ref.shape[0] * height, 128)

        def field(k):
            return flat[pl.ds(cell * height + row + k, n, stride=height), :]

        x = [field(0) + (r - row_mid), field(1) + (c - col_mid), field(2)]
        norm = x[0] * x[0] + x[1] * x[1] + x[2] * x[2]
        m = field(6)
        cube = jnp.exp2(jnp.log2(jnp.maximum(m, 1e-30)) * (1.0 / 3.0))
        cube = cube - (cube - m / (cube * cube)) * (1.0 / 3.0)
        cube = jnp.where(m > 0.0, cube, 0.0)

        def put(target, k, value):
            target[pl.ds(index * ROWS_K + k, n, stride=apart * ROWS_K), :] = value

        for k, value in enumerate([x[0] * cube, x[1] * cube, x[2] * cube, -norm * cube, cube]):
            hi, mid, low = thirds(value)
            for block, piece in enumerate((hi, mid, low, hi, mid, hi)):
                put(row_t, 5 * block + k, piece)
        put(row_t, 30, jnp.zeros_like(m))
        put(row_t, 31, jnp.zeros_like(m))
        for k in range(n):
            mass[pl.ds(index + k * apart, 1), :] = m[k : k + 1]
            root[pl.ds(index + k * apart, 1), :] = cube[k : k + 1]
        if center:
            for k, value in enumerate([x[0] + x[0], x[1] + x[1], x[2] + x[2], jnp.ones_like(m), 1.0 - norm]):
                hi, mid, low = thirds(value)
                for block, piece in enumerate((hi, hi, hi, mid, mid, low)):
                    put(row_s, 5 * block + k, piece)
            put(row_s, 30, jnp.zeros_like(m))
            put(row_s, 31, jnp.zeros_like(m))

    def sub(n):
        return sub_iota((n, 128)).astype(F32)

    per = 8

    def local_geo(i):
        first = i * per
        r, c = first // cols + 2, first % cols + 2
        geometry(cells, first, 128, 0, per, r * width + c, 1, r.astype(F32), c.astype(F32) + sub(per), True)

    loop(own // per, local_geo)
    for ref, first, second in ((a_low, 1, 0), (a_high, rows + 2, rows + 3)):
        for k in range(0, cols, per):
            c = k + 2.0 + sub(per)
            geometry(ref, k, 136, 0, per, first * width + k + 2, 1, float(first), c, True)
            geometry(ref, k, 136, 128, per, second * width + k + 2, 1, float(second), c, False)
    for ref, first, second in ((z_low, 1, 0), (z_high, cols + 2, cols + 3)):
        r = 2.0 + sub(rows)
        geometry(ref, 0, 136, 0, rows, 2 * width + first, width, r, float(first), True)
        geometry(ref, 0, 136, 128, rows, 2 * width + second, width, r, float(second), False)
    for ref, k1, k0 in ((corner_low, 1, 0), (corner_high, cols + 2, cols + 3)):
        for n, (r1, r0) in enumerate(((1, 0), (rows + 2, rows + 3))):
            for row, r, k, center in ((0, r1, k1, True), (128, r0, k1, False), (136, r1, k0, False), (144, r0, k0, False)):
                geometry(ref, n, 152, row, 1, r * width + k, 1, float(r), float(k), center)

    def block32(ref, index):
        return ref[pl.ds(pl.multiple_of(index * ROWS_K, ROWS_K), ROWS_K), :].astype(BF16)

    zero_t = jnp.zeros((96, 128), BF16)
    turns = 10

    def turn(i):
        for k in range(turns // 2):
            index = i * turns + 2 * k
            rhs = jnp.concatenate([block32(row_t, index), zero_t, block32(row_t, index + 1), zero_t], axis=0)
            t = lax.dot_general(eye, rhs, (((1,), (1,)), ((), ())), preferred_element_type=F32)
            for n in range(2):
                side_t[index + n] = t[:, n * 128 : (n + 1) * 128].astype(BF16)
                side_s[index + n] = block32(row_s, index + n)

    loop((rows + 4) * width // turns, turn)

    for copy in copies:
        copy.wait()
    zero_s = jnp.zeros((96, 128), BF16)

    def density(center, partners, n):
        rhs = jnp.concatenate([side_s[center], zero_s], axis=0)
        total = jnp.zeros((8, 128), F32)
        for j, partner in enumerate(partners):
            y = jnp.maximum(jnp.dot(side_t[partner], rhs, preferred_element_type=F32), 0.0)
            square = y * y
            total = total + jnp.sum((square * y).reshape(16, 8, 128), axis=0)
            if n is not None:
                squares[n, j * 128 : (j + 1) * 128, :] = square.astype(BF16)
        rho[pl.ds(center, 1), :] = jnp.sum(total, axis=0, keepdims=True)

    def linked(center, code):
        up = (code * 11) >> 5
        return center + up * (width - 3) + code - (width + 1)

    def own_cell(n):
        r, c = n // cols, n % cols
        center = (r + 2) * width + c + 2
        return r, c, center, [linked(center, codes[r, c, j]) for j in range(6)]

    def own_density(i):
        for k in range(8):
            n = i * 8 + k
            r, c, center, partners = own_cell(n)
            density(center, partners, n)

    loop(own // 8, own_density)

    def ring_cell(center, n):
        density(center, [linked(center, ring_codes[n, j].astype(I32)) for j in range(6)], None)

    def a_density(i):
        for k in range(4):
            n = i * 4 + k
            ring_cell(width + n + 2, n)
            ring_cell((rows + 2) * width + n + 2, cols + n)

    loop(cols // 4, a_density)
    for k in range(rows):
        ring_cell((k + 2) * width + 1, 2 * cols + k)
        ring_cell((k + 2) * width + cols + 2, 2 * cols + rows + k)
    for k, r in enumerate((1, rows + 2)):
        ring_cell(r * width + 1, 2 * cols + 2 * rows + k)
        ring_cell(r * width + cols + 2, 2 * cols + 2 * rows + 2 + k)

    living = mass[...] > 0.0
    guarded = jnp.where(living, rho[...], 1.0)
    ratio[...] = jnp.where(living, (guarded - 1.0) / (guarded * guarded), 0.0)
    inverse[...] = jnp.where(living, 1.0 / guarded, 0.0)

    def row8(ref, index):
        return rows_of(ref[pl.ds(index, 1), :], 8)

    def shifted(g, r, c):
        off_r = r.astype(F32) - row_mid
        off_c = c.astype(F32) - col_mid
        return jnp.where(sub8 == 0, g + off_r, jnp.where(sub8 == 1, g + off_c, g))

    def positions(g, r, c):
        x = shifted(g, r, c)
        return jnp.where((sub8 == 0) | (sub8 == 4), 1.0, jnp.where(sub8 < 4, pltpu.roll(x, 1, 0), pltpu.roll(x, 5, 0)))

    def features(ref, n, r, c):
        index = r * width + c
        cube = row8(root, index)
        scale = cube * row8(inverse, index)

        def load(k):
            return ref[n, 8 * k : 8 * k + 8, :]

        g = load(0)
        nu = rows_of(g[7:8], 8)
        first = jnp.where(sub8 < 3, pltpu.roll(g, 5, 0) * nu, jnp.where(sub8 == 6, 1.0, g)) * scale
        press = positions(g, r, c) * jnp.where(sub8 < 4, cube, cube * row8(ratio, index))
        hi, lo = halves(press)
        feat[index, 128:144, :] = jnp.concatenate([hi.astype(F32), lo.astype(F32)], axis=0).astype(BF16)
        feat[index, 0:16, :] = jnp.concatenate([first, load(1) * scale], axis=0).astype(BF16)
        for k in range(1, 8):
            feat[index, 16 * k : 16 * k + 16, :] = jnp.concatenate([load(2 * k) * scale, load(2 * k + 1) * scale], axis=0).astype(BF16)

    def local_feat(i):
        for k in range(4):
            n = i * 4 + k
            features(cells, n, n // cols + 2, n % cols + 2)

    loop(own // 4, local_feat)

    def a_feat(i):
        for k in range(2):
            n = i * 2 + k
            features(a_low, n, jnp.int32(1), n + 2)
            features(a_high, n, jnp.int32(rows + 2), n + 2)

    loop(cols // 2, a_feat)

    def z_feat(i):
        features(z_low, i, i + 2, jnp.int32(1))
        features(z_high, i, i + 2, jnp.int32(cols + 2))

    loop(rows, z_feat)
    for n, r in enumerate((1, rows + 2)):
        features(corner_low, n, jnp.int32(r), jnp.int32(1))
        features(corner_high, n, jnp.int32(r), jnp.int32(cols + 2))

    def force(n):
        r, c, index, partners = own_cell(n)
        lhs = jnp.concatenate([feat[partner] for partner in partners], axis=1)
        sums = jnp.dot(lhs, squares[n], preferred_element_type=F32)
        g = cells[n, 0:8, :]
        m, nu = rows_of(g[6:7], 8), rows_of(g[7:8], 8)
        alive = jnp.where(m > 0.0, time_step, 0.0)
        first = sums[0:8]
        press = sums[128:136] + sums[136:144]
        press = press - positions(g, r + 2, c + 2) * jnp.where(sub8 < 4, rows_of(press[0:1], 8), rows_of(press[4:5], 8))
        press = press * jnp.where(sub8 < 4, row8(ratio, index), 1.0)
        press = press + pltpu.roll(press, 4, 0)
        weight, friction = rows_of(first[6:7], 8), rows_of(first[7:8], 8)
        surface = jnp.where(sub8 == 3, surf[n * 4], jnp.where(sub8 == 4, surf[n * 4 + 1], surf[n * 4 + 2]))
        wall = wall_gain * jnp.maximum(1.0 - 3.0 * rows_of(g[2:3], 8), 0.0)
        accel = nu * (first - g * weight) + pltpu.roll(first, 3, 0) - g * friction + wall * (surface - g)
        accel = accel - 6.0 * pltpu.roll(press, 2, 0)
        velocity = g + accel * alive
        position = g + time_step * pltpu.roll(velocity, 5, 0)
        out[n, 0:8, :] = jnp.where(sub8 < 3, position, jnp.where(sub8 < 6, velocity, g))
        gain = 2.0 * alive
        stay = 1.0 - gain * weight
        for k in range(1, 16):
            out[n, 8 * k : 8 * k + 8, :] = cells[n, 8 * k : 8 * k + 8, :] * stay + gain * sums[8 * k : 8 * k + 8]
        if not leaving:
            dens[pl.ds(n, 1), :] = jnp.where(m > 0.0, row8(rho, index), 0.0)[0:1]

    def forces(i):
        for k in range(8):
            force(i * 8 + k)

    loop(own // 8, forces)
    if leaving:
        take_out(out, slots, buffer_row, sent, gathered)


def take_out(state, slots, buffer_row, sent, gathered):
    leaving, places = slots.shape[0], sent.shape[0]
    offset = jnp.broadcast_to(slots[...], (leaving, 128)) - lax.broadcasted_iota(I32, (leaving, 128), 1)
    gathered[...] = jnp.zeros_like(gathered)
    per = 4

    def body(i):
        hits, pieces = [], []
        for k in range(per):
            c = i * per + k
            hit = jnp.where(offset == c * 128, 1.0, 0.0)
            gone = jnp.sum(hit, axis=0, keepdims=True)
            whole = state[c]
            hi, lo = halves(whole)
            hits.append(hit.astype(BF16))
            pieces.append(jnp.concatenate([hi, lo], axis=0))
            state[c] = whole * (1.0 - gone)
        gathered[...] += lax.dot_general(jnp.concatenate(hits, axis=1), jnp.concatenate(pieces, axis=1), (((1,), (1,)), ((), ())), preferred_element_type=F32)

    loop(state.shape[0] // per, body)
    place = jnp.where(jnp.broadcast_to(buffer_row[...], (places, leaving)) == sub_iota((places, leaving)), 1.0, 0.0).astype(BF16)
    right = jnp.concatenate([gathered[...].astype(BF16), jnp.ones((leaving, 128), BF16)], axis=1)
    sums = jnp.dot(place, right, preferred_element_type=F32)
    lane = lax.broadcasted_iota(I32, (places, 128), 1)
    sent[...] = jnp.where((lane == 6) & (sums[:, 256:384] < 0.5), -1.0, sums[:, 0:128] + sums[:, 128:256])


def smem_spec():
    return pl.BlockSpec(memory_space=pltpu.SMEM)


def vmem_spec():
    return pl.BlockSpec(memory_space=pltpu.VMEM)


def step_call(rows, cols, codes, surface, cells, halo, leave=None):
    own = rows * cols
    patch = (rows + 4) * (cols + 4)
    ring = 2 * (rows + 2) + 2 * cols
    new = jax.ShapeDtypeStruct((own, 128, 128), F32)
    extra = []
    if leave:
        slots, buffer_row, places = leave
        outs = (new, jax.ShapeDtypeStruct((places, 128), F32))
        extra, first = [slots, buffer_row], [pltpu.VMEM((slots.shape[0], 256), F32)]
    else:
        outs, first = (new, jax.ShapeDtypeStruct((own, 128), F32)), []
    return pl.pallas_call(
        functools.partial(step_kernel, rows, cols, bool(leave)),
        out_shape=outs,
        in_specs=[smem_spec(), smem_spec()] + [vmem_spec()] * (7 + len(extra)),
        out_specs=(vmem_spec(), vmem_spec()),
        scratch_shapes=first
        + [
            pltpu.VMEM((patch, 128, 128), BF16),
            pltpu.VMEM((patch, 32, 128), BF16),
            pltpu.VMEM((patch, 144, 128), BF16),
            pltpu.VMEM((own, 768, 128), BF16),
            pltpu.VMEM((patch * ROWS_K, 128), F32),
            pltpu.VMEM((patch * ROWS_K, 128), F32),
        ]
        + [pltpu.VMEM((patch, 128), F32)] * 5
        + [pltpu.SMEM((ring, 128), F32), pltpu.SemaphoreType.DMA((6,))],
        compiler_params=pltpu.CompilerParams(vmem_limit_bytes=60 * MIB),
    )(codes, surface, cells, *halo, *extra)


def put_strips(state, rows, cols, codes, strips):
    a_up, a_down, z_up, z_down = strips
    lane = lax.broadcasted_iota(I32, (8, 128), 1)
    sub8 = sub_iota((8, 128))

    def coded(behind, r, c):
        listed = jnp.zeros((8, 128), F32)
        for j in range(6):
            listed = jnp.where(lane == j, codes[r, c, j].astype(F32), listed)
        return jnp.where(sub8 == 7, listed, behind)

    def along(n):
        for strip, first, second in ((a_up, rows - 1, rows - 2), (a_down, 0, 1)):
            strip[n, 0:128, :] = state(first * cols + n, 128)
            strip[n, 128:136, :] = coded(state(second * cols + n, 8), first, n)

    loop(cols, along)

    def across(n):
        for strip, first, second in ((z_up, cols - 1, cols - 2), (z_down, 0, 1)):
            strip[n, 0:128, :] = state(n * cols + first, 128)
            strip[n, 128:136, :] = coded(state(n * cols + second, 8), n, first)

    loop(rows, across)


def strip_shapes(rows, cols):
    return tuple(jax.ShapeDtypeStruct((n, 136, 128), F32) for n in (cols, cols, rows, rows))


def mask_kernel(rows, cols, counts, codes, state, *strips):
    def cell(n, height):
        held = lax.broadcasted_iota(I32, (height, 128), 1) < counts[n // cols, n % cols]
        return jnp.where(held, state[n, 0:height, :], 0.0)

    put_strips(cell, rows, cols, codes, strips)


def mask_strips(rows, cols, counts, codes, state):
    return pl.pallas_call(
        functools.partial(mask_kernel, rows, cols),
        out_shape=strip_shapes(rows, cols),
        in_specs=[smem_spec(), smem_spec(), vmem_spec()],
        out_specs=(vmem_spec(),) * 4,
        compiler_params=pltpu.CompilerParams(vmem_limit_bytes=40 * MIB),
    )(counts, codes, state)


def insert_kernel(rows, cols, codes, state, incoming, slots, out, *strips):
    places = slots.shape[0]
    data = incoming[...]
    absent = jnp.broadcast_to(data[:, 6:7], (places, 128)) < 0.0
    offset = jnp.broadcast_to(slots[...], (places, 128)) - lax.broadcasted_iota(I32, (places, 128), 1)
    offset = jnp.where(absent, -1, offset)
    hi, lo = halves(jnp.transpose(data))
    left = jnp.concatenate([hi, lo, jnp.ones((16, places), BF16)], axis=0)
    per = 4

    def body(i):
        for pair in range(per // 2):
            first = i * per + pair * 2
            hits = [jnp.where(offset == (first + k) * 128, 1.0, 0.0).astype(BF16) for k in range(2)]
            sums = jnp.dot(left, jnp.concatenate(hits, axis=1), preferred_element_type=F32)
            for k in range(2):
                part = sums[:, 128 * k : 128 * (k + 1)]
                out[first + k] = state[first + k] * (1.0 - part[256:257]) + (part[0:128] + part[128:256])

    loop(rows * cols // per, body)
    put_strips(lambda n, height: out[n, 0:height, :], rows, cols, codes, strips)


def insert(rows, cols, codes, state, incoming, slots):
    return pl.pallas_call(
        functools.partial(insert_kernel, rows, cols),
        out_shape=(jax.ShapeDtypeStruct(state.shape, F32),) + strip_shapes(rows, cols),
        in_specs=[smem_spec()] + [vmem_spec()] * 3,
        out_specs=(vmem_spec(),) * 5,
        compiler_params=pltpu.CompilerParams(vmem_limit_bytes=48 * MIB),
    )(codes, state, incoming, slots)


def exchange(strips):
    n_ax, n_az = lax.axis_size("ax"), lax.axis_size("az")
    a_up, a_down, z_up, z_down = strips
    up = [(i, i + 1) for i in range(n_ax - 1)]
    around = [(i, (i + 1) % n_az) for i in range(n_az)]
    a_low = lax.ppermute(a_up, "ax", up)
    a_high = lax.ppermute(a_down, "ax", [(j, i) for i, j in up])
    z_low = lax.ppermute(z_up, "az", around)
    z_high = lax.ppermute(z_down, "az", [(j, i) for i, j in around])

    def corner(end, behind):
        return jnp.stack([jnp.concatenate([x[end], x[behind, 0:8], x[behind, 128:136]], axis=0) for x in (a_low, a_high)])

    corner_low = lax.ppermute(corner(-1, -2), "az", around)
    corner_high = lax.ppermute(corner(0, 1), "az", [(j, i) for i, j in around])
    return a_low, a_high, z_low, z_high, corner_low, corner_high


def local(particles, counts, pair_codes, contact, twist_state, leaving_slot, leaving_dest, arrival_slot):
    rows, cols, fields, block = particles.shape
    ranks = lax.axis_size("ax") * lax.axis_size("az")
    own = rows * cols

    flat = particles.reshape(own, fields, block)
    halo = exchange(mask_strips(rows, cols, counts, pair_codes, flat))

    segments = twist_state.shape[0]
    told = jnp.broadcast_to(twist_state.reshape(1, segments * 3), (ranks, segments * 3))
    twist = lax.all_to_all(told, AXES, 0, 0, tiled=True).reshape(ranks * segments, 3)
    surface = jnp.pad(twist[contact.reshape(own)], ((0, 0), (0, 1))).reshape(-1)

    dest = leaving_dest[:, 0]
    leaving = dest.shape[0]
    same = dest[:, None] == dest[None, :]
    earlier = lax.broadcasted_iota(I32, (leaving, leaving), 0) > lax.broadcasted_iota(I32, (leaving, leaving), 1)
    order = jnp.sum((same & earlier).astype(I32), axis=1)
    capacity = arrival_slot.shape[0] // ranks
    buffer_row = (dest * capacity + order).reshape(1, leaving)

    keep = lax.broadcasted_iota(I32, (own, block), 1) < counts.reshape(own, 1)
    state = jnp.where(keep[:, None, :], flat, 0.0)
    state, outgoing = step_call(rows, cols, pair_codes, surface, state, halo, (leaving_slot.reshape(-1, 1), buffer_row, ranks * capacity))
    incoming = lax.all_to_all(outgoing.reshape(ranks, capacity, fields), AXES, 0, 0, tiled=True)
    state, *strips = insert(rows, cols, pair_codes, state, incoming.reshape(-1, fields), arrival_slot.reshape(-1, 1))
    state, density = step_call(rows, cols, pair_codes, surface, state, exchange(strips))
    return state.reshape(particles.shape), density.reshape(rows, cols, block)


def solution(mesh):
    both = P("ax", "az")
    flat = P(AXES)
    return jax.shard_map(
        local,
        mesh=mesh,
        in_specs=(P("ax", "az", None, None), both, P("ax", "az", None), both, P(AXES, None), flat, P(AXES, None), flat),
        out_specs=(P("ax", "az", None, None), P("ax", "az", None)),
        check_vma=False,
    )
```

time: 288 us -> 166 us (0.58)
  blocking collectives: 54.2 us -> 0 us
  Pallas kernels: 104 us -> 71.2 us
  local copies, waits for them, and re-layouts: 25.1 us -> 12.1 us
  other arithmetic: 16.8 us -> 6.83 us
  starting transfers between devices: 48.8 us -> 41.7 us
  waiting for transfers between devices: 36.8 us -> 32.9 us
    all_gather x1 -> x0, blocking collectives: 54.2 us -> none  [local(): lax.all_gather(packed.reshape(-1, 128), AXES).reshape(ranks, padded)]
    pallas_call x4, Pallas kernels: 104 us -> 71.2 us  [the longest x2 58.8 us: step_call(): pl.pallas_call(functools.partial(step_kernel, rows, cols, bool(leave)), o...]
    ppermute x16 -> x12, starting transfers between devices: 44.4 us -> 29.7 us  [the longest x2 9.43 us: exchange(): z_high = lax.ppermute(z_down, 'az', [(j, i) for i, j in around])]
    all_to_all x0 -> x1, starting transfers between devices: none -> 6.37 us  [local(): lax.all_to_all(told, AXES, 0, 0, tiled=True).reshape(ranks * segments, 3)]
    unnamed x61 -> x39, local copies, waits for them, and re-layouts: 10.4 us -> 5.03 us
    concatenate x9 -> x0, other arithmetic: 5.07 us -> none  [the longest x4 2.59 us: ax_part(): return jnp.concatenate([grid[first], grid[second, :, 0:8]], axis=1)]
    ppermute x16 -> x12, waiting for transfers between devices: 25.6 us -> 21.7 us  [the longest x2 9.33 us: exchange(): corner_low = lax.ppermute(corner(-1, -2), 'az', around)]
    slice x6 -> x0, local copies, waits for them, and re-layouts: 3.19 us -> none  [the longest x1 1.66 us: local(): everyone[:, segments * 3:used].reshape(ranks * len(listed), partners)]
  transfers between devices with their start and end apart: 17 -> 14, of which waited for: 6 -> 6; matrix products, arithmetic and copies ran while one was open for 9% -> 8% of each run, Pallas kernels for 0% -> 0%
where the time goes in v2:
time: 166 us
  Pallas kernels  71.2 us (43%)
  starting transfers between devices  41.7 us (25%)
  waiting for transfers between devices  32.9 us (20%)
  local copies, waits for them, and re-layouts  12.1 us (7%)
  other arithmetic  6.83 us (4%)
    pallas_call x2, Pallas kernels, step_call(): pl.pallas_call(functools.partial(step_kernel, rows, cols, bool(leave)), o...  58.8 us
    all_to_all x1, waiting for transfers between devices, local(): lax.all_to_all(outgoing.reshape(ranks, capacity, fields), AXES, 0, 0, til...  11.3 us
    pallas_call x1, Pallas kernels, insert(): pl.pallas_call(functools.partial(insert_kernel, rows, cols), out_shape=(j...  10.4 us
    ppermute x2, starting transfers between devices, exchange(): z_high = lax.ppermute(z_down, 'az', [(j, i) for i, j in around])  9.43 us
    ppermute x2, waiting for transfers between devices, exchange(): corner_low = lax.ppermute(corner(-1, -2), 'az', around)  9.33 us
    ppermute x2, starting transfers between devices, exchange(): a_low = lax.ppermute(a_up, 'ax', up)  7.12 us
    ppermute x2, starting transfers between devices, exchange(): corner_high = lax.ppermute(corner(0, 1), 'az', [(j, i) for i, j in around])  6.73 us
    all_to_all x1, starting transfers between devices, local(): lax.all_to_all(told, AXES, 0, 0, tiled=True).reshape(ranks * segments, 3)  6.37 us
  transfers between devices with their start and end apart: 14, of which 6 were waited for; matrix products, arithmetic and copies ran while one was open for 8% of the time, Pallas kernels for 0%

profile of v2, /device:TPU:1, one launch (start us, length us, event | category | flops | bytes accessed | tf_op | source)
XLA Modules:
  0.0 165.8 jit_solution(5139514172248462709)
XLA Ops:
  0.6 0.8 copy.31.codes
  1.4 2.2 %copy-done = f32[4,16,128,128]{3,2,1,0:T(8,128)S(1)} copy-done((f32[4,16,128,128]{3,2,1,0:T(8,128)S(1)}, f32[4,16,128,128]{3,2,1,0:T(8,128)}, u32[]{:S(2)}) %copy-start) | copy-done | bytes 4194328
  3.6 0.7 copy-done.3
  4.3 2.0 %shard_map.95 = (f32[16,136,128]{2,1,0:T(8,128)S(1)}, f32[16,136,128]{2,1,0:T(8,128)S(1)}, f32[4,136,128]{2,1,0:T(8,128)S(1)}, f32[4,136,128]{2,1,0:T(8,128)S(1)}) custom-call(s32[4,16]{1,0:T(4,128)S(1)} %copy-done.3, s32[4,16,6]{2,1,0:T(8,128)S(1)} %copy.31.codes, f32[64,128,128]{2,1,0:T(8,128)S(1)} %bitcast.78), custom_call_target="tpu_custom_call" | custom-call | tf_op jit(solution)/shard_map/pallas_call | solution.py:395
  6.3 4.5 %collective-permute-start = (f32[16,136,128]{2,1,0:T(8,128)S(1)}, f32[16,136,128]{2,1,0:T(8,128)}, u32[]{:S(2)}, u32[]{:S(2)}) collective-permute-start(f32[16,136,128]{2,1,0:T(8,128)S(1)} %get-tuple-element.15), channel_id=1, source_target_pairs={{0,16},{16,32},{32,48},{48,64},{64,80},{80,96},{96,112},{1,17},{17... | collective-permute-start | bytes 3342344 | tf_op jit(solution)/shard_map/ppermute | solution.py:442
  10.9 1.9 %collective-permute-start.1 = (f32[16,136,128]{2,1,0:T(8,128)S(1)}, f32[16,136,128]{2,1,0:T(8,128)}, u32[]{:S(2)}, u32[]{:S(2)}) collective-permute-start(f32[16,136,128]{2,1,0:T(8,128)S(1)} %get-tuple-element.16), channel_id=1, source_target_pairs={{16,0},{32,16},{48,32},{64,48},{80,64},{96,80},{112,96},{17,1},{33... | collective-permute-start | bytes 3342344 | tf_op jit(solution)/shard_map/ppermute | solution.py:443
  12.8 1.4 collective-permute-start.2
  14.2 5.0 %collective-permute-start.3 = (f32[4,136,128]{2,1,0:T(8,128)S(1)}, f32[4,136,128]{2,1,0:T(8,128)}, u32[]{:S(2)}, u32[]{:S(2)}) collective-permute-start(f32[4,136,128]{2,1,0:T(8,128)S(1)} %get-tuple-element.18), channel_id=1, source_target_pairs={{1,0},{2,1},{3,2},{4,3},{5,4},{6,5},{7,6},{8,7},{9,8},{10,9},{11,1... | collective-permute-start | bytes 835592 | tf_op jit(solution)/shard_map/ppermute | solution.py:445
  19.1 0.1 broadcast_in_dim.21
  19.2 0.7 broadcast_in_dim.22
  19.9 6.4 %all-to-all-start = ((f32[128,1,12]{2,1,0:T(1,128)}), f32[128,1,12]{2,1,0:T(1,128)S(1)}, u32[]{:S(2)}, u32[]{:S(2)}) async-start(f32[128,1,12]{2,1,0:T(1,128)} %broadcast_in_dim.22), calls=%async_computation | async-start | bytes 131072 | tf_op jit(solution)/shard_map/all_to_all | solution.py:465
  26.3 0.1 lt.29
  26.4 0.1 reshape.113
  26.5 0.2 convert_reduce_fusion
  26.6 0.1 iota_compare_fusion.1
  26.7 0.6 bitcast_add_fusion.refs_8_
  27.3 5.1 %broadcast_select_fusion.refs_0_ = f32[64,128,128]{2,1,0:T(8,128)} fusion(pred[64,128]{1,0:T(8,128)(4,1)S(1)} %iota_compare_fusion.1, f32[4,16,128,128]{3,2,1,0:T(8,128)} %param.8), kind=kLoop, calls=%fused_computation.1 | loop fusion | flops 1048576 | bytes 8396800 | tf_op jit(solution)/shard_map/jit(_where)/select_n | solution.py:477
  32.4 0.7 slice_bitcast_fusion.19
  33.1 0.9 slice_bitcast_fusion.5
  34.1 0.7 slice_bitcast_fusion.17
  34.8 0.9 slice_bitcast_fusion.4
  35.8 5.6 %collective-permute-start.5 = (f32[2,152,128]{2,1,0:T(8,128)S(1)}, f32[2,152,128]{2,1,0:T(8,128)S(1)}, u32[]{:S(2)}, u32[]{:S(2)}) collective-permute-start(f32[2,152,128]{2,1,0:T(8,128)S(1)} %pad_maximum_fusion.1), channel_id=1, source_target_pairs={{1,0},{2,1},{3,2},{4,3},{5,4},{6,5},{7,6},{8,7},{9,8},{10,9},{11,1... | collective-permute-start | bytes 466952 | tf_op jit(solution)/shard_map/ppermute | solution.py:451
  41.4 0.1 collective-permute-start.4
  41.6 0.8 copy.28.refs_7_
  42.4 0.5 broadcast.41
  42.9 0.7 reduce.3
  43.6 0.1 reshape.112
  43.8 0.6 gather_fusion
  44.4 0.6 reshape.114.surf
  45.1 4.7 %collective-permute-done.4.refs_5_ = f32[2,152,128]{2,1,0:T(8,128)S(1)} collective-permute-done((f32[2,152,128]{2,1,0:T(8,128)S(1)}, f32[2,152,128]{2,1,0:T(8,128)S(1)}, u32[]{:S(2)}, u32[]{:S(2)}) %collective-permute-start.4) | collective-permute-done | bytes 155680 | tf_op jit(solution)/shard_map/ppermute | solution.py:450
  49.8 0.7 copy-done.11
  50.4 31.8 %shard_map.96 = (f32[64,128,128]{2,1,0:T(8,128)}, f32[512,128]{1,0:T(8,128)}) custom-call(s32[4,16,6]{2,1,0:T(8,128)} %copy-done.1, f32[256]{0:T(256)} %reshape.114.surf, f32[64,128,128]{2,1,0:T(8,128)} %broadcast_select_fusion.refs_0_, f32[16,136,128]{2,1,0:T(8,128)} %collective-permute-done.refs_1_, f32[16,136,128]{2,1,0:T(8,128)} %collective-permute-done.1.refs_2_, ...), custom_call_target="tpu_custom_call" | custom-call | tf_op jit(solution)/shard_map/pallas_call | solution.py:336
  82.2 5.6 %all-to-all-start.1 = ((f32[128,4,128]{2,1,0:T(4,128)}), f32[128,4,128]{2,1,0:T(4,128)S(1)}, u32[]{:S(2)}, u32[]{:S(2)}) async-start(f32[128,4,128]{2,1,0:T(4,128)} %bitcast.80), calls=%async_computation.1 | async-start | bytes 524288 | tf_op jit(solution)/shard_map/all_to_all | solution.py:479
  87.9 0.1 copy.30.slots
  88.0 11.3 %all-to-all-done.1 = f32[128,4,128]{2,1,0:T(4,128)S(1)} async-done(((f32[128,4,128]{2,1,0:T(4,128)}), f32[128,4,128]{2,1,0:T(4,128)S(1)}, u32[]{:S(2)}, u32[]{:S(2)}) %all-to-all-start.1) | async-done | bytes 262176 | tf_op jit(solution)/shard_map/all_to_all | solution.py:479
  99.3 10.4 %shard_map.97 = (f32[64,128,128]{2,1,0:T(8,128)}, f32[16,136,128]{2,1,0:T(8,128)S(1)}, f32[16,136,128]{2,1,0:T(8,128)S(1)}, f32[4,136,128]{2,1,0:T(8,128)S(1)}, f32[4,136,128]{2,1,0:T(8,128)S(1)}) custom-call(s32[4,16,6]{2,1,0:T(8,128)S(1)} %copy-done.2, f32[64,128,128]{2,1,0:T(8,128)} %get-tuple-element.19.state, f32[512,128]{1,0:T(8,128)S(1)} %bitcast.79, ...), custom_call_target="tpu_custom_call" | custom-call | tf_op jit(solution)/shard_map/pallas_call | solution.py:428
  109.7 2.6 %collective-permute-start.6 = (f32[16,136,128]{2,1,0:T(8,128)S(1)}, f32[16,136,128]{2,1,0:T(8,128)S(1)}, u32[]{:S(2)}, u32[]{:S(2)}) collective-permute-start(f32[16,136,128]{2,1,0:T(8,128)S(1)} %get-tuple-element.22), channel_id=1, source_target_pairs={{0,16},{16,32},{32,48},{48,64},{64,80},{80,96},{96,112},{1,17},{17... | collective-permute-start | bytes 3342344 | tf_op jit(solution)/shard_map/ppermute | solution.py:442
  112.3 1.9 %collective-permute-start.7 = (f32[16,136,128]{2,1,0:T(8,128)S(1)}, f32[16,136,128]{2,1,0:T(8,128)S(1)}, u32[]{:S(2)}, u32[]{:S(2)}) collective-permute-start(f32[16,136,128]{2,1,0:T(8,128)S(1)} %get-tuple-element.23), channel_id=1, source_target_pairs={{16,0},{32,16},{48,32},{64,48},{80,64},{96,80},{112,96},{17,1},{33... | collective-permute-start | bytes 3342344 | tf_op jit(solution)/shard_map/ppermute | solution.py:443
  114.2 0.4 collective-permute-start.8
  114.7 4.4 %collective-permute-start.9 = (f32[4,136,128]{2,1,0:T(8,128)S(1)}, f32[4,136,128]{2,1,0:T(8,128)S(1)}, u32[]{:S(2)}, u32[]{:S(2)}) collective-permute-start(f32[4,136,128]{2,1,0:T(8,128)S(1)} %get-tuple-element.25), channel_id=1, source_target_pairs={{1,0},{2,1},{3,2},{4,3},{5,4},{6,5},{7,6},{8,7},{9,8},{10,9},{11,1... | collective-permute-start | bytes 835592 | tf_op jit(solution)/shard_map/ppermute | solution.py:445
  119.1 5.6 %collective-permute-done.6.refs_1_ = f32[16,136,128]{2,1,0:T(8,128)S(1)} collective-permute-done((f32[16,136,128]{2,1,0:T(8,128)S(1)}, f32[16,136,128]{2,1,0:T(8,128)S(1)}, u32[]{:S(2)}, u32[]{:S(2)}) %collective-permute-start.6) | collective-permute-done | bytes 1114144 | tf_op jit(solution)/shard_map/ppermute | solution.py:442
  124.8 4.4 %collective-permute-done.7.refs_2_ = f32[16,136,128]{2,1,0:T(8,128)S(1)} collective-permute-done((f32[16,136,128]{2,1,0:T(8,128)S(1)}, f32[16,136,128]{2,1,0:T(8,128)S(1)}, u32[]{:S(2)}, u32[]{:S(2)}) %collective-permute-start.7) | collective-permute-done | bytes 1114144 | tf_op jit(solution)/shard_map/ppermute | solution.py:443
  129.2 1.1 collective-permute-start.11
  130.3 0.7 collective-permute-start.10
  131.0 2.3 %collective-permute-done.11.refs_6_ = f32[2,152,128]{2,1,0:T(8,128)S(1)} collective-permute-done((f32[2,152,128]{2,1,0:T(8,128)S(1)}, f32[2,152,128]{2,1,0:T(8,128)S(1)}, u32[]{:S(2)}, u32[]{:S(2)}) %collective-permute-start.11) | collective-permute-done | bytes 155680 | tf_op jit(solution)/shard_map/ppermute | solution.py:451
  133.3 4.6 %collective-permute-done.10.refs_5_ = f32[2,152,128]{2,1,0:T(8,128)S(1)} collective-permute-done((f32[2,152,128]{2,1,0:T(8,128)S(1)}, f32[2,152,128]{2,1,0:T(8,128)S(1)}, u32[]{:S(2)}, u32[]{:S(2)}) %collective-permute-start.10) | collective-permute-done | bytes 155680 | tf_op jit(solution)/shard_map/ppermute | solution.py:450
  138.0 0.6 copy-done.13
  138.6 27.1 %shard_map.98 = (f32[64,128,128]{2,1,0:T(8,128)}, f32[64,128]{1,0:T(8,128)}) custom-call(s32[4,16,6]{2,1,0:T(8,128)} %copy-done.1, f32[256]{0:T(256)} %reshape.114.surf, f32[64,128,128]{2,1,0:T(8,128)} %get-tuple-element.21.refs_0_, f32[16,136,128]{2,1,0:T(8,128)} %copy-done.5, f32[16,136,128]{2,1,0:T(8,128)} %copy-done.6, f32[4,136,128]{2,1,0:T(8,128)} %copy-done.8, ...), custom_call_target="tpu_custom_call" | custom-call | tf_op jit(solution)/shard_map/pallas_call | solution.py:336
  (59 shorter events, 0.2 us)
Async XLA Ops:
  1.4 4.9 %copy-start.1 = (s32[4,16,6]{2,1,0:T(8,128)}, s32[4,16,6]{2,1,0:T(8,128)S(1)}, u32[]{:S(2)}) copy-start(s32[4,16,6]{2,1,0:T(8,128)S(1)} %copy.31.codes) | copy-start | bytes 4612
  1.4 2.2 %copy-start = (f32[4,16,128,128]{3,2,1,0:T(8,128)S(1)}, f32[4,16,128,128]{3,2,1,0:T(8,128)}, u32[]{:S(2)}) copy-start(f32[4,16,128,128]{3,2,1,0:T(8,128)} %param.8) | copy-start | bytes 12582916
  3.6 0.7 copy-start.3
  4.3 14.8 %copy-start.16 = (f32[4,3]{1,0:T(4,128)S(1)}, f32[4,3]{1,0:T(4,128)}, u32[]{:S(2)}) copy-start(f32[4,3]{1,0:T(4,128)} %param.12) | copy-start | bytes 148
  4.3 22.0 %copy-start.4 = (s32[4,16]{1,0:T(4,128)S(1)}, s32[4,16]{1,0:T(4,128)}, u32[]{:S(2)}) copy-start(s32[4,16]{1,0:T(4,128)} %counts.1) | copy-start | bytes 772
  4.3 22.1 %copy-start.17 = (s32[4,16]{1,0:T(4,128)S(1)}, s32[4,16]{1,0:T(4,128)}, u32[]{:S(2)}) copy-start(s32[4,16]{1,0:T(4,128)} %param.11) | copy-start | bytes 772
  4.3 22.1 %copy-start.14 = (s32[256,1]{0,1:T(1,128)S(1)}, s32[256,1]{0,1:T(1,128)}, u32[]{:S(2)}) copy-start(s32[256,1]{0,1:T(1,128)} %param.14) | copy-start | bytes 3076
  6.3 26.1 %collective-permute-start = (f32[16,136,128]{2,1,0:T(8,128)S(1)}, f32[16,136,128]{2,1,0:T(8,128)}, u32[]{:S(2)}, u32[]{:S(2)}) collective-permute-start(f32[16,136,128]{2,1,0:T(8,128)S(1)} %get-tuple-element.15), channel_id=1, source_target_pairs={{0,16},{16,32},{32,48},{48,64},{64,80},{80,96},{96,112},{1,17},{17... | collective-permute-start | bytes 3342344 | tf_op jit(solution)/shard_map/ppermute | solution.py:442
  10.9 23.2 %collective-permute-start.1 = (f32[16,136,128]{2,1,0:T(8,128)S(1)}, f32[16,136,128]{2,1,0:T(8,128)}, u32[]{:S(2)}, u32[]{:S(2)}) collective-permute-start(f32[16,136,128]{2,1,0:T(8,128)S(1)} %get-tuple-element.16), channel_id=1, source_target_pairs={{16,0},{32,16},{48,32},{64,48},{80,64},{96,80},{112,96},{17,1},{33... | collective-permute-start | bytes 3342344 | tf_op jit(solution)/shard_map/ppermute | solution.py:443
  12.8 32.2 %collective-permute-start.2 = (f32[4,136,128]{2,1,0:T(8,128)S(1)}, f32[4,136,128]{2,1,0:T(8,128)S(1)}, u32[]{:S(2)}, u32[]{:S(2)}) collective-permute-start(f32[4,136,128]{2,1,0:T(8,128)S(1)} %get-tuple-element.17), channel_id=1, source_target_pairs={{0,1},{1,2},{2,3},{3,4},{4,5},{5,6},{6,7},{7,8},{8,9},{9,10},{10,1... | collective-permute-start | bytes 835592 | tf_op jit(solution)/shard_map/ppermute | solution.py:444
  14.2 30.9 %collective-permute-start.3 = (f32[4,136,128]{2,1,0:T(8,128)S(1)}, f32[4,136,128]{2,1,0:T(8,128)}, u32[]{:S(2)}, u32[]{:S(2)}) collective-permute-start(f32[4,136,128]{2,1,0:T(8,128)S(1)} %get-tuple-element.18), channel_id=1, source_target_pairs={{1,0},{2,1},{3,2},{4,3},{5,4},{6,5},{7,6},{8,7},{9,8},{10,9},{11,1... | collective-permute-start | bytes 835592 | tf_op jit(solution)/shard_map/ppermute | solution.py:445
  19.9 22.5 %all-to-all-start = ((f32[128,1,12]{2,1,0:T(1,128)}), f32[128,1,12]{2,1,0:T(1,128)S(1)}, u32[]{:S(2)}, u32[]{:S(2)}) async-start(f32[128,1,12]{2,1,0:T(1,128)} %broadcast_in_dim.22), calls=%async_computation | async-start | bytes 131072 | tf_op jit(solution)/shard_map/all_to_all | solution.py:465
  32.4 9.1 %copy-start.18 = (s32[256]{0:T(256)S(1)}, s32[256]{0:T(256)}, u32[]{:S(2)}) copy-start(s32[256]{0:T(256)} %param.13) | copy-start | bytes 3076
  35.8 9.3 %collective-permute-start.5 = (f32[2,152,128]{2,1,0:T(8,128)S(1)}, f32[2,152,128]{2,1,0:T(8,128)S(1)}, u32[]{:S(2)}, u32[]{:S(2)}) collective-permute-start(f32[2,152,128]{2,1,0:T(8,128)S(1)} %pad_maximum_fusion.1), channel_id=1, source_target_pairs={{1,0},{2,1},{3,2},{4,3},{5,4},{6,5},{7,6},{8,7},{9,8},{10,9},{11,1... | collective-permute-start | bytes 466952 | tf_op jit(solution)/shard_map/ppermute | solution.py:451
  41.4 8.3 %collective-permute-start.4 = (f32[2,152,128]{2,1,0:T(8,128)S(1)}, f32[2,152,128]{2,1,0:T(8,128)S(1)}, u32[]{:S(2)}, u32[]{:S(2)}) collective-permute-start(f32[2,152,128]{2,1,0:T(8,128)S(1)} %pad_maximum_fusion), channel_id=1, source_target_pairs={{0,1},{1,2},{2,3},{3,4},{4,5},{5,6},{6,7},{7,8},{8,9},{9,10},{10,1... | collective-permute-start | bytes 466952 | tf_op jit(solution)/shard_map/ppermute | solution.py:450
  45.0 42.9 %copy-start.15 = (s32[512]{0:T(512)S(1)}, s32[512]{0:T(512)}, u32[]{:S(2)}) copy-start(s32[512]{0:T(512)} %param.15) | copy-start | bytes 6148
  45.0 54.3 %copy-start.2 = (s32[4,16,6]{2,1,0:T(8,128)S(1)}, s32[4,16,6]{2,1,0:T(8,128)}, u32[]{:S(2)}) copy-start(s32[4,16,6]{2,1,0:T(8,128)} %copy-done.1) | copy-start | bytes 4612
  45.0 4.7 %copy-start.7 = (f32[4,136,128]{2,1,0:T(8,128)}, f32[4,136,128]{2,1,0:T(8,128)S(1)}, u32[]{:S(2)}) copy-start(f32[4,136,128]{2,1,0:T(8,128)S(1)} %collective-permute-done.2.refs_3_) | copy-start | bytes 835588
  45.0 4.7 %copy-start.10 = (f32[2,152,128]{2,1,0:T(8,128)}, f32[2,152,128]{2,1,0:T(8,128)S(1)}, u32[]{:S(2)}) copy-start(f32[2,152,128]{2,1,0:T(8,128)S(1)} %collective-permute-done.5.refs_6_) | copy-start | bytes 466948
  49.8 0.7 copy-start.11
  82.2 17.1 %all-to-all-start.1 = ((f32[128,4,128]{2,1,0:T(4,128)}), f32[128,4,128]{2,1,0:T(4,128)S(1)}, u32[]{:S(2)}, u32[]{:S(2)}) async-start(f32[128,4,128]{2,1,0:T(4,128)} %bitcast.80), calls=%async_computation.1 | async-start | bytes 524288 | tf_op jit(solution)/shard_map/all_to_all | solution.py:479
  109.7 15.0 %collective-permute-start.6 = (f32[16,136,128]{2,1,0:T(8,128)S(1)}, f32[16,136,128]{2,1,0:T(8,128)S(1)}, u32[]{:S(2)}, u32[]{:S(2)}) collective-permute-start(f32[16,136,128]{2,1,0:T(8,128)S(1)} %get-tuple-element.22), channel_id=1, source_target_pairs={{0,16},{16,32},{32,48},{48,64},{64,80},{80,96},{96,112},{1,17},{17... | collective-permute-start | bytes 3342344 | tf_op jit(solution)/shard_map/ppermute | solution.py:442
  112.3 16.8 %collective-permute-start.7 = (f32[16,136,128]{2,1,0:T(8,128)S(1)}, f32[16,136,128]{2,1,0:T(8,128)S(1)}, u32[]{:S(2)}, u32[]{:S(2)}) collective-permute-start(f32[16,136,128]{2,1,0:T(8,128)S(1)} %get-tuple-element.23), channel_id=1, source_target_pairs={{16,0},{32,16},{48,32},{64,48},{80,64},{96,80},{112,96},{17,1},{33... | collective-permute-start | bytes 3342344 | tf_op jit(solution)/shard_map/ppermute | solution.py:443
  114.2 16.8 %collective-permute-start.8 = (f32[4,136,128]{2,1,0:T(8,128)S(1)}, f32[4,136,128]{2,1,0:T(8,128)S(1)}, u32[]{:S(2)}, u32[]{:S(2)}) collective-permute-start(f32[4,136,128]{2,1,0:T(8,128)S(1)} %get-tuple-element.24), channel_id=1, source_target_pairs={{0,1},{1,2},{2,3},{3,4},{4,5},{5,6},{6,7},{7,8},{8,9},{9,10},{10,1... | collective-permute-start | bytes 835592 | tf_op jit(solution)/shard_map/ppermute | solution.py:444
  114.7 16.4 %collective-permute-start.9 = (f32[4,136,128]{2,1,0:T(8,128)S(1)}, f32[4,136,128]{2,1,0:T(8,128)S(1)}, u32[]{:S(2)}, u32[]{:S(2)}) collective-permute-start(f32[4,136,128]{2,1,0:T(8,128)S(1)} %get-tuple-element.25), channel_id=1, source_target_pairs={{1,0},{2,1},{3,2},{4,3},{5,4},{6,5},{7,6},{8,7},{9,8},{10,9},{11,1... | collective-permute-start | bytes 835592 | tf_op jit(solution)/shard_map/ppermute | solution.py:445
  124.7 13.2 %copy-start.5 = (f32[16,136,128]{2,1,0:T(8,128)}, f32[16,136,128]{2,1,0:T(8,128)S(1)}, u32[]{:S(2)}) copy-start(f32[16,136,128]{2,1,0:T(8,128)S(1)} %collective-permute-done.6.refs_1_) | copy-start | bytes 3342340
  129.1 8.8 %copy-start.6 = (f32[16,136,128]{2,1,0:T(8,128)}, f32[16,136,128]{2,1,0:T(8,128)S(1)}, u32[]{:S(2)}) copy-start(f32[16,136,128]{2,1,0:T(8,128)S(1)} %collective-permute-done.7.refs_2_) | copy-start | bytes 3342340
  129.2 4.2 %collective-permute-start.11 = (f32[2,152,128]{2,1,0:T(8,128)S(1)}, f32[2,152,128]{2,1,0:T(8,128)S(1)}, u32[]{:S(2)}, u32[]{:S(2)}) collective-permute-start(f32[2,152,128]{2,1,0:T(8,128)S(1)} %pad_maximum_fusion.3), channel_id=1, source_target_pairs={{1,0},{2,1},{3,2},{4,3},{5,4},{6,5},{7,6},{8,7},{9,8},{10,9},{11,1... | collective-permute-start | bytes 466952 | tf_op jit(solution)/shard_map/ppermute | solution.py:451
  130.3 7.7 %collective-permute-start.10 = (f32[2,152,128]{2,1,0:T(8,128)S(1)}, f32[2,152,128]{2,1,0:T(8,128)S(1)}, u32[]{:S(2)}, u32[]{:S(2)}) collective-permute-start(f32[2,152,128]{2,1,0:T(8,128)S(1)} %pad_maximum_fusion.2), channel_id=1, source_target_pairs={{0,1},{1,2},{2,3},{3,4},{4,5},{5,6},{6,7},{7,8},{8,9},{9,10},{10,1... | collective-permute-start | bytes 466952 | tf_op jit(solution)/shard_map/ppermute | solution.py:450
  131.0 7.0 %copy-start.8 = (f32[4,136,128]{2,1,0:T(8,128)}, f32[4,136,128]{2,1,0:T(8,128)S(1)}, u32[]{:S(2)}) copy-start(f32[4,136,128]{2,1,0:T(8,128)S(1)} %collective-permute-done.8.refs_3_) | copy-start | bytes 835588
  131.0 7.0 %copy-start.9 = (f32[4,136,128]{2,1,0:T(8,128)}, f32[4,136,128]{2,1,0:T(8,128)S(1)}, u32[]{:S(2)}) copy-start(f32[4,136,128]{2,1,0:T(8,128)S(1)} %collective-permute-done.9.refs_4_) | copy-start | bytes 835588
  133.3 4.7 %copy-start.12 = (f32[2,152,128]{2,1,0:T(8,128)}, f32[2,152,128]{2,1,0:T(8,128)S(1)}, u32[]{:S(2)}) copy-start(f32[2,152,128]{2,1,0:T(8,128)S(1)} %collective-permute-done.11.refs_6_) | copy-start | bytes 466948
  138.0 0.7 copy-start.13

commit v3 on v2

v3 whole, which is shorter than its diff:
```python
import functools

import jax
import jax.numpy as jnp
from jax import lax
from jax.experimental import pallas as pl
from jax.experimental.pallas import tpu as pltpu
from jax.sharding import PartitionSpec as P

AXES = ("ax", "az")
F32, BF16, I32 = jnp.float32, jnp.bfloat16, jnp.int32

wall_gain = 4.0
time_step = 0.05
MIB = 1 << 20


def rows_of(x, n):
    return jnp.broadcast_to(x, (n,) + x.shape[1:])


def sub_iota(shape):
    return lax.broadcasted_iota(I32, shape, 0)


def halves(x):
    hi = x.astype(BF16)
    return hi, (x - hi.astype(F32)).astype(BF16)


def thirds(x):
    hi = x.astype(BF16).astype(F32)
    rest = x - hi
    mid = rest.astype(BF16).astype(F32)
    return hi, mid, rest - mid


def loop(n, body):
    def step(i, carry):
        body(i)
        return carry

    lax.fori_loop(0, n, step, 0)


ROWS_K = 32
EDGE, CORNER = 136, 152


def live_rows(g, count):
    dead = (sub_iota((8, 128)) == 6) & (lax.broadcasted_iota(I32, (8, 128), 1) >= count)
    return jnp.where(dead, 0.0, g)


def with_codes(behind, codes, r, c):
    lane = lax.broadcasted_iota(I32, (8, 128), 1)
    listed = jnp.zeros((8, 128), F32)
    for j in range(6):
        listed = jnp.where(lane == j, codes[r, c, j].astype(F32), listed)
    return jnp.where(sub_iota((8, 128)) == 7, listed, behind)


def pieces(source, target, semaphore, per):
    def piece(i):
        part = pl.ds(i * per, per)
        return pltpu.make_async_copy(source.at[part], target.at[part], semaphore.at[i])

    return piece


def smem_spec():
    return pl.BlockSpec(memory_space=pltpu.SMEM)


def vmem_spec():
    return pl.BlockSpec(memory_space=pltpu.VMEM)


def any_spec():
    return pl.BlockSpec(memory_space=pl.ANY)


FULL = pltpu.CompilerParams(vmem_limit_bytes=60 * MIB)


def strip_shapes(rows, cols):
    entries = ((2, CORNER), (2, CORNER), (cols, EDGE), (cols, EDGE), (rows, EDGE), (rows, EDGE))
    return tuple(jax.ShapeDtypeStruct((n, height, 128), F32) for n, height in entries)


def put_strips(rows, cols, codes, geo, strips):
    ends_up, ends_down, a_up, a_down, z_up, z_down = strips
    sides = ((ends_up, a_up, rows - 1, rows - 2), (ends_down, a_down, 0, 1))

    def along(i):
        for k in range(4):
            n = i * 4 + k
            for _, strip, first, second in sides:
                strip[n, 0:8, :] = geo(first, n)
                strip[n, 128:136, :] = with_codes(geo(second, n), codes, first, n)

    loop(cols // 4, along)
    for strip, first, second in ((z_up, cols - 1, cols - 2), (z_down, 0, 1)):
        for r in range(rows):
            strip[r, 0:8, :] = geo(r, first)
            strip[r, 128:136, :] = with_codes(geo(r, second), codes, r, first)
    for strip, _, first, second in sides:
        for n, (near, far) in enumerate(((0, 1), (cols - 1, cols - 2))):
            strip[n, 0:8, :] = geo(first, near)
            strip[n, 128:136, :] = with_codes(geo(second, near), codes, first, near)
            strip[n, 136:144, :] = geo(first, far)
            strip[n, 144:152, :] = geo(second, far)


def fill_strips(rows, cols, state, strips, semaphore):
    ends_up, ends_down, a_up, a_down, z_up, z_down = strips
    parts = []
    for ends, strip, r in ((ends_up, a_up, rows - 1), (ends_down, a_down, 0)):
        parts.append((state.at[pl.ds(r * cols, cols), 8:128, :], strip.at[:, 8:128, :]))
        for n, c in enumerate((0, cols - 1)):
            parts.append((state.at[r * cols + c, 8:128, :], ends.at[n, 8:128, :]))
    for strip, c in ((z_up, cols - 1), (z_down, 0)):
        for r in range(rows):
            parts.append((state.at[r * cols + c, 8:128, :], strip.at[r, 8:128, :]))
    return [pltpu.make_async_copy(a, b, semaphore.at[k]) for k, (a, b) in enumerate(parts)]


def mask_kernel(rows, cols, counts, codes, state, *refs):
    strips, (rows8, came, semaphore) = refs[:6], refs[6:]
    first = pltpu.make_async_copy(state.at[:, 0:8, :], rows8, came)
    first.start()
    copies = fill_strips(rows, cols, state, strips, semaphore)
    for copy in copies:
        copy.start()
    first.wait()
    put_strips(rows, cols, codes, lambda r, c: live_rows(rows8[r * cols + c], counts[r, c]), strips)
    for copy in copies:
        copy.wait()


def mask_strips(rows, cols, counts, codes, state):
    return pl.pallas_call(
        functools.partial(mask_kernel, rows, cols),
        out_shape=strip_shapes(rows, cols),
        in_specs=[smem_spec(), smem_spec(), any_spec()],
        out_specs=(vmem_spec(),) * 6,
        scratch_shapes=[pltpu.VMEM((rows * cols, 8, 128), F32), pltpu.SemaphoreType.DMA(()), pltpu.SemaphoreType.DMA((6 + 2 * rows,))],
        compiler_params=FULL,
    )(counts, codes, state)


def linked(center, code, width):
    up = (code * 11) >> 5
    return center + up * (width - 3) + code - (width + 1)


def step_kernel(rows, cols, masked, leaving, *refs):
    if masked:
        counts, refs = refs[0], refs[1:]
    codes, surf, cells_in, a_low, a_high, z_low, z_high = refs[:7]
    if leaving:
        slots, buffer_row, out_ref, sent, gathered = refs[7:12]
        refs = refs[12:]
    else:
        out_ref, dens = refs[7:9]
        refs = refs[9:]
    geo, cells, out, side_t, side_s, feat, squares, row_t, row_s = refs[:9]
    mass, root, rho, ratio, inverse, ring_codes, geo_came, cells_came, out_left, codes_came = refs[9:]
    width = cols + 4
    own = rows * cols
    z_rows = rows * EDGE
    sub8 = sub_iota((8, 128))
    row_mid, col_mid = (rows + 3) / 2.0, (cols + 3) / 2.0

    geo_copy = pltpu.make_async_copy(cells_in.at[:, 0:8, :], geo, geo_came)
    geo_copy.start()
    code_copies = []

    def bring_codes(source, first, n):
        code_copies.append(pltpu.make_async_copy(source, ring_codes.at[pl.ds(first, n), :], codes_came.at[len(code_copies)]))

    bring_codes(a_low.at[:, EDGE - 1, :], 0, cols)
    bring_codes(a_high.at[:, EDGE - 1, :], cols, cols)
    for ref, first in ((z_low, 2 * cols), (z_high, 2 * cols + rows + 2)):
        for r in range(rows):
            bring_codes(ref.at[pl.ds(r * EDGE + EDGE - 1, 1), :], first + r, 1)
        for n in range(2):
            bring_codes(ref.at[pl.ds(z_rows + n * CORNER + EDGE - 1, 1), :], first + rows + n, 1)
    cells_piece = pieces(cells_in, cells, cells_came, 8)
    out_piece = pieces(out, out_ref, out_left, 8)
    for copy in code_copies:
        copy.start()
    for i in range(own // 8):
        cells_piece(i).start()

    def geometry(flat, row, stride, n, index, apart, r, c, center, limit=None):
        def field(k):
            return flat[pl.ds(row + k, n, stride=stride), :]

        x = [field(0) + (r - row_mid), field(1) + (c - col_mid), field(2)]
        norm = x[0] * x[0] + x[1] * x[1] + x[2] * x[2]
        m = field(6)
        if limit is not None:
            m = jnp.where(lax.broadcasted_iota(I32, (n, 128), 1) < limit, m, 0.0)
        cube = jnp.exp2(jnp.log2(jnp.maximum(m, 1e-30)) * (1.0 / 3.0))
        cube = cube - (cube - m / (cube * cube)) * (1.0 / 3.0)
        cube = jnp.where(m > 0.0, cube, 0.0)

        def put(target, k, value):
            target[pl.ds(index * ROWS_K + k, n, stride=apart * ROWS_K), :] = value

        for k, value in enumerate([x[0] * cube, x[1] * cube, x[2] * cube, -norm * cube, cube]):
            hi, mid, low = thirds(value)
            for block, piece in enumerate((hi, mid, low, hi, mid, hi)):
                put(row_t, 5 * block + k, piece)
        put(row_t, 30, jnp.zeros_like(m))
        put(row_t, 31, jnp.zeros_like(m))
        for k in range(n):
            mass[pl.ds(index + k * apart, 1), :] = m[k : k + 1]
            root[pl.ds(index + k * apart, 1), :] = cube[k : k + 1]
        if center:
            for k, value in enumerate([x[0] + x[0], x[1] + x[1], x[2] + x[2], jnp.ones_like(m), 1.0 - norm]):
                hi, mid, low = thirds(value)
                for block, piece in enumerate((hi, hi, hi, mid, mid, low)):
                    put(row_s, 5 * block + k, piece)
            put(row_s, 30, jnp.zeros_like(m))
            put(row_s, 31, jnp.zeros_like(m))

    def sub(n):
        return sub_iota((n, 128)).astype(F32)

    per = 8
    geo_copy.wait()
    geo_flat = geo.reshape(own * 8, 128)

    def local_geo(i):
        first = i * per
        r, c = first // cols + 2, first % cols + 2
        limit = None
        if masked:
            limit = jnp.zeros((per, 128), I32)
            for k in range(per):
                limit = jnp.where(sub_iota((per, 128)) == k, counts[first // cols, first % cols + k], limit)
        geometry(geo_flat, first * 8, 8, per, r * width + c, 1, r.astype(F32), c.astype(F32) + sub(per), True, limit)

    loop(own // per, local_geo)
    for ref, first, second in ((a_low, 1, 0), (a_high, rows + 2, rows + 3)):
        flat = ref.reshape(cols * EDGE, 128)
        for k in range(0, cols, per):
            c = k + 2.0 + sub(per)
            geometry(flat, k * EDGE, EDGE, per, first * width + k + 2, 1, float(first), c, True)
            geometry(flat, k * EDGE + 128, EDGE, per, second * width + k + 2, 1, float(second), c, False)
    for ref, near, far in ((z_low, 1, 0), (z_high, cols + 2, cols + 3)):
        r = 2.0 + sub(rows)
        geometry(ref, 0, EDGE, rows, 2 * width + near, width, r, float(near), True)
        geometry(ref, 128, EDGE, rows, 2 * width + far, width, r, float(far), False)
        apart = (rows + 1) * width
        r = 1.0 + (rows + 1.0) * sub(2)
        geometry(ref, z_rows, CORNER, 2, width + near, apart, r, float(near), True)
        geometry(ref, z_rows + 136, CORNER, 2, width + far, apart, r, float(far), False)
        apart = (rows + 3) * width
        r = (rows + 3.0) * sub(2)
        geometry(ref, z_rows + 128, CORNER, 2, near, apart, r, float(near), False)
        geometry(ref, z_rows + 144, CORNER, 2, far, apart, r, float(far), False)

    quarter = lax.broadcasted_iota(I32, (128, 128), 1) // ROWS_K
    only = [jnp.where(quarter == k, 1.0, 0.0).astype(BF16) for k in range(4)]

    def block32(ref, index):
        return ref[pl.ds(pl.multiple_of(index * ROWS_K, ROWS_K), ROWS_K), :]

    def turn(indices):
        t = jnp.transpose(jnp.concatenate([block32(row_t, index) for index in indices], axis=0)).astype(BF16)
        for k, index in enumerate(indices):
            side_t[index] = t * only[k]
            side_s[index] = block32(row_s, index).astype(BF16)

    def turn_own(i):
        for k in range(cols // 4):
            index = (i + 2) * width + 2 + 4 * k
            turn([index, index + 1, index + 2, index + 3])

    loop(rows, turn_own)

    def turn_ring(i):
        for r in (i, i + rows + 2):
            for k in range(width // 4):
                index = r * width + 4 * k
                turn([index, index + 1, index + 2, index + 3])
        for r in (2 * i + 2, 2 * i + 3):
            turn([r * width, r * width + 1, r * width + cols + 2, r * width + cols + 3])

    loop(2, turn_ring)

    def density(center, partners, n):
        rhs = jnp.concatenate([side_s[center]] * 4, axis=0)
        total = jnp.zeros((8, 128), F32)
        for j, partner in enumerate(partners):
            y = jnp.maximum(jnp.dot(side_t[partner], rhs, preferred_element_type=F32), 0.0)
            square = y * y
            total = total + jnp.sum((square * y).reshape(16, 8, 128), axis=0)
            if n is not None:
                squares[n, j * 128 : (j + 1) * 128, :] = square.astype(BF16)
        rho[pl.ds(center, 1), :] = jnp.sum(total, axis=0, keepdims=True)

    rho[...] = jnp.ones_like(rho)

    def own_density(i):
        for k in range(8):
            n = i * 8 + k
            r, c = n // cols, n % cols
            center = (r + 2) * width + c + 2
            density(center, [linked(center, codes[r, c, j], width) for j in range(6)], n)

    loop(own // 8, own_density)
    for copy in code_copies:
        copy.wait()

    def ring_cell(center, n):
        density(center, [linked(center, ring_codes[n, j].astype(I32), width) for j in range(6)], None)

    def ring_rows(i):
        for k in range(4):
            c = i * 4 + k
            ring_cell(width + c + 2, c)
            ring_cell((rows + 2) * width + c + 2, cols + c)

    loop(cols // 4, ring_rows)
    for k, r in enumerate([r + 2 for r in range(rows)] + [1, rows + 2]):
        ring_cell(r * width + 1, 2 * cols + k)
        ring_cell(r * width + cols + 2, 2 * cols + rows + 2 + k)

    living = mass[...] > 0.0
    guarded = jnp.where(living, rho[...], 1.0)
    ratio[...] = jnp.where(living, (guarded - 1.0) / (guarded * guarded), 0.0)
    inverse[...] = jnp.where(living, 1.0 / guarded, 0.0)

    def row8(ref, index):
        return rows_of(ref[pl.ds(index, 1), :], 8)

    def shifted(g, r, c):
        off_r = r.astype(F32) - row_mid
        off_c = c.astype(F32) - col_mid
        return jnp.where(sub8 == 0, g + off_r, jnp.where(sub8 == 1, g + off_c, g))

    def positions(g, r, c):
        x = shifted(g, r, c)
        return jnp.where((sub8 == 0) | (sub8 == 4), 1.0, jnp.where(sub8 < 4, pltpu.roll(x, 1, 0), pltpu.roll(x, 5, 0)))

    def features(load, r, c):
        index = r * width + c
        cube = row8(root, index)
        scale = cube * row8(inverse, index)

        g = load(0)
        nu = rows_of(g[7:8], 8)
        first = jnp.where(sub8 < 3, pltpu.roll(g, 5, 0) * nu, jnp.where(sub8 == 6, 1.0, g)) * scale
        press = positions(g, r, c) * jnp.where(sub8 < 4, cube, cube * row8(ratio, index))
        hi, lo = halves(press)
        feat[index, 128:144, :] = jnp.concatenate([hi.astype(F32), lo.astype(F32)], axis=0).astype(BF16)
        feat[index, 0:16, :] = jnp.concatenate([first, load(1) * scale], axis=0).astype(BF16)
        for k in range(1, 8):
            feat[index, 16 * k : 16 * k + 16, :] = jnp.concatenate([load(2 * k) * scale, load(2 * k + 1) * scale], axis=0).astype(BF16)

    def in_cell(ref, n):
        return lambda k: ref[n, 8 * k : 8 * k + 8, :]

    def in_rows(ref, row):
        return lambda k: ref[row + 8 * k : row + 8 * k + 8, :]

    def local_feat(i):
        cells_piece(i).wait()
        for k in range(8):
            n = i * 8 + k
            features(in_cell(cells, n), n // cols + 2, n % cols + 2)

    loop(own // 8, local_feat)

    def a_feat(i):
        for k in range(4):
            n = i * 4 + k
            features(in_cell(a_low, n), jnp.int32(1), n + 2)
            features(in_cell(a_high, n), jnp.int32(rows + 2), n + 2)

    loop(cols // 4, a_feat)
    for ref, c in ((z_low, 1), (z_high, cols + 2)):
        for r in range(rows):
            features(in_rows(ref, r * EDGE), jnp.int32(r + 2), jnp.int32(c))
        for n, r in enumerate((1, rows + 2)):
            features(in_rows(ref, z_rows + n * CORNER), jnp.int32(r), jnp.int32(c))

    def force(n):
        r, c = n // cols, n % cols
        index = (r + 2) * width + c + 2
        lhs = jnp.concatenate([feat[linked(index, codes[r, c, j], width)] for j in range(6)], axis=1)
        sums = jnp.dot(lhs, squares[n], preferred_element_type=F32)
        if masked:
            held = lax.broadcasted_iota(I32, (8, 128), 1) < counts[r, c]

        def load(k):
            value = cells[n, 8 * k : 8 * k + 8, :]
            return jnp.where(held, value, 0.0) if masked else value

        g = load(0)
        m, nu = rows_of(g[6:7], 8), rows_of(g[7:8], 8)
        alive = jnp.where(m > 0.0, time_step, 0.0)
        first = sums[0:8]
        press = sums[128:136] + sums[136:144]
        press = press - positions(g, r + 2, c + 2) * jnp.where(sub8 < 4, rows_of(press[0:1], 8), rows_of(press[4:5], 8))
        press = press * jnp.where(sub8 < 4, row8(ratio, index), 1.0)
        press = press + pltpu.roll(press, 4, 0)
        weight, friction = rows_of(first[6:7], 8), rows_of(first[7:8], 8)
        surface = jnp.where(sub8 == 3, surf[n * 4], jnp.where(sub8 == 4, surf[n * 4 + 1], surf[n * 4 + 2]))
        wall = wall_gain * jnp.maximum(1.0 - 3.0 * rows_of(g[2:3], 8), 0.0)
        accel = nu * (first - g * weight) + pltpu.roll(first, 3, 0) - g * friction + wall * (surface - g)
        accel = accel - 6.0 * pltpu.roll(press, 2, 0)
        velocity = g + accel * alive
        position = g + time_step * pltpu.roll(velocity, 5, 0)
        out[n, 0:8, :] = jnp.where(sub8 < 3, position, jnp.where(sub8 < 6, velocity, g))
        gain = 2.0 * alive
        stay = 1.0 - gain * weight
        for k in range(1, 16):
            out[n, 8 * k : 8 * k + 8, :] = load(k) * stay + gain * sums[8 * k : 8 * k + 8]
        if not leaving:
            dens[pl.ds(n, 1), :] = jnp.where(m > 0.0, row8(rho, index), 0.0)[0:1]

    def forces(i):
        for k in range(8):
            force(i * 8 + k)
        if not leaving:
            out_piece(i).start()

    loop(own // 8, forces)
    if leaving:
        take_out(out, slots, buffer_row, sent, gathered, out_piece)
    for i in range(own // 8):
        out_piece(i).wait()


def take_out(state, slots, buffer_row, sent, gathered, out_piece):
    leaving, places = slots.shape[0], sent.shape[0]
    offset = jnp.broadcast_to(slots[...], (leaving, 128)) - lax.broadcasted_iota(I32, (leaving, 128), 1)
    gathered[...] = jnp.zeros_like(gathered)
    per = 8

    def body(i):
        hits, parts = [], []
        for k in range(per):
            c = i * per + k
            hit = jnp.where(offset == c * 128, 1.0, 0.0)
            gone = jnp.sum(hit, axis=0, keepdims=True)
            whole = state[c]
            hi, lo = halves(whole)
            hits.append(hit.astype(BF16))
            parts.append(jnp.concatenate([hi, lo], axis=0))
            state[c] = whole * (1.0 - gone)
        gathered[...] += lax.dot_general(jnp.concatenate(hits, axis=1), jnp.concatenate(parts, axis=1), (((1,), (1,)), ((), ())), preferred_element_type=F32)
        out_piece(i).start()

    loop(state.shape[0] // per, body)
    place = jnp.where(jnp.broadcast_to(buffer_row[...], (places, leaving)) == sub_iota((places, leaving)), 1.0, 0.0).astype(BF16)
    right = jnp.concatenate([gathered[...].astype(BF16), jnp.ones((leaving, 128), BF16)], axis=1)
    sums = jnp.dot(place, right, preferred_element_type=F32)
    lane = lax.broadcasted_iota(I32, (places, 128), 1)
    sent[...] = jnp.where((lane == 6) & (sums[:, 256:384] < 0.5), -1.0, sums[:, 0:128] + sums[:, 128:256])


def smem_spec():
    return pl.BlockSpec(memory_space=pltpu.SMEM)


def vmem_spec():
    return pl.BlockSpec(memory_space=pltpu.VMEM)


def step_call(rows, cols, counts, codes, surface, cells, halo, leave=None):
    own = rows * cols
    patch = (rows + 4) * (cols + 4)
    ring = 2 * cols + 2 * (rows + 2)
    new = jax.ShapeDtypeStruct((own, 128, 128), F32)
    extra, first = [], []
    if leave:
        slots, buffer_row, places = leave
        outs = (new, jax.ShapeDtypeStruct((places, 128), F32))
        extra, first = [slots, buffer_row], [pltpu.VMEM((slots.shape[0], 256), F32)]
    else:
        outs = (new, jax.ShapeDtypeStruct((own, 128), F32))
    scalars = [] if counts is None else [counts]
    return pl.pallas_call(
        functools.partial(step_kernel, rows, cols, counts is not None, bool(leave)),
        out_shape=outs,
        in_specs=[smem_spec()] * (len(scalars) + 2) + [any_spec()] + [vmem_spec()] * (4 + len(extra)),
        out_specs=(any_spec(), vmem_spec()),
        scratch_shapes=first
        + [
            pltpu.VMEM((own, 8, 128), F32),
            pltpu.VMEM((own, 128, 128), F32),
            pltpu.VMEM((own, 128, 128), F32),
            pltpu.VMEM((patch, 128, 128), BF16),
            pltpu.VMEM((patch, 32, 128), BF16),
            pltpu.VMEM((patch, 144, 128), BF16),
            pltpu.VMEM((own, 768, 128), BF16),
            pltpu.VMEM((patch * ROWS_K, 128), F32),
            pltpu.VMEM((patch * ROWS_K, 128), F32),
        ]
        + [pltpu.VMEM((patch, 128), F32)] * 5
        + [
            pltpu.SMEM((ring, 128), F32),
            pltpu.SemaphoreType.DMA(()),
            pltpu.SemaphoreType.DMA((own // 8,)),
            pltpu.SemaphoreType.DMA((own // 8,)),
            pltpu.SemaphoreType.DMA((2 + 2 * (rows + 2),)),
        ],
        compiler_params=pltpu.CompilerParams(vmem_limit_bytes=52 * MIB),
    )(*scalars, codes, surface, cells, *halo, *extra)


def insert_kernel(rows, cols, codes, state_in, incoming, slots, out_ref, *refs):
    strips, (state, out, came, left_for, semaphore) = refs[:6], refs[6:]
    arrive = pieces(state_in, state, came, 8)
    leave = pieces(out, out_ref, left_for, 8)
    for i in range(rows * cols // 8):
        arrive(i).start()
    places = slots.shape[0]
    data = incoming[...]
    absent = jnp.broadcast_to(data[:, 6:7], (places, 128)) < 0.0
    offset = jnp.broadcast_to(slots[...], (places, 128)) - lax.broadcasted_iota(I32, (places, 128), 1)
    offset = jnp.where(absent, -1, offset)
    hi, lo = halves(jnp.transpose(data))
    left = jnp.concatenate([hi, lo, jnp.ones((16, places), BF16)], axis=0)
    per = 8

    def body(i):
        arrive(i).wait()
        for pair in range(per // 2):
            first = i * per + pair * 2
            hits = [jnp.where(offset == (first + k) * 128, 1.0, 0.0).astype(BF16) for k in range(2)]
            sums = jnp.dot(left, jnp.concatenate(hits, axis=1), preferred_element_type=F32)
            for k in range(2):
                part = sums[:, 128 * k : 128 * (k + 1)]
                out[first + k] = state[first + k] * (1.0 - part[256:257]) + (part[0:128] + part[128:256])
        leave(i).start()

    loop(rows * cols // per, body)
    copies = fill_strips(rows, cols, out, strips, semaphore)
    for copy in copies:
        copy.start()
    put_strips(rows, cols, codes, lambda r, c: out[r * cols + c, 0:8, :], strips)
    for copy in copies:
        copy.wait()
    for i in range(rows * cols // per):
        leave(i).wait()


def insert(rows, cols, codes, state, incoming, slots):
    own = rows * cols
    return pl.pallas_call(
        functools.partial(insert_kernel, rows, cols),
        out_shape=(jax.ShapeDtypeStruct(state.shape, F32),) + strip_shapes(rows, cols),
        in_specs=[smem_spec(), any_spec(), vmem_spec(), vmem_spec()],
        out_specs=(any_spec(),) + (vmem_spec(),) * 6,
        scratch_shapes=[pltpu.VMEM((own, 128, 128), F32)] * 2 + [pltpu.SemaphoreType.DMA((own // 8,))] * 2 + [pltpu.SemaphoreType.DMA((6 + 2 * rows,))],
        compiler_params=pltpu.CompilerParams(vmem_limit_bytes=52 * MIB),
    )(codes, state, incoming, slots)


def swap(up, down, axis):
    n = lax.axis_size(axis)
    pairs = [(i, (i + 1) % n) for i in range(n if axis == "az" else n - 1)]
    return lax.ppermute(up, axis, pairs), lax.ppermute(down, axis, [(j, i) for i, j in pairs])


def exchange(strips):
    ends_up, ends_down, a_up, a_down, z_up, z_down = strips
    low, high = swap(ends_up, ends_down, "ax")
    a_low, a_high = swap(a_up, a_down, "ax")

    def beside(strip, n):
        return jnp.concatenate([strip.reshape(-1, 128), low[n], high[n]], axis=0)

    sides = beside(z_up, 1), beside(z_down, 0)
    return (a_low, a_high) + swap(*sides, "az"), sides


def local(particles, counts, pair_codes, contact, twist_state, leaving_slot, leaving_dest, arrival_slot):
    rows, cols, fields, block = particles.shape
    ranks = lax.axis_size("ax") * lax.axis_size("az")
    own = rows * cols
    state = particles.reshape(own, fields, block)
    halo, sides = exchange(mask_strips(rows, cols, counts, pair_codes, state))

    segments = twist_state.shape[0]
    twist_state, _ = lax.optimization_barrier((twist_state, sides))
    told = jnp.broadcast_to(twist_state.reshape(1, segments * 3), (ranks, segments * 3))
    twist = lax.all_to_all(told, AXES, 0, 0, tiled=True).reshape(ranks * segments, 3)
    surface = jnp.pad(twist[contact.reshape(own)], ((0, 0), (0, 1))).reshape(-1)

    dest = leaving_dest[:, 0]
    leaving = dest.shape[0]
    same = dest[:, None] == dest[None, :]
    earlier = lax.broadcasted_iota(I32, (leaving, leaving), 0) > lax.broadcasted_iota(I32, (leaving, leaving), 1)
    order = jnp.sum((same & earlier).astype(I32), axis=1)
    capacity = arrival_slot.shape[0] // ranks
    buffer_row = (dest * capacity + order).reshape(1, leaving)

    leave = (leaving_slot.reshape(-1, 1), buffer_row, ranks * capacity)
    state, outgoing = step_call(rows, cols, counts, pair_codes, surface, state, halo, leave)
    incoming = lax.all_to_all(outgoing.reshape(ranks, capacity, fields), AXES, 0, 0, tiled=True)
    state, *strips = insert(rows, cols, pair_codes, state, incoming.reshape(-1, fields), arrival_slot.reshape(-1, 1))
    state, density = step_call(rows, cols, None, pair_codes, surface, state, exchange(strips)[0])
    return state.reshape(particles.shape), density.reshape(rows, cols, block)


def solution(mesh):
    both = P("ax", "az")
    flat = P(AXES)
    return jax.shard_map(
        local,
        mesh=mesh,
        in_specs=(P("ax", "az", None, None), both, P("ax", "az", None), both, P(AXES, None), flat, P(AXES, None), flat),
        out_specs=(P("ax", "az", None, None), P("ax", "az", None)),
        check_vma=False,
    )
```

time: 166 us -> 151 us (0.910)
  local copies, waits for them, and re-layouts: 12.1 us -> 6.05 us
  Pallas kernels: 71.2 us -> 65.5 us
  other arithmetic: 6.83 us -> 2.12 us
  starting transfers between devices: 41.7 us -> 44.4 us
  waiting for transfers between devices: 32.9 us -> 30.8 us
    ppermute x12, waiting for transfers between devices: 21.7 us -> 9.88 us  [the longest x6 8.66 us: swap(): lax.ppermute(up, axis, pairs)]
    all_to_all x1, waiting for transfers between devices: 0.01 us -> 9.6 us  [local(): lax.all_to_all(told, AXES, 0, 0, tiled=True).reshape(ranks * segments, 3)]
    pallas_call x2, Pallas kernels: 58.8 us -> 51.2 us  [step_call(): pl.pallas_call(functools.partial(step_kernel, rows, cols, counts is not N...]
    select_n x1 -> x0, other arithmetic: 5.15 us -> none  [local(): state = jnp.where(keep[:, None, :], flat, 0.0)]
    ppermute x12, starting transfers between devices: 29.7 us -> 33.7 us  [the longest x6 17.4 us: swap(): lax.ppermute(down, axis, [(j, i) for i, j in pairs])]
    squeeze x8 -> x4, local copies, waits for them, and re-layouts: 3.29 us -> 0.05 us  [beside(): return jnp.concatenate([strip.reshape(-1, 128), low[n], high[n]], axis=0)]
    pallas_call x1, Pallas kernels: 1.99 us -> 5.17 us  [mask_strips(): pl.pallas_call(functools.partial(mask_kernel, rows, cols), out_shape=stri...]
    unnamed x39 -> x21, local copies, waits for them, and re-layouts: 5.03 us -> 3.48 us
  transfers between devices with their start and end apart: 14 -> 14, of which waited for: 6 -> 5; matrix products, arithmetic and copies ran while one was open for 8% -> 3% of each run, Pallas kernels for 0% -> 0%
where the time goes in v3:
time: 151 us; the launch traced here: 150 us
  Pallas kernels  65.5 us (43%)
  starting transfers between devices  44.4 us (29%)
  waiting for transfers between devices  30.8 us (20%)
  local copies, waits for them, and re-layouts  6.05 us (4%)
  other arithmetic  2.12 us (1%)
    pallas_call x2, Pallas kernels, step_call(): pl.pallas_call(functools.partial(step_kernel, rows, cols, counts is not N...  51.2 us
    ppermute x6, starting transfers between devices, swap(): lax.ppermute(down, axis, [(j, i) for i, j in pairs])  17.4 us
    ppermute x6, starting transfers between devices, swap(): lax.ppermute(up, axis, pairs)  16.3 us
    all_to_all x1, waiting for transfers between devices, local(): lax.all_to_all(outgoing.reshape(ranks, capacity, fields), AXES, 0, 0, til...  11.4 us
    all_to_all x1, waiting for transfers between devices, local(): lax.all_to_all(told, AXES, 0, 0, tiled=True).reshape(ranks * segments, 3)  9.6 us
    pallas_call x1, Pallas kernels, insert(): pl.pallas_call(functools.partial(insert_kernel, rows, cols), out_shape=(j...  9.15 us
    ppermute x6, waiting for transfers between devices, swap(): lax.ppermute(up, axis, pairs)  8.66 us
    all_to_all x1, starting transfers between devices, local(): lax.all_to_all(told, AXES, 0, 0, tiled=True).reshape(ranks * segments, 3)  6.42 us
  transfers between devices with their start and end apart: 14, of which 5 were waited for; matrix products, arithmetic and copies ran while one was open for 3% of the time, Pallas kernels for 0%

profile of v3, /device:TPU:1, one launch (start us, length us, event | category | flops | bytes accessed | tf_op | source)
XLA Modules:
  0.0 150.1 jit_solution(17766516489881862635)
XLA Ops:
  0.6 1.4 copy.31.codes.refs_1_.refs_0_
  2.0 5.2 %shard_map.95 = (f32[2,152,128]{2,1,0:T(8,128)}, f32[2,152,128]{2,1,0:T(8,128)}, f32[16,136,128]{2,1,0:T(8,128)}, f32[16,136,128]{2,1,0:T(8,128)}, f32[4,136,128]{2,1,0:T(8,128)}, /*index=5*/f32[4,136,128]{2,1,0:T(8,128)}) custom-call(s32[4,16]{1,0:T(4,128)} %refs_0_.2, s32[4,16,6]{2,1,0:T(8,128)} %copy.31.codes.refs_1_.refs_0_, f32[64,128,128]{2,1,0:T(8,128)} %bitcast.36), custom_call_target="tpu_custom_call" | custom-call | tf_op jit(solution)/shard_map/pallas_call | solution.py:142
  7.2 4.6 %collective-permute-start = (f32[2,152,128]{2,1,0:T(8,128)}, f32[2,152,128]{2,1,0:T(8,128)S(1)}, u32[]{:S(2)}, u32[]{:S(2)}) collective-permute-start(f32[2,152,128]{2,1,0:T(8,128)} %get-tuple-element.21), channel_id=1, source_target_pairs={{0,16},{16,32},{32,48},{48,64},{64,80},{80,96},{96,112},{1,17},{17... | collective-permute-start | bytes 466952 | tf_op jit(solution)/shard_map/ppermute | solution.py:570
  11.9 1.9 %collective-permute-start.1 = (f32[2,152,128]{2,1,0:T(8,128)}, f32[2,152,128]{2,1,0:T(8,128)S(1)}, u32[]{:S(2)}, u32[]{:S(2)}) collective-permute-start(f32[2,152,128]{2,1,0:T(8,128)} %get-tuple-element.22), channel_id=1, source_target_pairs={{16,0},{32,16},{48,32},{64,48},{80,64},{96,80},{112,96},{17,1},{33... | collective-permute-start | bytes 466952 | tf_op jit(solution)/shard_map/ppermute | solution.py:570
  13.8 3.6 %collective-permute-start.2 = (f32[16,136,128]{2,1,0:T(8,128)}, f32[16,136,128]{2,1,0:T(8,128)S(1)}, u32[]{:S(2)}, u32[]{:S(2)}) collective-permute-start(f32[16,136,128]{2,1,0:T(8,128)} %get-tuple-element.25), channel_id=1, source_target_pairs={{0,16},{16,32},{32,48},{48,64},{64,80},{80,96},{96,112},{1,17},{17... | collective-permute-start | bytes 3342344 | tf_op jit(solution)/shard_map/ppermute | solution.py:570
  17.5 1.9 %collective-permute-start.3 = (f32[16,136,128]{2,1,0:T(8,128)}, f32[16,136,128]{2,1,0:T(8,128)}, u32[]{:S(2)}, u32[]{:S(2)}) collective-permute-start(f32[16,136,128]{2,1,0:T(8,128)} %get-tuple-element.26), channel_id=1, source_target_pairs={{16,0},{32,16},{48,32},{64,48},{80,64},{96,80},{112,96},{17,1},{33... | collective-permute-start | bytes 3342344 | tf_op jit(solution)/shard_map/ppermute | solution.py:570
  19.4 0.1 reshape.109
  19.5 0.0 copy-start.8
  19.5 0.0 copy-start.9
  19.6 1.0 pad_maximum_fusion
  20.6 0.0 copy-start
  20.6 0.0 copy-start.1
  20.6 1.4 collective-permute-start.4
  22.0 5.0 %collective-permute-start.5 = (f32[848,128]{1,0:T(8,128)S(1)}, f32[848,128]{1,0:T(8,128)S(1)}, u32[]{:S(2)}, u32[]{:S(2)}) collective-permute-start(f32[848,128]{1,0:T(8,128)S(1)} %pad_maximum_fusion.1), channel_id=1, source_target_pairs={{1,0},{2,1},{3,2},{4,3},{5,4},{6,5},{7,6},{8,7},{9,8},{10,9},{11,1... | collective-permute-start | bytes 1302536 | tf_op jit(solution)/shard_map/ppermute | solution.py:570
  27.0 0.2 convert_reduce_fusion
  27.2 0.1 broadcast_in_dim.8
  27.3 0.7 broadcast_in_dim.9
  27.9 6.4 %all-to-all-start = ((f32[128,1,12]{2,1,0:T(1,128)}), f32[128,1,12]{2,1,0:T(1,128)S(1)}, u32[]{:S(2)}, u32[]{:S(2)}) async-start(f32[128,1,12]{2,1,0:T(1,128)} %broadcast_in_dim.9), calls=%async_computation | async-start | bytes 131072 | tf_op jit(solution)/shard_map/all_to_all | solution.py:595
  34.4 0.1 copy.28.refs_8_
  34.5 9.6 %all-to-all-done = f32[128,1,12]{2,1,0:T(1,128)S(1)} async-done(((f32[128,1,12]{2,1,0:T(1,128)}), f32[128,1,12]{2,1,0:T(1,128)S(1)}, u32[]{:S(2)}, u32[]{:S(2)}) %all-to-all-start) | async-done | bytes 6176 | tf_op jit(solution)/shard_map/all_to_all | solution.py:595
  44.1 0.6 broadcast.35
  44.7 0.8 reduce.3
  45.6 0.1 reshape.108
  45.7 0.6 gather_fusion
  46.3 0.1 reshape.110.refs_2_.refs_1_
  46.4 0.0 copy-start.6
  46.4 0.0 collective-permute-done.4.refs_6_
  46.5 0.0 collective-permute-done.2.refs_4_
  46.5 0.0 collective-permute-done.3.refs_5_
  46.5 1.0 copy-done.2
  47.5 27.4 %shard_map.96 = (f32[64,128,128]{2,1,0:T(8,128)}, f32[512,128]{1,0:T(8,128)}) custom-call(s32[4,16]{1,0:T(4,128)S(1)} %copy-done.1, s32[4,16,6]{2,1,0:T(8,128)S(1)} %copy-done, f32[256]{0:T(256)S(1)} %reshape.110.refs_2_.refs_1_, f32[64,128,128]{2,1,0:T(8,128)} %bitcast.37, f32[16,136,128]{2,1,0:T(8,128)} %copy-done.2, ...), custom_call_target="tpu_custom_call" | custom-call | tf_op jit(solution)/shard_map/pallas_call | solution.py:489
  74.9 4.3 %all-to-all-start.1 = ((f32[128,4,128]{2,1,0:T(4,128)}), f32[128,4,128]{2,1,0:T(4,128)S(1)}, u32[]{:S(2)}, u32[]{:S(2)}) async-start(f32[128,4,128]{2,1,0:T(4,128)} %bitcast.12), calls=%async_computation.1 | async-start | bytes 524288 | tf_op jit(solution)/shard_map/all_to_all | solution.py:608
  79.1 0.1 copy.30.slots
  79.3 11.4 %all-to-all-done.1 = f32[128,4,128]{2,1,0:T(4,128)S(1)} async-done(((f32[128,4,128]{2,1,0:T(4,128)}), f32[128,4,128]{2,1,0:T(4,128)S(1)}, u32[]{:S(2)}, u32[]{:S(2)}) %all-to-all-start.1) | async-done | bytes 262176 | tf_op jit(solution)/shard_map/all_to_all | solution.py:608
  90.7 9.2 %shard_map.97 = (f32[64,128,128]{2,1,0:T(8,128)}, f32[2,152,128]{2,1,0:T(8,128)S(1)}, f32[2,152,128]{2,1,0:T(8,128)S(1)}, f32[16,136,128]{2,1,0:T(8,128)}, f32[1...) custom-call(s32[4,16,6]{2,1,0:T(8,128)S(1)} %copy-done, ...), custom_call_target="tpu_custom_call" | custom-call | tf_op jit(solution)/shard_map/pallas_call | solution.py:557
  99.8 2.6 %collective-permute-start.8 = (f32[2,152,128]{2,1,0:T(8,128)S(1)}, f32[2,152,128]{2,1,0:T(8,128)S(1)}, u32[]{:S(2)}, u32[]{:S(2)}) collective-permute-start(f32[2,152,128]{2,1,0:T(8,128)S(1)} %get-tuple-element.33), channel_id=1, source_target_pairs={{0,16},{16,32},{32,48},{48,64},{64,80},{80,96},{96,112},{1,17},{17... | collective-permute-start | bytes 466952 | tf_op jit(solution)/shard_map/ppermute | solution.py:570
  102.4 1.9 %collective-permute-start.9 = (f32[2,152,128]{2,1,0:T(8,128)S(1)}, f32[2,152,128]{2,1,0:T(8,128)S(1)}, u32[]{:S(2)}, u32[]{:S(2)}) collective-permute-start(f32[2,152,128]{2,1,0:T(8,128)S(1)} %get-tuple-element.34), channel_id=1, source_target_pairs={{16,0},{32,16},{48,32},{64,48},{80,64},{96,80},{112,96},{17,1},{33... | collective-permute-start | bytes 466952 | tf_op jit(solution)/shard_map/ppermute | solution.py:570
  104.4 3.6 %collective-permute-start.6 = (f32[16,136,128]{2,1,0:T(8,128)}, f32[16,136,128]{2,1,0:T(8,128)S(1)}, u32[]{:S(2)}, u32[]{:S(2)}) collective-permute-start(f32[16,136,128]{2,1,0:T(8,128)} %get-tuple-element.30), channel_id=1, source_target_pairs={{0,16},{16,32},{32,48},{48,64},{64,80},{80,96},{96,112},{1,17},{17... | collective-permute-start | bytes 3342344 | tf_op jit(solution)/shard_map/ppermute | solution.py:570
  108.0 1.9 %collective-permute-start.7 = (f32[16,136,128]{2,1,0:T(8,128)}, f32[16,136,128]{2,1,0:T(8,128)S(1)}, u32[]{:S(2)}, u32[]{:S(2)}) collective-permute-start(f32[16,136,128]{2,1,0:T(8,128)} %get-tuple-element.31), channel_id=1, source_target_pairs={{16,0},{32,16},{48,32},{64,48},{80,64},{96,80},{112,96},{17,1},{33... | collective-permute-start | bytes 3342344 | tf_op jit(solution)/shard_map/ppermute | solution.py:570
  109.9 0.0 collective-permute-done.8
  110.0 0.0 collective-permute-done.9
  110.0 0.4 collective-permute-start.10
  110.5 4.7 %collective-permute-start.11 = (f32[848,128]{1,0:T(8,128)S(1)}, f32[848,128]{1,0:T(8,128)S(1)}, u32[]{:S(2)}, u32[]{:S(2)}) collective-permute-start(f32[848,128]{1,0:T(8,128)S(1)} %pad_maximum_fusion.3), channel_id=1, source_target_pairs={{1,0},{2,1},{3,2},{4,3},{5,4},{6,5},{7,6},{8,7},{9,8},{10,9},{11,1... | collective-permute-start | bytes 1302536 | tf_op jit(solution)/shard_map/ppermute | solution.py:570
  115.2 8.6 %collective-permute-done.10.refs_5_ = f32[848,128]{1,0:T(8,128)S(1)} collective-permute-done((f32[848,128]{1,0:T(8,128)S(1)}, f32[848,128]{1,0:T(8,128)S(1)}, u32[]{:S(2)}, u32[]{:S(2)}) %collective-permute-start.10) | collective-permute-done | bytes 434208 | tf_op jit(solution)/shard_map/ppermute | solution.py:570
  123.8 0.1 collective-permute-done.11.refs_6_
  124.0 1.1 collective-permute-done.7.refs_4_
  125.1 1.0 copy-done.3
  126.1 23.8 %shard_map.98 = (f32[64,128,128]{2,1,0:T(8,128)}, f32[64,128]{1,0:T(8,128)}) custom-call(s32[4,16,6]{2,1,0:T(8,128)S(1)} %copy-done, f32[256]{0:T(256)S(1)} %reshape.110.refs_2_.refs_1_, f32[64,128,128]{2,1,0:T(8,128)} %get-tuple-element.29.refs_2_, f32[16,136,128]{2,1,0:T(8,128)S(1)} %collective-permute-done.6.refs_3_, f32[16,136,128]{2,1,0:T(8,128)} %copy-done.3, ...), custom_call_target="tpu_custom_call" | custom-call | tf_op jit(solution)/shard_map/pallas_call | solution.py:489
  (28 shorter events, 0.2 us)
Async XLA Ops:
  2.0 17.4 %copy-start.7 = (s32[4,16]{1,0:T(4,128)S(1)}, s32[4,16]{1,0:T(4,128)}, u32[]{:S(2)}) copy-start(s32[4,16]{1,0:T(4,128)} %param.11) | copy-start | bytes 772
  7.2 14.7 %copy-start.4 = (f32[4,136,128]{2,1,0:T(8,128)S(1)}, f32[4,136,128]{2,1,0:T(8,128)}, u32[]{:S(2)}) copy-start(f32[4,136,128]{2,1,0:T(8,128)} %get-tuple-element.23) | copy-start | bytes 835588
  7.2 12.3 %collective-permute-start = (f32[2,152,128]{2,1,0:T(8,128)}, f32[2,152,128]{2,1,0:T(8,128)S(1)}, u32[]{:S(2)}, u32[]{:S(2)}) collective-permute-start(f32[2,152,128]{2,1,0:T(8,128)} %get-tuple-element.21), channel_id=1, source_target_pairs={{0,16},{16,32},{32,48},{48,64},{64,80},{80,96},{96,112},{1,17},{17... | collective-permute-start | bytes 466952 | tf_op jit(solution)/shard_map/ppermute | solution.py:570
  11.9 7.7 %collective-permute-start.1 = (f32[2,152,128]{2,1,0:T(8,128)}, f32[2,152,128]{2,1,0:T(8,128)S(1)}, u32[]{:S(2)}, u32[]{:S(2)}) collective-permute-start(f32[2,152,128]{2,1,0:T(8,128)} %get-tuple-element.22), channel_id=1, source_target_pairs={{16,0},{32,16},{48,32},{64,48},{80,64},{96,80},{112,96},{17,1},{33... | collective-permute-start | bytes 466952 | tf_op jit(solution)/shard_map/ppermute | solution.py:570
  13.8 32.6 %collective-permute-start.2 = (f32[16,136,128]{2,1,0:T(8,128)}, f32[16,136,128]{2,1,0:T(8,128)S(1)}, u32[]{:S(2)}, u32[]{:S(2)}) collective-permute-start(f32[16,136,128]{2,1,0:T(8,128)} %get-tuple-element.25), channel_id=1, source_target_pairs={{0,16},{16,32},{32,48},{48,64},{64,80},{80,96},{96,112},{1,17},{17... | collective-permute-start | bytes 3342344 | tf_op jit(solution)/shard_map/ppermute | solution.py:570
  17.5 29.0 %collective-permute-start.3 = (f32[16,136,128]{2,1,0:T(8,128)}, f32[16,136,128]{2,1,0:T(8,128)}, u32[]{:S(2)}, u32[]{:S(2)}) collective-permute-start(f32[16,136,128]{2,1,0:T(8,128)} %get-tuple-element.26), channel_id=1, source_target_pairs={{16,0},{32,16},{48,32},{64,48},{80,64},{96,80},{112,96},{17,1},{33... | collective-permute-start | bytes 3342344 | tf_op jit(solution)/shard_map/ppermute | solution.py:570
  19.5 7.5 %copy-start.5 = (s32[256,1]{0,1:T(1,128)S(1)}, s32[256,1]{0,1:T(1,128)}, u32[]{:S(2)}) copy-start(s32[256,1]{0,1:T(1,128)} %param.14) | copy-start | bytes 3076
  19.5 7.7 %copy-start.8 = (f32[4,3]{1,0:T(4,128)S(1)}, f32[4,3]{1,0:T(4,128)}, u32[]{:S(2)}) copy-start(f32[4,3]{1,0:T(4,128)} %param.12) | copy-start | bytes 148
  19.5 14.9 %copy-start.9 = (s32[256]{0:T(256)S(1)}, s32[256]{0:T(256)}, u32[]{:S(2)}) copy-start(s32[256]{0:T(256)} %param.13) | copy-start | bytes 3076
  20.6 26.9 %copy-start = (s32[4,16,6]{2,1,0:T(8,128)S(1)}, s32[4,16,6]{2,1,0:T(8,128)}, u32[]{:S(2)}) copy-start(s32[4,16,6]{2,1,0:T(8,128)} %copy.31.codes.refs_1_.refs_0_) | copy-start | bytes 4612
  20.6 26.9 %copy-start.1 = (s32[4,16]{1,0:T(4,128)S(1)}, s32[4,16]{1,0:T(4,128)}, u32[]{:S(2)}) copy-start(s32[4,16]{1,0:T(4,128)} %refs_0_.2) | copy-start | bytes 772
  20.6 25.8 %collective-permute-start.4 = (f32[848,128]{1,0:T(8,128)S(1)}, f32[848,128]{1,0:T(8,128)S(1)}, u32[]{:S(2)}, u32[]{:S(2)}) collective-permute-start(f32[848,128]{1,0:T(8,128)S(1)} %pad_maximum_fusion), channel_id=1, source_target_pairs={{0,1},{1,2},{2,3},{3,4},{4,5},{5,6},{6,7},{7,8},{8,9},{9,10},{10,1... | collective-permute-start | bytes 1302536 | tf_op jit(solution)/shard_map/ppermute | solution.py:570
  22.0 24.5 %collective-permute-start.5 = (f32[848,128]{1,0:T(8,128)S(1)}, f32[848,128]{1,0:T(8,128)S(1)}, u32[]{:S(2)}, u32[]{:S(2)}) collective-permute-start(f32[848,128]{1,0:T(8,128)S(1)} %pad_maximum_fusion.1), channel_id=1, source_target_pairs={{1,0},{2,1},{3,2},{4,3},{5,4},{6,5},{7,6},{8,7},{9,8},{10,9},{11,1... | collective-permute-start | bytes 1302536 | tf_op jit(solution)/shard_map/ppermute | solution.py:570
  27.9 16.2 %all-to-all-start = ((f32[128,1,12]{2,1,0:T(1,128)}), f32[128,1,12]{2,1,0:T(1,128)S(1)}, u32[]{:S(2)}, u32[]{:S(2)}) async-start(f32[128,1,12]{2,1,0:T(1,128)} %broadcast_in_dim.9), calls=%async_computation | async-start | bytes 131072 | tf_op jit(solution)/shard_map/all_to_all | solution.py:595
  46.4 32.7 %copy-start.6 = (s32[512]{0:T(512)S(1)}, s32[512]{0:T(512)}, u32[]{:S(2)}) copy-start(s32[512]{0:T(512)} %param.15) | copy-start | bytes 6148
  46.5 1.0 copy-start.2
  74.9 15.8 %all-to-all-start.1 = ((f32[128,4,128]{2,1,0:T(4,128)}), f32[128,4,128]{2,1,0:T(4,128)S(1)}, u32[]{:S(2)}, u32[]{:S(2)}) async-start(f32[128,4,128]{2,1,0:T(4,128)} %bitcast.12), calls=%async_computation.1 | async-start | bytes 524288 | tf_op jit(solution)/shard_map/all_to_all | solution.py:608
  99.8 10.1 %collective-permute-start.8 = (f32[2,152,128]{2,1,0:T(8,128)S(1)}, f32[2,152,128]{2,1,0:T(8,128)S(1)}, u32[]{:S(2)}, u32[]{:S(2)}) collective-permute-start(f32[2,152,128]{2,1,0:T(8,128)S(1)} %get-tuple-element.33), channel_id=1, source_target_pairs={{0,16},{16,32},{32,48},{48,64},{64,80},{80,96},{96,112},{1,17},{17... | collective-permute-start | bytes 466952 | tf_op jit(solution)/shard_map/ppermute | solution.py:570
  102.4 7.5 %collective-permute-start.9 = (f32[2,152,128]{2,1,0:T(8,128)S(1)}, f32[2,152,128]{2,1,0:T(8,128)S(1)}, u32[]{:S(2)}, u32[]{:S(2)}) collective-permute-start(f32[2,152,128]{2,1,0:T(8,128)S(1)} %get-tuple-element.34), channel_id=1, source_target_pairs={{16,0},{32,16},{48,32},{64,48},{80,64},{96,80},{112,96},{17,1},{33... | collective-permute-start | bytes 466952 | tf_op jit(solution)/shard_map/ppermute | solution.py:570
  104.4 19.6 %collective-permute-start.6 = (f32[16,136,128]{2,1,0:T(8,128)}, f32[16,136,128]{2,1,0:T(8,128)S(1)}, u32[]{:S(2)}, u32[]{:S(2)}) collective-permute-start(f32[16,136,128]{2,1,0:T(8,128)} %get-tuple-element.30), channel_id=1, source_target_pairs={{0,16},{16,32},{32,48},{48,64},{64,80},{80,96},{96,112},{1,17},{17... | collective-permute-start | bytes 3342344 | tf_op jit(solution)/shard_map/ppermute | solution.py:570
  108.0 17.0 %collective-permute-start.7 = (f32[16,136,128]{2,1,0:T(8,128)}, f32[16,136,128]{2,1,0:T(8,128)S(1)}, u32[]{:S(2)}, u32[]{:S(2)}) collective-permute-start(f32[16,136,128]{2,1,0:T(8,128)} %get-tuple-element.31), channel_id=1, source_target_pairs={{16,0},{32,16},{48,32},{64,48},{80,64},{96,80},{112,96},{17,1},{33... | collective-permute-start | bytes 3342344 | tf_op jit(solution)/shard_map/ppermute | solution.py:570
  110.0 13.8 %collective-permute-start.10 = (f32[848,128]{1,0:T(8,128)S(1)}, f32[848,128]{1,0:T(8,128)S(1)}, u32[]{:S(2)}, u32[]{:S(2)}) collective-permute-start(f32[848,128]{1,0:T(8,128)S(1)} %pad_maximum_fusion.2), channel_id=1, source_target_pairs={{0,1},{1,2},{2,3},{3,4},{4,5},{5,6},{6,7},{7,8},{8,9},{9,10},{10,1... | collective-permute-start | bytes 1302536 | tf_op jit(solution)/shard_map/ppermute | solution.py:570
  110.5 13.5 %collective-permute-start.11 = (f32[848,128]{1,0:T(8,128)S(1)}, f32[848,128]{1,0:T(8,128)S(1)}, u32[]{:S(2)}, u32[]{:S(2)}) collective-permute-start(f32[848,128]{1,0:T(8,128)S(1)} %pad_maximum_fusion.3), channel_id=1, source_target_pairs={{1,0},{2,1},{3,2},{4,3},{5,4},{6,5},{7,6},{8,7},{9,8},{10,9},{11,1... | collective-permute-start | bytes 1302536 | tf_op jit(solution)/shard_map/ppermute | solution.py:570
  125.0 1.0 copy-start.3

commit v4 on v3

--- a/solution.py
+++ b/solution.py
@@ -56,7 +56,7 @@
     lane = lax.broadcasted_iota(I32, (8, 128), 1)
     listed = jnp.zeros((8, 128), F32)
     for j in range(6):
-        listed = jnp.where(lane == j, codes[r, c, j].astype(F32), listed)
+        listed = jnp.where(lane == j, codes[j, r, c].astype(F32), listed)
     return jnp.where(sub_iota((8, 128)) == 7, listed, behind)
 
 
@@ -157,18 +157,19 @@
 def step_kernel(rows, cols, masked, leaving, *refs):
     if masked:
         counts, refs = refs[0], refs[1:]
-    codes, surf, cells_in, a_low, a_high, z_low, z_high = refs[:7]
+    codes, segments, contact, cells_in, a_low, a_high, z_low, z_high = refs[:8]
     if leaving:
-        slots, buffer_row, out_ref, sent, gathered = refs[7:12]
-        refs = refs[12:]
+        slots, buffer_row, out_ref, sent, gathered = refs[8:13]
+        refs = refs[13:]
     else:
-        out_ref, dens = refs[7:9]
-        refs = refs[9:]
+        out_ref, dens = refs[8:10]
+        refs = refs[10:]
     geo, cells, out, side_t, side_s, feat, squares, row_t, row_s = refs[:9]
     mass, root, rho, ratio, inverse, ring_codes, geo_came, cells_came, out_left, codes_came = refs[9:]
     width = cols + 4
     own = rows * cols
     z_rows = rows * EDGE
+    per_device = segments.shape[1] // 3
     sub8 = sub_iota((8, 128))
     row_mid, col_mid = (rows + 3) / 2.0, (cols + 3) / 2.0
 
@@ -306,13 +307,13 @@
     rho[...] = jnp.ones_like(rho)
 
     def own_density(i):
-        for k in range(8):
-            n = i * 8 + k
+        for k in range(16):
+            n = i * 16 + k
             r, c = n // cols, n % cols
             center = (r + 2) * width + c + 2
-            density(center, [linked(center, codes[r, c, j], width) for j in range(6)], n)
-
-    loop(own // 8, own_density)
+            density(center, [linked(center, codes[j, r, c], width) for j in range(6)], n)
+
+    loop(own // 16, own_density)
     for copy in code_copies:
         copy.wait()
 
@@ -320,12 +321,12 @@
         density(center, [linked(center, ring_codes[n, j].astype(I32), width) for j in range(6)], None)
 
     def ring_rows(i):
-        for k in range(4):
-            c = i * 4 + k
+        for k in range(8):
+            c = i * 8 + k
             ring_cell(width + c + 2, c)
             ring_cell((rows + 2) * width + c + 2, cols + c)
 
-    loop(cols // 4, ring_rows)
+    loop(cols // 8, ring_rows)
     for k, r in enumerate([r + 2 for r in range(rows)] + [1, rows + 2]):
         ring_cell(r * width + 1, 2 * cols + k)
         ring_cell(r * width + cols + 2, 2 * cols + rows + 2 + k)
@@ -392,7 +393,7 @@
     def force(n):
         r, c = n // cols, n % cols
         index = (r + 2) * width + c + 2
-        lhs = jnp.concatenate([feat[linked(index, codes[r, c, j], width)] for j in range(6)], axis=1)
+        lhs = jnp.concatenate([feat[linked(index, codes[j, r, c], width)] for j in range(6)], axis=1)
         sums = jnp.dot(lhs, squares[n], preferred_element_type=F32)
         if masked:
             held = lax.broadcasted_iota(I32, (8, 128), 1) < counts[r, c]
@@ -410,7 +411,9 @@
         press = press * jnp.where(sub8 < 4, row8(ratio, index), 1.0)
         press = press + pltpu.roll(press, 4, 0)
         weight, friction = rows_of(first[6:7], 8), rows_of(first[7:8], 8)
-        surface = jnp.where(sub8 == 3, surf[n * 4], jnp.where(sub8 == 4, surf[n * 4 + 1], surf[n * 4 + 2]))
+        touching = contact[r, c]
+        device, place = touching // per_device, (touching % per_device) * 3
+        surface = jnp.where(sub8 == 3, segments[device, place], jnp.where(sub8 == 4, segments[device, place + 1], segments[device, place + 2]))
         wall = wall_gain * jnp.maximum(1.0 - 3.0 * rows_of(g[2:3], 8), 0.0)
         accel = nu * (first - g * weight) + pltpu.roll(first, 3, 0) - g * friction + wall * (surface - g)
         accel = accel - 6.0 * pltpu.roll(press, 2, 0)
@@ -473,7 +476,7 @@
     return pl.BlockSpec(memory_space=pltpu.VMEM)
 
 
-def step_call(rows, cols, counts, codes, surface, cells, halo, leave=None):
+def step_call(rows, cols, counts, codes, segments, contact, cells, halo, leave=None):
     own = rows * cols
     patch = (rows + 4) * (cols + 4)
     ring = 2 * cols + 2 * (rows + 2)
@@ -489,7 +492,7 @@
     return pl.pallas_call(
         functools.partial(step_kernel, rows, cols, counts is not None, bool(leave)),
         out_shape=outs,
-        in_specs=[smem_spec()] * (len(scalars) + 2) + [any_spec()] + [vmem_spec()] * (4 + len(extra)),
+        in_specs=[smem_spec()] * (len(scalars) + 3) + [any_spec()] + [vmem_spec()] * (4 + len(extra)),
         out_specs=(any_spec(), vmem_spec()),
         scratch_shapes=first
         + [
@@ -511,8 +514,8 @@
             pltpu.SemaphoreType.DMA((own // 8,)),
             pltpu.SemaphoreType.DMA((2 + 2 * (rows + 2),)),
         ],
-        compiler_params=pltpu.CompilerParams(vmem_limit_bytes=52 * MIB),
-    )(*scalars, codes, surface, cells, *halo, *extra)
+        compiler_params=pltpu.CompilerParams(vmem_limit_bytes=47 * MIB),
+    )(*scalars, codes, segments, contact, cells, *halo, *extra)
 
 
 def insert_kernel(rows, cols, codes, state_in, incoming, slots, out_ref, *refs):
@@ -587,13 +590,13 @@
     ranks = lax.axis_size("ax") * lax.axis_size("az")
     own = rows * cols
     state = particles.reshape(own, fields, block)
+    pair_codes = pair_codes.transpose(2, 0, 1)
     halo, sides = exchange(mask_strips(rows, cols, counts, pair_codes, state))
 
     segments = twist_state.shape[0]
     twist_state, _ = lax.optimization_barrier((twist_state, sides))
     told = jnp.broadcast_to(twist_state.reshape(1, segments * 3), (ranks, segments * 3))
-    twist = lax.all_to_all(told, AXES, 0, 0, tiled=True).reshape(ranks * segments, 3)
-    surface = jnp.pad(twist[contact.reshape(own)], ((0, 0), (0, 1))).reshape(-1)
+    told = lax.all_to_all(told, AXES, 0, 0, tiled=True)
 
     dest = leaving_dest[:, 0]
     leaving = dest.shape[0]
@@ -604,10 +607,10 @@
     buffer_row = (dest * capacity + order).reshape(1, leaving)
 
     leave = (leaving_slot.reshape(-1, 1), buffer_row, ranks * capacity)
-    state, outgoing = step_call(rows, cols, counts, pair_codes, surface, state, halo, leave)
+    state, outgoing = step_call(rows, cols, counts, pair_codes, told, contact, state, halo, leave)
     incoming = lax.all_to_all(outgoing.reshape(ranks, capacity, fields), AXES, 0, 0, tiled=True)
     state, *strips = insert(rows, cols, pair_codes, state, incoming.reshape(-1, fields), arrival_slot.reshape(-1, 1))
-    state, density = step_call(rows, cols, None, pair_codes, surface, state, exchange(strips)[0])
+    state, density = step_call(rows, cols, None, pair_codes, told, contact, state, exchange(strips)[0])
     return state.reshape(particles.shape), density.reshape(rows, cols, block)
 
 

time: 151 us -> 145 us (0.960)
  local copies, waits for them, and re-layouts: 6.05 us -> 1.12 us
    unnamed x21 -> x16, local copies, waits for them, and re-layouts: 3.48 us -> 0.05 us
    concatenate x4, other arithmetic: 1.07 us -> 2.64 us  [beside(): return jnp.concatenate([strip.reshape(-1, 128), low[n], high[n]], axis=0)]
where the time goes in v4:
time: 145 us; the launch traced here: 144 us
  Pallas kernels  64 us (44%)
  starting transfers between devices  44.3 us (31%)
  waiting for transfers between devices  30.8 us (21%)
  other arithmetic  2.82 us (2%)
    pallas_call x2, Pallas kernels, step_call(): pl.pallas_call(functools.partial(step_kernel, rows, cols, counts is not N...  50.4 us
    ppermute x6, starting transfers between devices, swap(): lax.ppermute(down, axis, [(j, i) for i, j in pairs])  17.3 us
    ppermute x6, starting transfers between devices, swap(): lax.ppermute(up, axis, pairs)  16.3 us
    all_to_all x1, waiting for transfers between devices, local(): lax.all_to_all(outgoing.reshape(ranks, capacity, fields), AXES, 0, 0, til...  11.3 us
    all_to_all x1, waiting for transfers between devices, local(): told = lax.all_to_all(told, AXES, 0, 0, tiled=True)  9.6 us
    pallas_call x1, Pallas kernels, insert(): pl.pallas_call(functools.partial(insert_kernel, rows, cols), out_shape=(j...  8.87 us
    ppermute x6, waiting for transfers between devices, swap(): lax.ppermute(up, axis, pairs)  8.66 us
    all_to_all x1, starting transfers between devices, local(): told = lax.all_to_all(told, AXES, 0, 0, tiled=True)  6.44 us
  transfers between devices with their start and end apart: 14, of which 5 were waited for; matrix products, arithmetic and copies ran while one was open for 3% of the time, Pallas kernels for 0%

profile of v4, /device:TPU:1, one launch (start us, length us, event | category | flops | bytes accessed | tf_op | source)
XLA Modules:
  0.0 144.2 jit_solution(15988576820313427587)
XLA Ops:
  0.6 4.7 %shard_map.95 = (f32[2,152,128]{2,1,0:T(8,128)}, f32[2,152,128]{2,1,0:T(8,128)}, f32[16,136,128]{2,1,0:T(8,128)}, f32[16,136,128]{2,1,0:T(8,128)}, f32[4,136,128]{2,1,0:T(8,128)}, /*index=5*/f32[4,136,128]{2,1,0:T(8,128)}) custom-call(s32[4,16]{1,0:T(4,128)} %refs_0_.1, s32[6,4,16]{2,1,0:T(4,128)} %bitcast.38, f32[64,128,128]{2,1,0:T(8,128)} %bitcast.42), custom_call_target="tpu_custom_call" | custom-call | tf_op jit(solution)/shard_map/pallas_call | solution.py:142
  5.4 0.0 copy-start.3
  5.4 4.6 %collective-permute-start = (f32[2,152,128]{2,1,0:T(8,128)}, f32[2,152,128]{2,1,0:T(8,128)S(1)}, u32[]{:S(2)}, u32[]{:S(2)}) collective-permute-start(f32[2,152,128]{2,1,0:T(8,128)} %get-tuple-element.21), channel_id=1, source_target_pairs={{0,16},{16,32},{32,48},{48,64},{64,80},{80,96},{96,112},{1,17},{17... | collective-permute-start | bytes 466952 | tf_op jit(solution)/shard_map/ppermute | solution.py:573
  10.0 1.9 %collective-permute-start.1 = (f32[2,152,128]{2,1,0:T(8,128)}, f32[2,152,128]{2,1,0:T(8,128)S(1)}, u32[]{:S(2)}, u32[]{:S(2)}) collective-permute-start(f32[2,152,128]{2,1,0:T(8,128)} %get-tuple-element.22), channel_id=1, source_target_pairs={{16,0},{32,16},{48,32},{64,48},{80,64},{96,80},{112,96},{17,1},{33... | collective-permute-start | bytes 466952 | tf_op jit(solution)/shard_map/ppermute | solution.py:573
  12.0 3.6 %collective-permute-start.2 = (f32[16,136,128]{2,1,0:T(8,128)}, f32[16,136,128]{2,1,0:T(8,128)S(1)}, u32[]{:S(2)}, u32[]{:S(2)}) collective-permute-start(f32[16,136,128]{2,1,0:T(8,128)} %get-tuple-element.25), channel_id=1, source_target_pairs={{0,16},{16,32},{32,48},{48,64},{64,80},{80,96},{96,112},{1,17},{17... | collective-permute-start | bytes 3342344 | tf_op jit(solution)/shard_map/ppermute | solution.py:573
  15.6 0.0 copy-start.4
  15.6 0.0 copy-start.6
  15.6 1.9 %collective-permute-start.3 = (f32[16,136,128]{2,1,0:T(8,128)}, f32[16,136,128]{2,1,0:T(8,128)S(1)}, u32[]{:S(2)}, u32[]{:S(2)}) collective-permute-start(f32[16,136,128]{2,1,0:T(8,128)} %get-tuple-element.26), channel_id=1, source_target_pairs={{16,0},{32,16},{48,32},{64,48},{80,64},{96,80},{112,96},{17,1},{33... | collective-permute-start | bytes 3342344 | tf_op jit(solution)/shard_map/ppermute | solution.py:573
  17.6 0.0 collective-permute-done
  17.6 0.0 copy-start.7
  17.6 0.0 collective-permute-done.1
  17.6 0.0 copy-start
  17.6 0.0 copy-start.1
  17.7 0.0 copy-start.2
  17.7 1.8 %pad_maximum_fusion = f32[848,128]{1,0:T(8,128)} fusion(f32[152,128]{1,0:T(8,128)S(1)} %get-tuple-element.45, f32[152,128]{1,0:T(8,128)S(1)} %get-tuple-element.43, f32[544,128]{1,0:T(8,128)} %bitcast.45), kind=kLoop, calls=%fused_computation | loop fusion | flops 217088 | bytes 868352 | tf_op jit(solution)/shard_map/concatenate | solution.py:582
  19.4 1.3 collective-permute-start.4
  20.7 0.8 pad_maximum_fusion.1
  21.5 4.9 %collective-permute-start.5 = (f32[848,128]{1,0:T(8,128)}, f32[848,128]{1,0:T(8,128)S(1)}, u32[]{:S(2)}, u32[]{:S(2)}) collective-permute-start(f32[848,128]{1,0:T(8,128)} %pad_maximum_fusion.1), channel_id=1, source_target_pairs={{1,0},{2,1},{3,2},{4,3},{5,4},{6,5},{7,6},{8,7},{9,8},{10,9},{11,1... | collective-permute-start | bytes 1302536 | tf_op jit(solution)/shard_map/ppermute | solution.py:573
  26.5 0.2 convert_reduce_fusion
  26.6 0.1 broadcast_in_dim.7
  26.7 0.7 broadcast_in_dim.8
  27.4 6.4 %all-to-all-start = ((f32[128,1,12]{2,1,0:T(1,128)}), f32[128,1,12]{2,1,0:T(1,128)S(1)}, u32[]{:S(2)}, u32[]{:S(2)}) async-start(f32[128,1,12]{2,1,0:T(1,128)} %broadcast_in_dim.8), calls=%async_computation | async-start | bytes 131072 | tf_op jit(solution)/shard_map/all_to_all | solution.py:599
  33.9 0.0 copy-done.7
  33.9 0.1 copy.14.refs_9_
  34.0 9.6 %all-to-all-done = f32[128,1,12]{2,1,0:T(1,128)S(1)} async-done(((f32[128,1,12]{2,1,0:T(1,128)}), f32[128,1,12]{2,1,0:T(1,128)S(1)}, u32[]{:S(2)}, u32[]{:S(2)}) %all-to-all-start) | async-done | bytes 6176 | tf_op jit(solution)/shard_map/all_to_all | solution.py:599
  43.6 0.0 collective-permute-done.4.refs_7_
  43.6 0.0 collective-permute-done.5.refs_8_
  43.6 0.0 collective-permute-done.2.refs_5_
  43.6 0.0 collective-permute-done.3.refs_6_
  43.7 0.0 copy-start.5
  43.7 26.8 %shard_map.96 = (f32[64,128,128]{2,1,0:T(8,128)}, f32[512,128]{1,0:T(8,128)}) custom-call(s32[4,16]{1,0:T(4,128)S(1)} %copy-done.1, s32[6,4,16]{2,1,0:T(4,128)S(1)} %bitcast.39, f32[128,12]{1,0:T(8,128)S(1)} %bitcast.34, s32[4,16]{1,0:T(4,128)S(1)} %copy-done.2, f32[64,128,128]{2,1,0:T(8,128)} %bitcast.43, ...), custom_call_target="tpu_custom_call" | custom-call | tf_op jit(solution)/shard_map/pallas_call | solution.py:492
  70.5 4.3 %all-to-all-start.1 = ((f32[128,4,128]{2,1,0:T(4,128)}), f32[128,4,128]{2,1,0:T(4,128)S(1)}, u32[]{:S(2)}, u32[]{:S(2)}) async-start(f32[128,4,128]{2,1,0:T(4,128)} %bitcast.13), calls=%async_computation.1 | async-start | bytes 524288 | tf_op jit(solution)/shard_map/all_to_all | solution.py:611
  74.8 0.1 copy.15.slots
  75.0 11.3 %all-to-all-done.1 = f32[128,4,128]{2,1,0:T(4,128)S(1)} async-done(((f32[128,4,128]{2,1,0:T(4,128)}), f32[128,4,128]{2,1,0:T(4,128)S(1)}, u32[]{:S(2)}, u32[]{:S(2)}) %all-to-all-start.1) | async-done | bytes 262176 | tf_op jit(solution)/shard_map/all_to_all | solution.py:611
  86.3 8.9 %shard_map.97 = (f32[64,128,128]{2,1,0:T(8,128)}, f32[2,152,128]{2,1,0:T(8,128)S(1)}, f32[2,152,128]{2,1,0:T(8,128)S(1)}, f32[16,136,128]{2,1,0:T(8,128)}, f32[1...) custom-call(s32[6,4,16]{2,1,0:T(4,128)S(1)} %bitcast.40, ...), custom_call_target="tpu_custom_call" | custom-call | tf_op jit(solution)/shard_map/pallas_call | solution.py:560
  95.2 2.6 %collective-permute-start.8 = (f32[2,152,128]{2,1,0:T(8,128)S(1)}, f32[2,152,128]{2,1,0:T(8,128)S(1)}, u32[]{:S(2)}, u32[]{:S(2)}) collective-permute-start(f32[2,152,128]{2,1,0:T(8,128)S(1)} %get-tuple-element.33), channel_id=1, source_target_pairs={{0,16},{16,32},{32,48},{48,64},{64,80},{80,96},{96,112},{1,17},{17... | collective-permute-start | bytes 466952 | tf_op jit(solution)/shard_map/ppermute | solution.py:573
  97.8 1.9 %collective-permute-start.9 = (f32[2,152,128]{2,1,0:T(8,128)S(1)}, f32[2,152,128]{2,1,0:T(8,128)S(1)}, u32[]{:S(2)}, u32[]{:S(2)}) collective-permute-start(f32[2,152,128]{2,1,0:T(8,128)S(1)} %get-tuple-element.34), channel_id=1, source_target_pairs={{16,0},{32,16},{48,32},{64,48},{80,64},{96,80},{112,96},{17,1},{33... | collective-permute-start | bytes 466952 | tf_op jit(solution)/shard_map/ppermute | solution.py:573
  99.7 3.6 %collective-permute-start.6 = (f32[16,136,128]{2,1,0:T(8,128)}, f32[16,136,128]{2,1,0:T(8,128)S(1)}, u32[]{:S(2)}, u32[]{:S(2)}) collective-permute-start(f32[16,136,128]{2,1,0:T(8,128)} %get-tuple-element.30), channel_id=1, source_target_pairs={{0,16},{16,32},{32,48},{48,64},{64,80},{80,96},{96,112},{1,17},{17... | collective-permute-start | bytes 3342344 | tf_op jit(solution)/shard_map/ppermute | solution.py:573
  103.4 1.9 %collective-permute-start.7 = (f32[16,136,128]{2,1,0:T(8,128)}, f32[16,136,128]{2,1,0:T(8,128)S(1)}, u32[]{:S(2)}, u32[]{:S(2)}) collective-permute-start(f32[16,136,128]{2,1,0:T(8,128)} %get-tuple-element.31), channel_id=1, source_target_pairs={{16,0},{32,16},{48,32},{64,48},{80,64},{96,80},{112,96},{17,1},{33... | collective-permute-start | bytes 3342344 | tf_op jit(solution)/shard_map/ppermute | solution.py:573
  105.3 0.0 collective-permute-done.8
  105.3 0.0 collective-permute-done.9
  105.4 0.4 collective-permute-start.10
  105.8 4.7 %collective-permute-start.11 = (f32[848,128]{1,0:T(8,128)S(1)}, f32[848,128]{1,0:T(8,128)S(1)}, u32[]{:S(2)}, u32[]{:S(2)}) collective-permute-start(f32[848,128]{1,0:T(8,128)S(1)} %pad_maximum_fusion.3), channel_id=1, source_target_pairs={{1,0},{2,1},{3,2},{4,3},{5,4},{6,5},{7,6},{8,7},{9,8},{10,9},{11,1... | collective-permute-start | bytes 1302536 | tf_op jit(solution)/shard_map/ppermute | solution.py:573
  110.5 8.6 %collective-permute-done.10.refs_6_ = f32[848,128]{1,0:T(8,128)S(1)} collective-permute-done((f32[848,128]{1,0:T(8,128)S(1)}, f32[848,128]{1,0:T(8,128)S(1)}, u32[]{:S(2)}, u32[]{:S(2)}) %collective-permute-start.10) | collective-permute-done | bytes 434208 | tf_op jit(solution)/shard_map/ppermute | solution.py:573
  119.2 0.1 collective-permute-done.11.refs_7_
  119.3 0.0 collective-permute-done.6.refs_4_
  119.3 1.1 collective-permute-done.7.refs_5_
  120.4 23.6 %shard_map.98 = (f32[64,128,128]{2,1,0:T(8,128)}, f32[64,128]{1,0:T(8,128)}) custom-call(s32[6,4,16]{2,1,0:T(4,128)S(1)} %bitcast.41, f32[128,12]{1,0:T(8,128)S(1)} %bitcast.35, s32[4,16]{1,0:T(4,128)S(1)} %copy-done.2, f32[64,128,128]{2,1,0:T(8,128)} %get-tuple-element.29.refs_3_, f32[16,136,128]{2,1,0:T(8,128)S(1)} %collective-permute-done.6.refs_4_, ...), custom_call_target="tpu_custom_call" | custom-call | tf_op jit(solution)/shard_map/pallas_call | solution.py:492
  (14 shorter events, 0.1 us)
Async XLA Ops:
  5.4 15.4 %copy-start.3 = (f32[4,136,128]{2,1,0:T(8,128)S(1)}, f32[4,136,128]{2,1,0:T(8,128)}, u32[]{:S(2)}) copy-start(f32[4,136,128]{2,1,0:T(8,128)} %get-tuple-element.23) | copy-start | bytes 835588
  5.4 12.2 %collective-permute-start = (f32[2,152,128]{2,1,0:T(8,128)}, f32[2,152,128]{2,1,0:T(8,128)S(1)}, u32[]{:S(2)}, u32[]{:S(2)}) collective-permute-start(f32[2,152,128]{2,1,0:T(8,128)} %get-tuple-element.21), channel_id=1, source_target_pairs={{0,16},{16,32},{32,48},{48,64},{64,80},{80,96},{96,112},{1,17},{17... | collective-permute-start | bytes 466952 | tf_op jit(solution)/shard_map/ppermute | solution.py:573
  10.0 7.6 %collective-permute-start.1 = (f32[2,152,128]{2,1,0:T(8,128)}, f32[2,152,128]{2,1,0:T(8,128)S(1)}, u32[]{:S(2)}, u32[]{:S(2)}) collective-permute-start(f32[2,152,128]{2,1,0:T(8,128)} %get-tuple-element.22), channel_id=1, source_target_pairs={{16,0},{32,16},{48,32},{64,48},{80,64},{96,80},{112,96},{17,1},{33... | collective-permute-start | bytes 466952 | tf_op jit(solution)/shard_map/ppermute | solution.py:573
  12.0 31.7 %collective-permute-start.2 = (f32[16,136,128]{2,1,0:T(8,128)}, f32[16,136,128]{2,1,0:T(8,128)S(1)}, u32[]{:S(2)}, u32[]{:S(2)}) collective-permute-start(f32[16,136,128]{2,1,0:T(8,128)} %get-tuple-element.25), channel_id=1, source_target_pairs={{0,16},{16,32},{32,48},{48,64},{64,80},{80,96},{96,112},{1,17},{17... | collective-permute-start | bytes 3342344 | tf_op jit(solution)/shard_map/ppermute | solution.py:573
  15.6 10.9 %copy-start.4 = (s32[256,1]{0,1:T(1,128)S(1)}, s32[256,1]{0,1:T(1,128)}, u32[]{:S(2)}) copy-start(s32[256,1]{0,1:T(1,128)} %param.14) | copy-start | bytes 3076
  15.6 11.0 %copy-start.6 = (f32[4,3]{1,0:T(4,128)S(1)}, f32[4,3]{1,0:T(4,128)}, u32[]{:S(2)}) copy-start(f32[4,3]{1,0:T(4,128)} %param.12) | copy-start | bytes 148
  15.6 28.0 %collective-permute-start.3 = (f32[16,136,128]{2,1,0:T(8,128)}, f32[16,136,128]{2,1,0:T(8,128)S(1)}, u32[]{:S(2)}, u32[]{:S(2)}) collective-permute-start(f32[16,136,128]{2,1,0:T(8,128)} %get-tuple-element.26), channel_id=1, source_target_pairs={{16,0},{32,16},{48,32},{64,48},{80,64},{96,80},{112,96},{17,1},{33... | collective-permute-start | bytes 3342344 | tf_op jit(solution)/shard_map/ppermute | solution.py:573
  17.6 16.3 %copy-start.7 = (s32[256]{0:T(256)S(1)}, s32[256]{0:T(256)}, u32[]{:S(2)}) copy-start(s32[256]{0:T(256)} %param.13) | copy-start | bytes 3076
  17.6 26.0 %copy-start = (s32[4,16,6]{1,0,2:T(4,128)S(1)}, s32[4,16,6]{1,0,2:T(4,128)}, u32[]{:S(2)}) copy-start(s32[4,16,6]{1,0,2:T(4,128)} %param.10) | copy-start | bytes 4612
  17.6 26.0 %copy-start.1 = (s32[4,16]{1,0:T(4,128)S(1)}, s32[4,16]{1,0:T(4,128)}, u32[]{:S(2)}) copy-start(s32[4,16]{1,0:T(4,128)} %refs_0_.1) | copy-start | bytes 772
  17.7 26.0 %copy-start.2 = (s32[4,16]{1,0:T(4,128)S(1)}, s32[4,16]{1,0:T(4,128)}, u32[]{:S(2)}) copy-start(s32[4,16]{1,0:T(4,128)} %refs_2_.1) | copy-start | bytes 772
  19.4 24.2 %collective-permute-start.4 = (f32[848,128]{1,0:T(8,128)}, f32[848,128]{1,0:T(8,128)S(1)}, u32[]{:S(2)}, u32[]{:S(2)}) collective-permute-start(f32[848,128]{1,0:T(8,128)} %pad_maximum_fusion), channel_id=1, source_target_pairs={{0,1},{1,2},{2,3},{3,4},{4,5},{5,6},{6,7},{7,8},{8,9},{9,10},{10,1... | collective-permute-start | bytes 1302536 | tf_op jit(solution)/shard_map/ppermute | solution.py:573
  21.5 22.1 %collective-permute-start.5 = (f32[848,128]{1,0:T(8,128)}, f32[848,128]{1,0:T(8,128)S(1)}, u32[]{:S(2)}, u32[]{:S(2)}) collective-permute-start(f32[848,128]{1,0:T(8,128)} %pad_maximum_fusion.1), channel_id=1, source_target_pairs={{1,0},{2,1},{3,2},{4,3},{5,4},{6,5},{7,6},{8,7},{9,8},{10,9},{11,1... | collective-permute-start | bytes 1302536 | tf_op jit(solution)/shard_map/ppermute | solution.py:573
  27.4 16.2 %all-to-all-start = ((f32[128,1,12]{2,1,0:T(1,128)}), f32[128,1,12]{2,1,0:T(1,128)S(1)}, u32[]{:S(2)}, u32[]{:S(2)}) async-start(f32[128,1,12]{2,1,0:T(1,128)} %broadcast_in_dim.8), calls=%async_computation | async-start | bytes 131072 | tf_op jit(solution)/shard_map/all_to_all | solution.py:599
  43.7 31.2 %copy-start.5 = (s32[512]{0:T(512)S(1)}, s32[512]{0:T(512)}, u32[]{:S(2)}) copy-start(s32[512]{0:T(512)} %param.15) | copy-start | bytes 6148
  70.5 15.8 %all-to-all-start.1 = ((f32[128,4,128]{2,1,0:T(4,128)}), f32[128,4,128]{2,1,0:T(4,128)S(1)}, u32[]{:S(2)}, u32[]{:S(2)}) async-start(f32[128,4,128]{2,1,0:T(4,128)} %bitcast.13), calls=%async_computation.1 | async-start | bytes 524288 | tf_op jit(solution)/shard_map/all_to_all | solution.py:611
  95.2 10.1 %collective-permute-start.8 = (f32[2,152,128]{2,1,0:T(8,128)S(1)}, f32[2,152,128]{2,1,0:T(8,128)S(1)}, u32[]{:S(2)}, u32[]{:S(2)}) collective-permute-start(f32[2,152,128]{2,1,0:T(8,128)S(1)} %get-tuple-element.33), channel_id=1, source_target_pairs={{0,16},{16,32},{32,48},{48,64},{64,80},{80,96},{96,112},{1,17},{17... | collective-permute-start | bytes 466952 | tf_op jit(solution)/shard_map/ppermute | solution.py:573
  97.8 7.5 %collective-permute-start.9 = (f32[2,152,128]{2,1,0:T(8,128)S(1)}, f32[2,152,128]{2,1,0:T(8,128)S(1)}, u32[]{:S(2)}, u32[]{:S(2)}) collective-permute-start(f32[2,152,128]{2,1,0:T(8,128)S(1)} %get-tuple-element.34), channel_id=1, source_target_pairs={{16,0},{32,16},{48,32},{64,48},{80,64},{96,80},{112,96},{17,1},{33... | collective-permute-start | bytes 466952 | tf_op jit(solution)/shard_map/ppermute | solution.py:573
  99.7 19.6 %collective-permute-start.6 = (f32[16,136,128]{2,1,0:T(8,128)}, f32[16,136,128]{2,1,0:T(8,128)S(1)}, u32[]{:S(2)}, u32[]{:S(2)}) collective-permute-start(f32[16,136,128]{2,1,0:T(8,128)} %get-tuple-element.30), channel_id=1, source_target_pairs={{0,16},{16,32},{32,48},{48,64},{64,80},{80,96},{96,112},{1,17},{17... | collective-permute-start | bytes 3342344 | tf_op jit(solution)/shard_map/ppermute | solution.py:573
  103.4 17.0 %collective-permute-start.7 = (f32[16,136,128]{2,1,0:T(8,128)}, f32[16,136,128]{2,1,0:T(8,128)S(1)}, u32[]{:S(2)}, u32[]{:S(2)}) collective-permute-start(f32[16,136,128]{2,1,0:T(8,128)} %get-tuple-element.31), channel_id=1, source_target_pairs={{16,0},{32,16},{48,32},{64,48},{80,64},{96,80},{112,96},{17,1},{33... | collective-permute-start | bytes 3342344 | tf_op jit(solution)/shard_map/ppermute | solution.py:573
  105.4 13.8 %collective-permute-start.10 = (f32[848,128]{1,0:T(8,128)S(1)}, f32[848,128]{1,0:T(8,128)S(1)}, u32[]{:S(2)}, u32[]{:S(2)}) collective-permute-start(f32[848,128]{1,0:T(8,128)S(1)} %pad_maximum_fusion.2), channel_id=1, source_target_pairs={{0,1},{1,2},{2,3},{3,4},{4,5},{5,6},{6,7},{7,8},{8,9},{9,10},{10,1... | collective-permute-start | bytes 1302536 | tf_op jit(solution)/shard_map/ppermute | solution.py:573
  105.8 13.5 %collective-permute-start.11 = (f32[848,128]{1,0:T(8,128)S(1)}, f32[848,128]{1,0:T(8,128)S(1)}, u32[]{:S(2)}, u32[]{:S(2)}) collective-permute-start(f32[848,128]{1,0:T(8,128)S(1)} %pad_maximum_fusion.3), channel_id=1, source_target_pairs={{1,0},{2,1},{3,2},{4,3},{5,4},{6,5},{7,6},{8,7},{9,8},{10,9},{11,1... | collective-permute-start | bytes 1302536 | tf_op jit(solution)/shard_map/ppermute | solution.py:573

commit v5 on v4

--- a/solution.py
+++ b/solution.py
@@ -154,45 +154,9 @@
     return center + up * (width - 3) + code - (width + 1)
 
 
-def step_kernel(rows, cols, masked, leaving, *refs):
-    if masked:
-        counts, refs = refs[0], refs[1:]
-    codes, segments, contact, cells_in, a_low, a_high, z_low, z_high = refs[:8]
-    if leaving:
-        slots, buffer_row, out_ref, sent, gathered = refs[8:13]
-        refs = refs[13:]
-    else:
-        out_ref, dens = refs[8:10]
-        refs = refs[10:]
-    geo, cells, out, side_t, side_s, feat, squares, row_t, row_s = refs[:9]
-    mass, root, rho, ratio, inverse, ring_codes, geo_came, cells_came, out_left, codes_came = refs[9:]
+def makers(rows, cols, row_t, row_s, side_t, side_s, mass, root, rho, squares):
     width = cols + 4
-    own = rows * cols
-    z_rows = rows * EDGE
-    per_device = segments.shape[1] // 3
-    sub8 = sub_iota((8, 128))
     row_mid, col_mid = (rows + 3) / 2.0, (cols + 3) / 2.0
-
-    geo_copy = pltpu.make_async_copy(cells_in.at[:, 0:8, :], geo, geo_came)
-    geo_copy.start()
-    code_copies = []
-
-    def bring_codes(source, first, n):
-        code_copies.append(pltpu.make_async_copy(source, ring_codes.at[pl.ds(first, n), :], codes_came.at[len(code_copies)]))
-
-    bring_codes(a_low.at[:, EDGE - 1, :], 0, cols)
-    bring_codes(a_high.at[:, EDGE - 1, :], cols, cols)
-    for ref, first in ((z_low, 2 * cols), (z_high, 2 * cols + rows + 2)):
-        for r in range(rows):
-            bring_codes(ref.at[pl.ds(r * EDGE + EDGE - 1, 1), :], first + r, 1)
-        for n in range(2):
-            bring_codes(ref.at[pl.ds(z_rows + n * CORNER + EDGE - 1, 1), :], first + rows + n, 1)
-    cells_piece = pieces(cells_in, cells, cells_came, 8)
-    out_piece = pieces(out, out_ref, out_left, 8)
-    for copy in code_copies:
-        copy.start()
-    for i in range(own // 8):
-        cells_piece(i).start()
 
     def geometry(flat, row, stride, n, index, apart, r, c, center, limit=None):
         def field(k):
@@ -230,7 +194,60 @@
     def sub(n):
         return sub_iota((n, 128)).astype(F32)
 
+    quarter = lax.broadcasted_iota(I32, (128, 128), 1) // ROWS_K
+    only = [jnp.where(quarter == k, 1.0, 0.0).astype(BF16) for k in range(4)]
+
+    def block32(ref, index):
+        return ref[pl.ds(pl.multiple_of(index * ROWS_K, ROWS_K), ROWS_K), :]
+
+    def turn(indices):
+        t = jnp.transpose(jnp.concatenate([block32(row_t, index) for index in indices], axis=0)).astype(BF16)
+        for k, index in enumerate(indices):
+            side_t[index] = t * only[k]
+            side_s[index] = block32(row_s, index).astype(BF16)
+
+    def density(center, partners, n):
+        rhs = jnp.concatenate([side_s[center]] * 4, axis=0)
+        total = jnp.zeros((8, 128), F32)
+        for j, partner in enumerate(partners):
+            y = jnp.maximum(jnp.dot(side_t[partner], rhs, preferred_element_type=F32), 0.0)
+            square = y * y
+            total = total + jnp.sum((square * y).reshape(16, 8, 128), axis=0)
+            if n is not None:
+                squares[n, j * 128 : (j + 1) * 128, :] = square.astype(BF16)
+        rho[pl.ds(center, 1), :] = jnp.sum(total, axis=0, keepdims=True)
+
+    return geometry, sub, turn, density
+
+
+def own_copies(rows, cols, pairs, semaphore):
+    width = cols + 4
+    copies = []
+    for source, target in pairs:
+        for r in range(rows):
+            part = pl.ds((r + 2) * width + 2, cols)
+            copies.append(pltpu.make_async_copy(source.at[part], target.at[part], semaphore.at[len(copies)]))
+    return copies
+
+
+def inner_copies(rows, cols, source, target, semaphore):
+    parts = [pl.ds(r * cols + 1, cols - 2) for r in range(1, rows - 1)]
+    return [pltpu.make_async_copy(source.at[part], target.at[part], semaphore.at[k]) for k, part in enumerate(parts)]
+
+
+def own_kernel(rows, cols, masked, *refs):
+    if masked:
+        counts, refs = refs[0], refs[1:]
+    codes, cells_in, side_t_out, side_s_out, squares_out, mass, root, rho = refs[:8]
+    geo, side_t, side_s, squares, row_t, row_s, geo_came, sides_left, squares_left = refs[8:]
+    width = cols + 4
+    own = rows * cols
     per = 8
+    geometry, sub, turn, density = makers(rows, cols, row_t, row_s, side_t, side_s, mass, root, rho, squares)
+    geo_copy = pltpu.make_async_copy(cells_in.at[:, 0:8, :], geo, geo_came)
+    geo_copy.start()
+    for ref in (mass, root, rho):
+        ref[...] = jnp.ones_like(ref)
     geo_copy.wait()
     geo_flat = geo.reshape(own * 8, 128)
 
@@ -245,6 +262,125 @@
         geometry(geo_flat, first * 8, 8, per, r * width + c, 1, r.astype(F32), c.astype(F32) + sub(per), True, limit)
 
     loop(own // per, local_geo)
+    def turn_own(i):
+        for k in range(cols // 4):
+            index = (i + 2) * width + 2 + 4 * k
+            turn([index, index + 1, index + 2, index + 3])
+
+    loop(rows, turn_own)
+
+    sides = own_copies(rows, cols, ((side_t, side_t_out), (side_s, side_s_out)), sides_left)
+    for copy in sides:
+        copy.start()
+
+    def inner_density(i):
+        r = i + 1
+        for k in range(1, cols - 1):
+            center = (r + 2) * width + k + 2
+            density(center, [linked(center, codes[j, r, k], width) for j in range(6)], r * cols + k)
+
+    loop(rows - 2, inner_density)
+    inner = inner_copies(rows, cols, squares, squares_out, squares_left)
+    for copy in inner:
+        copy.start()
+    for copy in sides + inner:
+        copy.wait()
+
+
+def own_call(rows, cols, counts, codes, cells):
+    own = rows * cols
+    patch = (rows + 4) * (cols + 4)
+    scalars = [] if counts is None else [counts]
+    field = jax.ShapeDtypeStruct((patch, 128), F32)
+    return pl.pallas_call(
+        functools.partial(own_kernel, rows, cols, counts is not None),
+        out_shape=(jax.ShapeDtypeStruct((patch, 128, 128), BF16), jax.ShapeDtypeStruct((patch, 32, 128), BF16), jax.ShapeDtypeStruct((own, 768, 128), BF16), field, field, field),
+        in_specs=[smem_spec()] * (len(scalars) + 1) + [any_spec()],
+        out_specs=(any_spec(),) * 3 + (vmem_spec(),) * 3,
+        scratch_shapes=[
+            pltpu.VMEM((own, 8, 128), F32),
+            pltpu.VMEM((patch, 128, 128), BF16),
+            pltpu.VMEM((patch, 32, 128), BF16),
+            pltpu.VMEM((own, 768, 128), BF16),
+            pltpu.VMEM((patch * ROWS_K, 128), F32),
+            pltpu.VMEM((patch * ROWS_K, 128), F32),
+            pltpu.SemaphoreType.DMA(()),
+            pltpu.SemaphoreType.DMA((2 * rows,)),
+            pltpu.SemaphoreType.DMA((rows - 2,)),
+        ],
+        compiler_params=pltpu.CompilerParams(vmem_limit_bytes=47 * MIB),
+        cost_estimate=pl.CostEstimate(flops=5 * 10**9, bytes_accessed=16 * MIB, transcendentals=0),
+    )(*scalars, codes, cells)
+
+
+def step_kernel(rows, cols, masked, leaving, ahead, *refs):
+    if masked:
+        counts, refs = refs[0], refs[1:]
+    codes, segments, contact, cells_in, a_low, a_high, z_low, z_high = refs[:8]
+    if ahead:
+        side_t_in, side_s_in, squares_in, mass_in, root_in, rho_in = refs[8:14]
+        refs = refs[:8] + refs[14:]
+    if leaving:
+        slots, buffer_row, out_ref, sent, gathered = refs[8:13]
+        refs = refs[13:]
+    else:
+        out_ref, dens = refs[8:10]
+        refs = refs[10:]
+    geo, cells, out, side_t, side_s, feat, squares, row_t, row_s = refs[:9]
+    mass, root, rho, ratio, inverse, ring_codes, geo_came, sides_came, squares_came, cells_came, out_left, codes_came = refs[9:]
+    width = cols + 4
+    own = rows * cols
+    z_rows = rows * EDGE
+    per_device = segments.shape[1] // 3
+    sub8 = sub_iota((8, 128))
+    row_mid, col_mid = (rows + 3) / 2.0, (cols + 3) / 2.0
+
+    if not ahead:
+        geo_copy = pltpu.make_async_copy(cells_in.at[:, 0:8, :], geo, geo_came)
+        geo_copy.start()
+    code_copies = []
+
+    def bring_codes(source, first, n):
+        code_copies.append(pltpu.make_async_copy(source, ring_codes.at[pl.ds(first, n), :], codes_came.at[len(code_copies)]))
+
+    bring_codes(a_low.at[:, EDGE - 1, :], 0, cols)
+    bring_codes(a_high.at[:, EDGE - 1, :], cols, cols)
+    for ref, first in ((z_low, 2 * cols), (z_high, 2 * cols + rows + 2)):
+        for r in range(rows):
+            bring_codes(ref.at[pl.ds(r * EDGE + EDGE - 1, 1), :], first + r, 1)
+        for n in range(2):
+            bring_codes(ref.at[pl.ds(z_rows + n * CORNER + EDGE - 1, 1), :], first + rows + n, 1)
+    cells_piece = pieces(cells_in, cells, cells_came, 8)
+    out_piece = pieces(out, out_ref, out_left, 8)
+    for copy in code_copies:
+        copy.start()
+    for i in range(own // 8):
+        cells_piece(i).start()
+
+    geometry, sub, turn, density = makers(rows, cols, row_t, row_s, side_t, side_s, mass, root, rho, squares)
+    per = 8
+    if ahead:
+        for copy in own_copies(rows, cols, ((side_t_in, side_t), (side_s_in, side_s)), sides_came) + inner_copies(rows, cols, squares_in, squares, squares_came):
+            copy.start()
+        for source, target in ((mass_in, mass), (root_in, root), (rho_in, rho)):
+            target[...] = source[...]
+    else:
+        rho[...] = jnp.ones_like(rho)
+        geo_copy.wait()
+    geo_flat = geo.reshape(own * 8, 128)
+
+    def local_geo(i):
+        first = i * per
+        r, c = first // cols + 2, first % cols + 2
+        limit = None
+        if masked:
+            limit = jnp.zeros((per, 128), I32)
+            for k in range(per):
+                limit = jnp.where(sub_iota((per, 128)) == k, counts[first // cols, first % cols + k], limit)
+        geometry(geo_flat, first * 8, 8, per, r * width + c, 1, r.astype(F32), c.astype(F32) + sub(per), True, limit)
+
+    if not ahead:
+        loop(own // per, local_geo)
     for ref, first, second in ((a_low, 1, 0), (a_high, rows + 2, rows + 3)):
         flat = ref.reshape(cols * EDGE, 128)
         for k in range(0, cols, per):
@@ -264,24 +400,13 @@
         geometry(ref, z_rows + 128, CORNER, 2, near, apart, r, float(near), False)
         geometry(ref, z_rows + 144, CORNER, 2, far, apart, r, float(far), False)
 
-    quarter = lax.broadcasted_iota(I32, (128, 128), 1) // ROWS_K
-    only = [jnp.where(quarter == k, 1.0, 0.0).astype(BF16) for k in range(4)]
-
-    def block32(ref, index):
-        return ref[pl.ds(pl.multiple_of(index * ROWS_K, ROWS_K), ROWS_K), :]
-
-    def turn(indices):
-        t = jnp.transpose(jnp.concatenate([block32(row_t, index) for index in indices], axis=0)).astype(BF16)
-        for k, index in enumerate(indices):
-            side_t[index] = t * only[k]
-            side_s[index] = block32(row_s, index).astype(BF16)
-
     def turn_own(i):
         for k in range(cols // 4):
             index = (i + 2) * width + 2 + 4 * k
             turn([index, index + 1, index + 2, index + 3])
 
-    loop(rows, turn_own)
+    if not ahead:
+        loop(rows, turn_own)
 
     def turn_ring(i):
         for r in (i, i + rows + 2):
@@ -293,27 +418,23 @@
 
     loop(2, turn_ring)
 
-    def density(center, partners, n):
-        rhs = jnp.concatenate([side_s[center]] * 4, axis=0)
-        total = jnp.zeros((8, 128), F32)
-        for j, partner in enumerate(partners):
-            y = jnp.maximum(jnp.dot(side_t[partner], rhs, preferred_element_type=F32), 0.0)
-            square = y * y
-            total = total + jnp.sum((square * y).reshape(16, 8, 128), axis=0)
-            if n is not None:
-                squares[n, j * 128 : (j + 1) * 128, :] = square.astype(BF16)
-        rho[pl.ds(center, 1), :] = jnp.sum(total, axis=0, keepdims=True)
-
-    rho[...] = jnp.ones_like(rho)
-
-    def own_density(i):
-        for k in range(16):
-            n = i * 16 + k
-            r, c = n // cols, n % cols
-            center = (r + 2) * width + c + 2
-            density(center, [linked(center, codes[j, r, c], width) for j in range(6)], n)
-
-    loop(own // 16, own_density)
+    def own_cell(r, c):
+        center = (r + 2) * width + c + 2
+        density(center, [linked(center, codes[j, r, c], width) for j in range(6)], r * cols + c)
+
+    def whole_row(r):
+        for c in range(cols):
+            own_cell(r, c)
+
+    if ahead:
+        for copy in own_copies(rows, cols, ((side_t_in, side_t), (side_s_in, side_s)), sides_came):
+            copy.wait()
+        loop(2, lambda i: whole_row(i * (rows - 1)))
+        for r in range(1, rows - 1):
+            own_cell(r, 0)
+            own_cell(r, cols - 1)
+    else:
+        loop(rows, whole_row)
     for copy in code_copies:
         copy.wait()
 
@@ -375,6 +496,9 @@
             n = i * 8 + k
             features(in_cell(cells, n), n // cols + 2, n % cols + 2)
 
+    if ahead:
+        for copy in inner_copies(rows, cols, squares_in, squares, squares_came):
+            copy.wait()
     loop(own // 8, local_feat)
 
     def a_feat(i):
@@ -476,7 +600,7 @@
     return pl.BlockSpec(memory_space=pltpu.VMEM)
 
 
-def step_call(rows, cols, counts, codes, segments, contact, cells, halo, leave=None):
+def step_call(rows, cols, counts, codes, segments, contact, cells, halo, ahead, leave=None):
     own = rows * cols
     patch = (rows + 4) * (cols + 4)
     ring = 2 * cols + 2 * (rows + 2)
@@ -490,9 +614,9 @@
         outs = (new, jax.ShapeDtypeStruct((own, 128), F32))
     scalars = [] if counts is None else [counts]
     return pl.pallas_call(
-        functools.partial(step_kernel, rows, cols, counts is not None, bool(leave)),
+        functools.partial(step_kernel, rows, cols, counts is not None, bool(leave), ahead is not None),
         out_shape=outs,
-        in_specs=[smem_spec()] * (len(scalars) + 3) + [any_spec()] + [vmem_spec()] * (4 + len(extra)),
+        in_specs=[smem_spec()] * (len(scalars) + 3) + [any_spec()] + [vmem_spec()] * 4 + ([] if ahead is None else [any_spec()] * 3 + [vmem_spec()] * 3) + [vmem_spec()] * len(extra),
         out_specs=(any_spec(), vmem_spec()),
         scratch_shapes=first
         + [
@@ -510,12 +634,14 @@
         + [
             pltpu.SMEM((ring, 128), F32),
             pltpu.SemaphoreType.DMA(()),
+            pltpu.SemaphoreType.DMA((2 * rows,)),
+            pltpu.SemaphoreType.DMA((rows - 2,)),
             pltpu.SemaphoreType.DMA((own // 8,)),
             pltpu.SemaphoreType.DMA((own // 8,)),
             pltpu.SemaphoreType.DMA((2 + 2 * (rows + 2),)),
         ],
         compiler_params=pltpu.CompilerParams(vmem_limit_bytes=47 * MIB),
-    )(*scalars, codes, segments, contact, cells, *halo, *extra)
+    )(*scalars, codes, segments, contact, cells, *halo, *(ahead or ()), *extra)
 
 
 def insert_kernel(rows, cols, codes, state_in, incoming, slots, out_ref, *refs):
@@ -607,10 +733,12 @@
     buffer_row = (dest * capacity + order).reshape(1, leaving)
 
     leave = (leaving_slot.reshape(-1, 1), buffer_row, ranks * capacity)
-    state, outgoing = step_call(rows, cols, counts, pair_codes, told, contact, state, halo, leave)
+    state, outgoing = step_call(rows, cols, counts, pair_codes, told, contact, state, halo, None, leave)
     incoming = lax.all_to_all(outgoing.reshape(ranks, capacity, fields), AXES, 0, 0, tiled=True)
     state, *strips = insert(rows, cols, pair_codes, state, incoming.reshape(-1, fields), arrival_slot.reshape(-1, 1))
-    state, density = step_call(rows, cols, None, pair_codes, told, contact, state, exchange(strips)[0])
+    halo, sides = exchange(strips)
+    ahead = own_call(rows, cols, None, pair_codes, lax.optimization_barrier((state, sides))[0])
+    state, density = step_call(rows, cols, None, pair_codes, told, contact, state, halo, ahead)
     return state.reshape(particles.shape), density.reshape(rows, cols, block)
 
 

time: 145 us -> 140 us (0.966)
  waiting for transfers between devices: 30.8 us -> 21 us
  Pallas kernels: 64 us -> 67.3 us
  local copies, waits for them, and re-layouts: 1.12 us -> 3.31 us
    ppermute x6, waiting for transfers between devices: 8.66 us -> 0.02 us  [swap(): lax.ppermute(up, axis, pairs)]
    pallas_call x0 -> x1, Pallas kernels: none -> 7.94 us  [own_call(): pl.pallas_call(functools.partial(own_kernel, rows, cols, counts is not No...]
    pallas_call x2, Pallas kernels: 50.4 us -> 45.8 us  [step_call(): pl.pallas_call(functools.partial(step_kernel, rows, cols, counts is not N...]
    unnamed x16 -> x18, local copies, waits for them, and re-layouts: 0.05 us -> 2.24 us
  transfers between devices with their start and end apart: 14 -> 14, of which waited for: 5 -> 2; matrix products, arithmetic and copies ran while one was open for 3% -> 3% of each run, Pallas kernels for 0% -> 6%
where the time goes in v5:
time: 140 us
  Pallas kernels  67.3 us (48%)
  starting transfers between devices  44.2 us (32%)
  waiting for transfers between devices  21 us (15%)
  local copies, waits for them, and re-layouts  3.31 us (2%)
  other arithmetic  2.81 us (2%)
    pallas_call x2, Pallas kernels, step_call(): pl.pallas_call(functools.partial(step_kernel, rows, cols, counts is not N...  45.8 us
    ppermute x6, starting transfers between devices, swap(): lax.ppermute(down, axis, [(j, i) for i, j in pairs])  17.3 us
    ppermute x6, starting transfers between devices, swap(): lax.ppermute(up, axis, pairs)  16.3 us
    all_to_all x1, waiting for transfers between devices, local(): lax.all_to_all(outgoing.reshape(ranks, capacity, fields), AXES, 0, 0, til...  11.4 us
    all_to_all x1, waiting for transfers between devices, local(): told = lax.all_to_all(told, AXES, 0, 0, tiled=True)  9.6 us
    pallas_call x1, Pallas kernels, insert(): pl.pallas_call(functools.partial(insert_kernel, rows, cols), out_shape=(j...  8.81 us
    pallas_call x1, Pallas kernels, own_call(): pl.pallas_call(functools.partial(own_kernel, rows, cols, counts is not No...  7.94 us
    all_to_all x1, starting transfers between devices, local(): told = lax.all_to_all(told, AXES, 0, 0, tiled=True)  6.44 us
  transfers between devices with their start and end apart: 14, of which 2 were waited for; matrix products, arithmetic and copies ran while one was open for 3% of the time, Pallas kernels for 6%

profile of v5, /device:TPU:1, one launch (start us, length us, event | category | flops | bytes accessed | tf_op | source)
XLA Modules:
  0.0 139.8 jit_solution(5887370414989575683)
XLA Ops:
  0.6 4.7 %shard_map.95 = (f32[2,152,128]{2,1,0:T(8,128)}, f32[2,152,128]{2,1,0:T(8,128)}, f32[16,136,128]{2,1,0:T(8,128)}, f32[16,136,128]{2,1,0:T(8,128)}, f32[4,136,128]{2,1,0:T(8,128)}, /*index=5*/f32[4,136,128]{2,1,0:T(8,128)}) custom-call(s32[4,16]{1,0:T(4,128)} %refs_0_.1, s32[6,4,16]{2,1,0:T(4,128)} %bitcast.38, f32[64,128,128]{2,1,0:T(8,128)} %bitcast.43), custom_call_target="tpu_custom_call" | custom-call | tf_op jit(solution)/shard_map/pallas_call | solution.py:142
  5.4 4.6 %collective-permute-start = (f32[2,152,128]{2,1,0:T(8,128)}, f32[2,152,128]{2,1,0:T(8,128)S(1)}, u32[]{:S(2)}, u32[]{:S(2)}) collective-permute-start(f32[2,152,128]{2,1,0:T(8,128)} %get-tuple-element.28), channel_id=1, source_target_pairs={{0,16},{16,32},{32,48},{48,64},{64,80},{80,96},{96,112},{1,17},{17... | collective-permute-start | bytes 466952 | tf_op jit(solution)/shard_map/ppermute | solution.py:699
  10.0 1.9 %collective-permute-start.1 = (f32[2,152,128]{2,1,0:T(8,128)}, f32[2,152,128]{2,1,0:T(8,128)S(1)}, u32[]{:S(2)}, u32[]{:S(2)}) collective-permute-start(f32[2,152,128]{2,1,0:T(8,128)} %get-tuple-element.29), channel_id=1, source_target_pairs={{16,0},{32,16},{48,32},{64,48},{80,64},{96,80},{112,96},{17,1},{33... | collective-permute-start | bytes 466952 | tf_op jit(solution)/shard_map/ppermute | solution.py:699
  12.0 3.6 %collective-permute-start.2 = (f32[16,136,128]{2,1,0:T(8,128)}, f32[16,136,128]{2,1,0:T(8,128)S(1)}, u32[]{:S(2)}, u32[]{:S(2)}) collective-permute-start(f32[16,136,128]{2,1,0:T(8,128)} %get-tuple-element.32), channel_id=1, source_target_pairs={{0,16},{16,32},{32,48},{48,64},{64,80},{80,96},{96,112},{1,17},{17... | collective-permute-start | bytes 3342344 | tf_op jit(solution)/shard_map/ppermute | solution.py:699
  15.6 0.0 copy-start.5
  15.6 0.0 copy-start.7
  15.6 1.9 %collective-permute-start.3 = (f32[16,136,128]{2,1,0:T(8,128)}, f32[16,136,128]{2,1,0:T(8,128)S(1)}, u32[]{:S(2)}, u32[]{:S(2)}) collective-permute-start(f32[16,136,128]{2,1,0:T(8,128)} %get-tuple-element.33), channel_id=1, source_target_pairs={{16,0},{32,16},{48,32},{64,48},{80,64},{96,80},{112,96},{17,1},{33... | collective-permute-start | bytes 3342344 | tf_op jit(solution)/shard_map/ppermute | solution.py:699
  17.6 0.0 collective-permute-done
  17.6 0.0 copy-start.8
  17.6 0.0 collective-permute-done.1
  17.6 0.0 copy-start.1
  17.7 0.0 copy-start.2
  17.7 0.0 copy-start.3
  17.7 1.8 %pad_maximum_fusion = f32[848,128]{1,0:T(8,128)} fusion(f32[152,128]{1,0:T(8,128)S(1)} %get-tuple-element.59, f32[152,128]{1,0:T(8,128)S(1)} %get-tuple-element.57, f32[544,128]{1,0:T(8,128)} %bitcast.46), kind=kLoop, calls=%fused_computation | loop fusion | flops 217088 | bytes 868352 | tf_op jit(solution)/shard_map/concatenate | solution.py:708
  19.4 1.3 collective-permute-start.4
  20.7 0.8 pad_maximum_fusion.1
  21.5 4.9 %collective-permute-start.5 = (f32[848,128]{1,0:T(8,128)}, f32[848,128]{1,0:T(8,128)S(1)}, u32[]{:S(2)}, u32[]{:S(2)}) collective-permute-start(f32[848,128]{1,0:T(8,128)} %pad_maximum_fusion.1), channel_id=1, source_target_pairs={{1,0},{2,1},{3,2},{4,3},{5,4},{6,5},{7,6},{8,7},{9,8},{10,9},{11,1... | collective-permute-start | bytes 1302536 | tf_op jit(solution)/shard_map/ppermute | solution.py:699
  26.5 0.2 convert_reduce_fusion
  26.7 0.1 broadcast_in_dim.7
  26.7 0.7 broadcast_in_dim.8
  27.4 6.4 %all-to-all-start = ((f32[128,1,12]{2,1,0:T(1,128)}), f32[128,1,12]{2,1,0:T(1,128)S(1)}, u32[]{:S(2)}, u32[]{:S(2)}) async-start(f32[128,1,12]{2,1,0:T(1,128)} %broadcast_in_dim.8), calls=%async_computation | async-start | bytes 131072 | tf_op jit(solution)/shard_map/all_to_all | solution.py:725
  33.9 0.1 copy.14.refs_9_
  34.0 9.6 %all-to-all-done = f32[128,1,12]{2,1,0:T(1,128)S(1)} async-done(((f32[128,1,12]{2,1,0:T(1,128)}), f32[128,1,12]{2,1,0:T(1,128)S(1)}, u32[]{:S(2)}, u32[]{:S(2)}) %all-to-all-start) | async-done | bytes 6176 | tf_op jit(solution)/shard_map/all_to_all | solution.py:725
  43.6 0.0 collective-permute-done.4.refs_7_
  43.6 0.0 collective-permute-done.5.refs_8_
  43.6 0.0 collective-permute-done.2.refs_5_
  43.6 0.0 collective-permute-done.3.refs_6_
  43.7 0.0 copy-start.6
  43.7 27.0 %shard_map.96 = (f32[64,128,128]{2,1,0:T(8,128)}, f32[512,128]{1,0:T(8,128)}) custom-call(s32[4,16]{1,0:T(4,128)S(1)} %copy-done.2, s32[6,4,16]{2,1,0:T(4,128)S(1)} %bitcast.39, f32[128,12]{1,0:T(8,128)S(1)} %bitcast.34, s32[4,16]{1,0:T(4,128)S(1)} %copy-done.3, f32[64,128,128]{2,1,0:T(8,128)} %bitcast.44, ...), custom_call_target="tpu_custom_call" | custom-call | tf_op jit(solution)/shard_map/pallas_call | solution.py:616
  70.7 4.3 %all-to-all-start.1 = ((f32[128,4,128]{2,1,0:T(4,128)}), f32[128,4,128]{2,1,0:T(4,128)S(1)}, u32[]{:S(2)}, u32[]{:S(2)}) async-start(f32[128,4,128]{2,1,0:T(4,128)} %bitcast.13), calls=%async_computation.1 | async-start | bytes 524288 | tf_op jit(solution)/shard_map/all_to_all | solution.py:737
  75.0 0.1 copy.15.slots
  75.2 11.4 %all-to-all-done.1 = f32[128,4,128]{2,1,0:T(4,128)S(1)} async-done(((f32[128,4,128]{2,1,0:T(4,128)}), f32[128,4,128]{2,1,0:T(4,128)S(1)}, u32[]{:S(2)}, u32[]{:S(2)}) %all-to-all-start.1) | async-done | bytes 262176 | tf_op jit(solution)/shard_map/all_to_all | solution.py:737
  86.6 8.8 %shard_map.97 = (f32[64,128,128]{2,1,0:T(8,128)}, f32[2,152,128]{2,1,0:T(8,128)S(1)}, f32[2,152,128]{2,1,0:T(8,128)S(1)}, f32[16,136,128]{2,1,0:T(8,128)}, f32[1...) custom-call(s32[6,4,16]{2,1,0:T(4,128)S(1)} %bitcast.40, ...), custom_call_target="tpu_custom_call" | custom-call | tf_op jit(solution)/shard_map/pallas_call | solution.py:686
  95.4 2.6 %collective-permute-start.8 = (f32[2,152,128]{2,1,0:T(8,128)S(1)}, f32[2,152,128]{2,1,0:T(8,128)S(1)}, u32[]{:S(2)}, u32[]{:S(2)}) collective-permute-start(f32[2,152,128]{2,1,0:T(8,128)S(1)} %get-tuple-element.40), channel_id=1, source_target_pairs={{0,16},{16,32},{32,48},{48,64},{64,80},{80,96},{96,112},{1,17},{17... | collective-permute-start | bytes 466952 | tf_op jit(solution)/shard_map/ppermute | solution.py:699
  98.0 1.9 %collective-permute-start.9 = (f32[2,152,128]{2,1,0:T(8,128)S(1)}, f32[2,152,128]{2,1,0:T(8,128)S(1)}, u32[]{:S(2)}, u32[]{:S(2)}) collective-permute-start(f32[2,152,128]{2,1,0:T(8,128)S(1)} %get-tuple-element.41), channel_id=1, source_target_pairs={{16,0},{32,16},{48,32},{64,48},{80,64},{96,80},{112,96},{17,1},{33... | collective-permute-start | bytes 466952 | tf_op jit(solution)/shard_map/ppermute | solution.py:699
  99.9 3.6 %collective-permute-start.6 = (f32[16,136,128]{2,1,0:T(8,128)}, f32[16,136,128]{2,1,0:T(8,128)S(1)}, u32[]{:S(2)}, u32[]{:S(2)}) collective-permute-start(f32[16,136,128]{2,1,0:T(8,128)} %get-tuple-element.37), channel_id=1, source_target_pairs={{0,16},{16,32},{32,48},{48,64},{64,80},{80,96},{96,112},{1,17},{17... | collective-permute-start | bytes 3342344 | tf_op jit(solution)/shard_map/ppermute | solution.py:699
  103.6 1.9 %collective-permute-start.7 = (f32[16,136,128]{2,1,0:T(8,128)}, f32[16,136,128]{2,1,0:T(8,128)S(1)}, u32[]{:S(2)}, u32[]{:S(2)}) collective-permute-start(f32[16,136,128]{2,1,0:T(8,128)} %get-tuple-element.38), channel_id=1, source_target_pairs={{16,0},{32,16},{48,32},{64,48},{80,64},{96,80},{112,96},{17,1},{33... | collective-permute-start | bytes 3342344 | tf_op jit(solution)/shard_map/ppermute | solution.py:699
  105.5 0.0 collective-permute-done.8
  105.5 0.0 collective-permute-done.9
  105.6 0.4 collective-permute-start.10
  106.1 4.7 %collective-permute-start.11 = (f32[848,128]{1,0:T(8,128)S(1)}, f32[848,128]{1,0:T(8,128)S(1)}, u32[]{:S(2)}, u32[]{:S(2)}) collective-permute-start(f32[848,128]{1,0:T(8,128)S(1)} %pad_maximum_fusion.3), channel_id=1, source_target_pairs={{1,0},{2,1},{3,2},{4,3},{5,4},{6,5},{7,6},{8,7},{9,8},{10,9},{11,1... | collective-permute-start | bytes 1302536 | tf_op jit(solution)/shard_map/ppermute | solution.py:699
  110.7 2.2 %copy-done = f32[64,128,128]{2,1,0:T(8,128)S(1)} copy-done((f32[64,128,128]{2,1,0:T(8,128)S(1)}, f32[64,128,128]{2,1,0:T(8,128)}, u32[]{:S(2)}) %copy-start) | copy-done | bytes 4194328
  112.9 7.9 %shard_map.98 = (bf16[160,128,128]{2,1,0:T(8,128)(2,1)}, bf16[160,32,128]{2,1,0:T(8,128)(2,1)S(1)}, bf16[64,768,128]{2,1,0:T(8,128)(2,1)}, f32[160,128]{1,0:T(8,...) custom-call(s32[6,4,16]{2,1,0:T(4,128)S(1)} %bitcast.41, f32[64,128,128]{2,1,0:T(8,128)S(1)} %copy-done), custom_call_target="tpu_custom_call" | custom-call | flops 5000000000 | bytes 16777216 | tf_op jit(solution)/shard_map/pallas_call | solution.py:295
  120.9 0.0 collective-permute-done.10.refs_6_
  120.9 0.0 collective-permute-done.11.refs_7_
  120.9 0.0 collective-permute-done.6.refs_4_
  120.9 0.0 collective-permute-done.7.refs_5_
  120.9 18.7 %shard_map.99 = (f32[64,128,128]{2,1,0:T(8,128)}, f32[64,128]{1,0:T(8,128)}) custom-call(s32[6,4,16]{2,1,0:T(4,128)S(1)} %bitcast.42, f32[128,12]{1,0:T(8,128)S(1)} %bitcast.35, s32[4,16]{1,0:T(4,128)S(1)} %copy-done.3, f32[64,128,128]{2,1,0:T(8,128)} %get-tuple-element.43.refs_1_.refs_3_, f32[16,136,128]{2,1,0:T(8,128)S(1)} %collective-permute-done.6.refs_4_, ...), custom_call_target="tpu_custom_call" | custom-call | tf_op jit(solution)/shard_map/pallas_call | solution.py:616
  (17 shorter events, 0.1 us)
Async XLA Ops:
  5.4 15.4 %copy-start.4 = (f32[4,136,128]{2,1,0:T(8,128)S(1)}, f32[4,136,128]{2,1,0:T(8,128)}, u32[]{:S(2)}) copy-start(f32[4,136,128]{2,1,0:T(8,128)} %get-tuple-element.30) | copy-start | bytes 835588
  5.4 12.2 %collective-permute-start = (f32[2,152,128]{2,1,0:T(8,128)}, f32[2,152,128]{2,1,0:T(8,128)S(1)}, u32[]{:S(2)}, u32[]{:S(2)}) collective-permute-start(f32[2,152,128]{2,1,0:T(8,128)} %get-tuple-element.28), channel_id=1, source_target_pairs={{0,16},{16,32},{32,48},{48,64},{64,80},{80,96},{96,112},{1,17},{17... | collective-permute-start | bytes 466952 | tf_op jit(solution)/shard_map/ppermute | solution.py:699
  10.0 7.6 %collective-permute-start.1 = (f32[2,152,128]{2,1,0:T(8,128)}, f32[2,152,128]{2,1,0:T(8,128)S(1)}, u32[]{:S(2)}, u32[]{:S(2)}) collective-permute-start(f32[2,152,128]{2,1,0:T(8,128)} %get-tuple-element.29), channel_id=1, source_target_pairs={{16,0},{32,16},{48,32},{64,48},{80,64},{96,80},{112,96},{17,1},{33... | collective-permute-start | bytes 466952 | tf_op jit(solution)/shard_map/ppermute | solution.py:699
  12.0 31.7 %collective-permute-start.2 = (f32[16,136,128]{2,1,0:T(8,128)}, f32[16,136,128]{2,1,0:T(8,128)S(1)}, u32[]{:S(2)}, u32[]{:S(2)}) collective-permute-start(f32[16,136,128]{2,1,0:T(8,128)} %get-tuple-element.32), channel_id=1, source_target_pairs={{0,16},{16,32},{32,48},{48,64},{64,80},{80,96},{96,112},{1,17},{17... | collective-permute-start | bytes 3342344 | tf_op jit(solution)/shard_map/ppermute | solution.py:699
  15.6 10.9 %copy-start.5 = (s32[256,1]{0,1:T(1,128)S(1)}, s32[256,1]{0,1:T(1,128)}, u32[]{:S(2)}) copy-start(s32[256,1]{0,1:T(1,128)} %param.14) | copy-start | bytes 3076
  15.6 11.0 %copy-start.7 = (f32[4,3]{1,0:T(4,128)S(1)}, f32[4,3]{1,0:T(4,128)}, u32[]{:S(2)}) copy-start(f32[4,3]{1,0:T(4,128)} %param.12) | copy-start | bytes 148
  15.6 28.0 %collective-permute-start.3 = (f32[16,136,128]{2,1,0:T(8,128)}, f32[16,136,128]{2,1,0:T(8,128)S(1)}, u32[]{:S(2)}, u32[]{:S(2)}) collective-permute-start(f32[16,136,128]{2,1,0:T(8,128)} %get-tuple-element.33), channel_id=1, source_target_pairs={{16,0},{32,16},{48,32},{64,48},{80,64},{96,80},{112,96},{17,1},{33... | collective-permute-start | bytes 3342344 | tf_op jit(solution)/shard_map/ppermute | solution.py:699
  17.6 16.3 %copy-start.8 = (s32[256]{0:T(256)S(1)}, s32[256]{0:T(256)}, u32[]{:S(2)}) copy-start(s32[256]{0:T(256)} %param.13) | copy-start | bytes 3076
  17.6 26.0 %copy-start.1 = (s32[4,16,6]{1,0,2:T(4,128)S(1)}, s32[4,16,6]{1,0,2:T(4,128)}, u32[]{:S(2)}) copy-start(s32[4,16,6]{1,0,2:T(4,128)} %param.10) | copy-start | bytes 4612
  17.7 26.0 %copy-start.2 = (s32[4,16]{1,0:T(4,128)S(1)}, s32[4,16]{1,0:T(4,128)}, u32[]{:S(2)}) copy-start(s32[4,16]{1,0:T(4,128)} %refs_0_.1) | copy-start | bytes 772
  17.7 26.0 %copy-start.3 = (s32[4,16]{1,0:T(4,128)S(1)}, s32[4,16]{1,0:T(4,128)}, u32[]{:S(2)}) copy-start(s32[4,16]{1,0:T(4,128)} %refs_2_.1) | copy-start | bytes 772
  19.4 24.2 %collective-permute-start.4 = (f32[848,128]{1,0:T(8,128)}, f32[848,128]{1,0:T(8,128)S(1)}, u32[]{:S(2)}, u32[]{:S(2)}) collective-permute-start(f32[848,128]{1,0:T(8,128)} %pad_maximum_fusion), channel_id=1, source_target_pairs={{0,1},{1,2},{2,3},{3,4},{4,5},{5,6},{6,7},{7,8},{8,9},{9,10},{10,1... | collective-permute-start | bytes 1302536 | tf_op jit(solution)/shard_map/ppermute | solution.py:699
  21.5 22.1 %collective-permute-start.5 = (f32[848,128]{1,0:T(8,128)}, f32[848,128]{1,0:T(8,128)S(1)}, u32[]{:S(2)}, u32[]{:S(2)}) collective-permute-start(f32[848,128]{1,0:T(8,128)} %pad_maximum_fusion.1), channel_id=1, source_target_pairs={{1,0},{2,1},{3,2},{4,3},{5,4},{6,5},{7,6},{8,7},{9,8},{10,9},{11,1... | collective-permute-start | bytes 1302536 | tf_op jit(solution)/shard_map/ppermute | solution.py:699
  27.4 16.2 %all-to-all-start = ((f32[128,1,12]{2,1,0:T(1,128)}), f32[128,1,12]{2,1,0:T(1,128)S(1)}, u32[]{:S(2)}, u32[]{:S(2)}) async-start(f32[128,1,12]{2,1,0:T(1,128)} %broadcast_in_dim.8), calls=%async_computation | async-start | bytes 131072 | tf_op jit(solution)/shard_map/all_to_all | solution.py:725
  43.7 31.3 %copy-start.6 = (s32[512]{0:T(512)S(1)}, s32[512]{0:T(512)}, u32[]{:S(2)}) copy-start(s32[512]{0:T(512)} %param.15) | copy-start | bytes 6148
  70.7 15.8 %all-to-all-start.1 = ((f32[128,4,128]{2,1,0:T(4,128)}), f32[128,4,128]{2,1,0:T(4,128)S(1)}, u32[]{:S(2)}, u32[]{:S(2)}) async-start(f32[128,4,128]{2,1,0:T(4,128)} %bitcast.13), calls=%async_computation.1 | async-start | bytes 524288 | tf_op jit(solution)/shard_map/all_to_all | solution.py:737
  95.4 10.1 %collective-permute-start.8 = (f32[2,152,128]{2,1,0:T(8,128)S(1)}, f32[2,152,128]{2,1,0:T(8,128)S(1)}, u32[]{:S(2)}, u32[]{:S(2)}) collective-permute-start(f32[2,152,128]{2,1,0:T(8,128)S(1)} %get-tuple-element.40), channel_id=1, source_target_pairs={{0,16},{16,32},{32,48},{48,64},{64,80},{80,96},{96,112},{1,17},{17... | collective-permute-start | bytes 466952 | tf_op jit(solution)/shard_map/ppermute | solution.py:699
  98.0 7.5 %collective-permute-start.9 = (f32[2,152,128]{2,1,0:T(8,128)S(1)}, f32[2,152,128]{2,1,0:T(8,128)S(1)}, u32[]{:S(2)}, u32[]{:S(2)}) collective-permute-start(f32[2,152,128]{2,1,0:T(8,128)S(1)} %get-tuple-element.41), channel_id=1, source_target_pairs={{16,0},{32,16},{48,32},{64,48},{80,64},{96,80},{112,96},{17,1},{33... | collective-permute-start | bytes 466952 | tf_op jit(solution)/shard_map/ppermute | solution.py:699
  99.9 21.0 %collective-permute-start.6 = (f32[16,136,128]{2,1,0:T(8,128)}, f32[16,136,128]{2,1,0:T(8,128)S(1)}, u32[]{:S(2)}, u32[]{:S(2)}) collective-permute-start(f32[16,136,128]{2,1,0:T(8,128)} %get-tuple-element.37), channel_id=1, source_target_pairs={{0,16},{16,32},{32,48},{48,64},{64,80},{80,96},{96,112},{1,17},{17... | collective-permute-start | bytes 3342344 | tf_op jit(solution)/shard_map/ppermute | solution.py:699
  103.6 17.3 %collective-permute-start.7 = (f32[16,136,128]{2,1,0:T(8,128)}, f32[16,136,128]{2,1,0:T(8,128)S(1)}, u32[]{:S(2)}, u32[]{:S(2)}) collective-permute-start(f32[16,136,128]{2,1,0:T(8,128)} %get-tuple-element.38), channel_id=1, source_target_pairs={{16,0},{32,16},{48,32},{64,48},{80,64},{96,80},{112,96},{17,1},{33... | collective-permute-start | bytes 3342344 | tf_op jit(solution)/shard_map/ppermute | solution.py:699
  105.6 15.3 %collective-permute-start.10 = (f32[848,128]{1,0:T(8,128)S(1)}, f32[848,128]{1,0:T(8,128)S(1)}, u32[]{:S(2)}, u32[]{:S(2)}) collective-permute-start(f32[848,128]{1,0:T(8,128)S(1)} %pad_maximum_fusion.2), channel_id=1, source_target_pairs={{0,1},{1,2},{2,3},{3,4},{4,5},{5,6},{6,7},{7,8},{8,9},{9,10},{10,1... | collective-permute-start | bytes 1302536 | tf_op jit(solution)/shard_map/ppermute | solution.py:699
  106.1 14.8 %collective-permute-start.11 = (f32[848,128]{1,0:T(8,128)S(1)}, f32[848,128]{1,0:T(8,128)S(1)}, u32[]{:S(2)}, u32[]{:S(2)}) collective-permute-start(f32[848,128]{1,0:T(8,128)S(1)} %pad_maximum_fusion.3), channel_id=1, source_target_pairs={{1,0},{2,1},{3,2},{4,3},{5,4},{6,5},{7,6},{8,7},{9,8},{10,9},{11,1... | collective-permute-start | bytes 1302536 | tf_op jit(solution)/shard_map/ppermute | solution.py:699
  110.7 2.2 %copy-start = (f32[64,128,128]{2,1,0:T(8,128)S(1)}, f32[64,128,128]{2,1,0:T(8,128)}, u32[]{:S(2)}) copy-start(f32[64,128,128]{2,1,0:T(8,128)} %get-tuple-element.43.refs_1_.refs_3_) | copy-start | bytes 12582916

commit v6 on v5

--- a/solution.py
+++ b/solution.py
@@ -308,7 +308,7 @@
             pltpu.SemaphoreType.DMA((2 * rows,)),
             pltpu.SemaphoreType.DMA((rows - 2,)),
         ],
-        compiler_params=pltpu.CompilerParams(vmem_limit_bytes=47 * MIB),
+        compiler_params=pltpu.CompilerParams(vmem_limit_bytes=50 * MIB),
         cost_estimate=pl.CostEstimate(flops=5 * 10**9, bytes_accessed=16 * MIB, transcendentals=0),
     )(*scalars, codes, cells)
 

time: 140 us -> 140 us (level)
  local copies, waits for them, and re-layouts: 3.31 us -> 1.13 us
    unnamed x18 -> x16, local copies, waits for them, and re-layouts: 2.24 us -> 0.05 us
  transfers between devices with their start and end apart: 14 -> 14, of which waited for: 2 -> 3; matrix products, arithmetic and copies ran while one was open for 3% -> 3% of each run, Pallas kernels for 6% -> 6%
where the time goes in v6:
time: 140 us; the launch traced here: 139 us
  Pallas kernels  68.1 us (49%)
  starting transfers between devices  44.3 us (32%)
  waiting for transfers between devices  22 us (16%)
  other arithmetic  2.81 us (2%)
    pallas_call x2, Pallas kernels, step_call(): pl.pallas_call(functools.partial(step_kernel, rows, cols, counts is not N...  45.7 us
    ppermute x6, starting transfers between devices, swap(): lax.ppermute(down, axis, [(j, i) for i, j in pairs])  17.3 us
    ppermute x6, starting transfers between devices, swap(): lax.ppermute(up, axis, pairs)  16.3 us
    all_to_all x1, waiting for transfers between devices, local(): lax.all_to_all(outgoing.reshape(ranks, capacity, fields), AXES, 0, 0, til...  11.3 us
    all_to_all x1, waiting for transfers between devices, local(): told = lax.all_to_all(told, AXES, 0, 0, tiled=True)  9.62 us
    pallas_call x1, Pallas kernels, own_call(): pl.pallas_call(functools.partial(own_kernel, rows, cols, counts is not No...  8.85 us
    pallas_call x1, Pallas kernels, insert(): pl.pallas_call(functools.partial(insert_kernel, rows, cols), out_shape=(j...  8.81 us
    all_to_all x1, starting transfers between devices, local(): told = lax.all_to_all(told, AXES, 0, 0, tiled=True)  6.44 us
  transfers between devices with their start and end apart: 14, of which 3 were waited for; matrix products, arithmetic and copies ran while one was open for 3% of the time, Pallas kernels for 6%

profile of v6, /device:TPU:1, one launch (start us, length us, event | category | flops | bytes accessed | tf_op | source)
XLA Modules:
  0.0 139.4 jit_solution(15805068600983589698)
XLA Ops:
  0.6 4.7 %shard_map.95 = (f32[2,152,128]{2,1,0:T(8,128)}, f32[2,152,128]{2,1,0:T(8,128)}, f32[16,136,128]{2,1,0:T(8,128)}, f32[16,136,128]{2,1,0:T(8,128)}, f32[4,136,128]{2,1,0:T(8,128)}, /*index=5*/f32[4,136,128]{2,1,0:T(8,128)}) custom-call(s32[4,16]{1,0:T(4,128)} %refs_0_.1, s32[6,4,16]{2,1,0:T(4,128)} %bitcast.38, f32[64,128,128]{2,1,0:T(8,128)} %bitcast.43), custom_call_target="tpu_custom_call" | custom-call | tf_op jit(solution)/shard_map/pallas_call | solution.py:142
  5.4 4.6 %collective-permute-start = (f32[2,152,128]{2,1,0:T(8,128)}, f32[2,152,128]{2,1,0:T(8,128)S(1)}, u32[]{:S(2)}, u32[]{:S(2)}) collective-permute-start(f32[2,152,128]{2,1,0:T(8,128)} %get-tuple-element.28), channel_id=1, source_target_pairs={{0,16},{16,32},{32,48},{48,64},{64,80},{80,96},{96,112},{1,17},{17... | collective-permute-start | bytes 466952 | tf_op jit(solution)/shard_map/ppermute | solution.py:699
  10.0 1.9 %collective-permute-start.1 = (f32[2,152,128]{2,1,0:T(8,128)}, f32[2,152,128]{2,1,0:T(8,128)S(1)}, u32[]{:S(2)}, u32[]{:S(2)}) collective-permute-start(f32[2,152,128]{2,1,0:T(8,128)} %get-tuple-element.29), channel_id=1, source_target_pairs={{16,0},{32,16},{48,32},{64,48},{80,64},{96,80},{112,96},{17,1},{33... | collective-permute-start | bytes 466952 | tf_op jit(solution)/shard_map/ppermute | solution.py:699
  12.0 3.6 %collective-permute-start.2 = (f32[16,136,128]{2,1,0:T(8,128)}, f32[16,136,128]{2,1,0:T(8,128)S(1)}, u32[]{:S(2)}, u32[]{:S(2)}) collective-permute-start(f32[16,136,128]{2,1,0:T(8,128)} %get-tuple-element.32), channel_id=1, source_target_pairs={{0,16},{16,32},{32,48},{48,64},{64,80},{80,96},{96,112},{1,17},{17... | collective-permute-start | bytes 3342344 | tf_op jit(solution)/shard_map/ppermute | solution.py:699
  15.6 0.0 copy-start.4
  15.6 0.0 copy-start.6
  15.6 1.9 %collective-permute-start.3 = (f32[16,136,128]{2,1,0:T(8,128)}, f32[16,136,128]{2,1,0:T(8,128)S(1)}, u32[]{:S(2)}, u32[]{:S(2)}) collective-permute-start(f32[16,136,128]{2,1,0:T(8,128)} %get-tuple-element.33), channel_id=1, source_target_pairs={{16,0},{32,16},{48,32},{64,48},{80,64},{96,80},{112,96},{17,1},{33... | collective-permute-start | bytes 3342344 | tf_op jit(solution)/shard_map/ppermute | solution.py:699
  17.6 0.0 collective-permute-done
  17.6 0.0 copy-start.7
  17.6 0.0 collective-permute-done.1
  17.6 0.0 copy-start
  17.6 0.0 copy-start.1
  17.7 0.0 copy-start.2
  17.7 1.8 %pad_maximum_fusion = f32[848,128]{1,0:T(8,128)} fusion(f32[152,128]{1,0:T(8,128)S(1)} %get-tuple-element.59, f32[152,128]{1,0:T(8,128)S(1)} %get-tuple-element.57, f32[544,128]{1,0:T(8,128)} %bitcast.46), kind=kLoop, calls=%fused_computation | loop fusion | flops 217088 | bytes 868352 | tf_op jit(solution)/shard_map/concatenate | solution.py:708
  19.4 1.3 collective-permute-start.4
  20.7 0.8 pad_maximum_fusion.1
  21.5 4.9 %collective-permute-start.5 = (f32[848,128]{1,0:T(8,128)}, f32[848,128]{1,0:T(8,128)S(1)}, u32[]{:S(2)}, u32[]{:S(2)}) collective-permute-start(f32[848,128]{1,0:T(8,128)} %pad_maximum_fusion.1), channel_id=1, source_target_pairs={{1,0},{2,1},{3,2},{4,3},{5,4},{6,5},{7,6},{8,7},{9,8},{10,9},{11,1... | collective-permute-start | bytes 1302536 | tf_op jit(solution)/shard_map/ppermute | solution.py:699
  26.4 0.0 copy-done.4
  26.5 0.2 convert_reduce_fusion
  26.6 0.1 broadcast_in_dim.7
  26.7 0.7 broadcast_in_dim.8
  27.4 6.4 %all-to-all-start = ((f32[128,1,12]{2,1,0:T(1,128)}), f32[128,1,12]{2,1,0:T(1,128)S(1)}, u32[]{:S(2)}, u32[]{:S(2)}) async-start(f32[128,1,12]{2,1,0:T(1,128)} %broadcast_in_dim.8), calls=%async_computation | async-start | bytes 131072 | tf_op jit(solution)/shard_map/all_to_all | solution.py:725
  33.9 0.1 copy.14.refs_9_
  34.0 9.6 %all-to-all-done = f32[128,1,12]{2,1,0:T(1,128)S(1)} async-done(((f32[128,1,12]{2,1,0:T(1,128)}), f32[128,1,12]{2,1,0:T(1,128)S(1)}, u32[]{:S(2)}, u32[]{:S(2)}) %all-to-all-start) | async-done | bytes 6176 | tf_op jit(solution)/shard_map/all_to_all | solution.py:725
  43.6 0.0 collective-permute-done.4.refs_7_
  43.6 0.0 collective-permute-done.5.refs_8_
  43.6 0.0 collective-permute-done.2.refs_5_
  43.6 0.0 collective-permute-done.3.refs_6_
  43.7 0.0 copy-start.5
  43.7 27.0 %shard_map.96 = (f32[64,128,128]{2,1,0:T(8,128)}, f32[512,128]{1,0:T(8,128)}) custom-call(s32[4,16]{1,0:T(4,128)S(1)} %copy-done.1, s32[6,4,16]{2,1,0:T(4,128)S(1)} %bitcast.39, f32[128,12]{1,0:T(8,128)S(1)} %bitcast.34, s32[4,16]{1,0:T(4,128)S(1)} %copy-done.2, f32[64,128,128]{2,1,0:T(8,128)} %bitcast.44, ...), custom_call_target="tpu_custom_call" | custom-call | tf_op jit(solution)/shard_map/pallas_call | solution.py:616
  70.7 4.3 %all-to-all-start.1 = ((f32[128,4,128]{2,1,0:T(4,128)}), f32[128,4,128]{2,1,0:T(4,128)S(1)}, u32[]{:S(2)}, u32[]{:S(2)}) async-start(f32[128,4,128]{2,1,0:T(4,128)} %bitcast.13), calls=%async_computation.1 | async-start | bytes 524288 | tf_op jit(solution)/shard_map/all_to_all | solution.py:737
  75.0 0.1 copy.15.slots
  75.2 11.3 %all-to-all-done.1 = f32[128,4,128]{2,1,0:T(4,128)S(1)} async-done(((f32[128,4,128]{2,1,0:T(4,128)}), f32[128,4,128]{2,1,0:T(4,128)S(1)}, u32[]{:S(2)}, u32[]{:S(2)}) %all-to-all-start.1) | async-done | bytes 262176 | tf_op jit(solution)/shard_map/all_to_all | solution.py:737
  86.5 8.8 %shard_map.97 = (f32[64,128,128]{2,1,0:T(8,128)}, f32[2,152,128]{2,1,0:T(8,128)S(1)}, f32[2,152,128]{2,1,0:T(8,128)S(1)}, f32[16,136,128]{2,1,0:T(8,128)}, f32[1...) custom-call(s32[6,4,16]{2,1,0:T(4,128)S(1)} %bitcast.40, ...), custom_call_target="tpu_custom_call" | custom-call | tf_op jit(solution)/shard_map/pallas_call | solution.py:686
  95.3 2.6 %collective-permute-start.8 = (f32[2,152,128]{2,1,0:T(8,128)S(1)}, f32[2,152,128]{2,1,0:T(8,128)S(1)}, u32[]{:S(2)}, u32[]{:S(2)}) collective-permute-start(f32[2,152,128]{2,1,0:T(8,128)S(1)} %get-tuple-element.40), channel_id=1, source_target_pairs={{0,16},{16,32},{32,48},{48,64},{64,80},{80,96},{96,112},{1,17},{17... | collective-permute-start | bytes 466952 | tf_op jit(solution)/shard_map/ppermute | solution.py:699
  98.0 1.9 %collective-permute-start.9 = (f32[2,152,128]{2,1,0:T(8,128)S(1)}, f32[2,152,128]{2,1,0:T(8,128)S(1)}, u32[]{:S(2)}, u32[]{:S(2)}) collective-permute-start(f32[2,152,128]{2,1,0:T(8,128)S(1)} %get-tuple-element.41), channel_id=1, source_target_pairs={{16,0},{32,16},{48,32},{64,48},{80,64},{96,80},{112,96},{17,1},{33... | collective-permute-start | bytes 466952 | tf_op jit(solution)/shard_map/ppermute | solution.py:699
  99.9 3.6 %collective-permute-start.6 = (f32[16,136,128]{2,1,0:T(8,128)}, f32[16,136,128]{2,1,0:T(8,128)S(1)}, u32[]{:S(2)}, u32[]{:S(2)}) collective-permute-start(f32[16,136,128]{2,1,0:T(8,128)} %get-tuple-element.37), channel_id=1, source_target_pairs={{0,16},{16,32},{32,48},{48,64},{64,80},{80,96},{96,112},{1,17},{17... | collective-permute-start | bytes 3342344 | tf_op jit(solution)/shard_map/ppermute | solution.py:699
  103.5 1.9 %collective-permute-start.7 = (f32[16,136,128]{2,1,0:T(8,128)}, f32[16,136,128]{2,1,0:T(8,128)S(1)}, u32[]{:S(2)}, u32[]{:S(2)}) collective-permute-start(f32[16,136,128]{2,1,0:T(8,128)} %get-tuple-element.38), channel_id=1, source_target_pairs={{16,0},{32,16},{48,32},{64,48},{80,64},{96,80},{112,96},{17,1},{33... | collective-permute-start | bytes 3342344 | tf_op jit(solution)/shard_map/ppermute | solution.py:699
  105.5 0.0 collective-permute-done.8
  105.5 0.0 collective-permute-done.9
  105.6 0.4 collective-permute-start.10
  106.0 4.7 %collective-permute-start.11 = (f32[848,128]{1,0:T(8,128)S(1)}, f32[848,128]{1,0:T(8,128)S(1)}, u32[]{:S(2)}, u32[]{:S(2)}) collective-permute-start(f32[848,128]{1,0:T(8,128)S(1)} %pad_maximum_fusion.3), channel_id=1, source_target_pairs={{1,0},{2,1},{3,2},{4,3},{5,4},{6,5},{7,6},{8,7},{9,8},{10,9},{11,1... | collective-permute-start | bytes 1302536 | tf_op jit(solution)/shard_map/ppermute | solution.py:699
  110.7 8.9 %shard_map.98 = (bf16[160,128,128]{2,1,0:T(8,128)(2,1)}, bf16[160,32,128]{2,1,0:T(8,128)(2,1)S(1)}, bf16[64,768,128]{2,1,0:T(8,128)(2,1)}, f32[160,128]{1,0:T(8,...) custom-call(s32[6,4,16]{2,1,0:T(4,128)S(1)} %bitcast.41, f32[64,128,128]{2,1,0:T(8,128)} %get-tuple-element.43.refs_1_.refs_3_), custom_call_target="tpu_custom_call" | custom-call | flops 5000000000 | bytes 16777216 | tf_op jit(solution)/shard_map/pallas_call | solution.py:295
  119.6 0.0 collective-permute-done.10.refs_6_
  119.6 0.0 collective-permute-done.11.refs_7_
  119.6 0.0 collective-permute-done.6.refs_4_
  119.6 1.0 collective-permute-done.7.refs_5_
  120.6 18.7 %shard_map.99 = (f32[64,128,128]{2,1,0:T(8,128)}, f32[64,128]{1,0:T(8,128)}) custom-call(s32[6,4,16]{2,1,0:T(4,128)S(1)} %bitcast.42, f32[128,12]{1,0:T(8,128)S(1)} %bitcast.35, s32[4,16]{1,0:T(4,128)S(1)} %copy-done.2, f32[64,128,128]{2,1,0:T(8,128)} %get-tuple-element.43.refs_1_.refs_3_, f32[16,136,128]{2,1,0:T(8,128)S(1)} %collective-permute-done.6.refs_4_, ...), custom_call_target="tpu_custom_call" | custom-call | tf_op jit(solution)/shard_map/pallas_call | solution.py:616
  (15 shorter events, 0.1 us)
Async XLA Ops:
  5.4 15.4 %copy-start.3 = (f32[4,136,128]{2,1,0:T(8,128)S(1)}, f32[4,136,128]{2,1,0:T(8,128)}, u32[]{:S(2)}) copy-start(f32[4,136,128]{2,1,0:T(8,128)} %get-tuple-element.30) | copy-start | bytes 835588
  5.4 12.2 %collective-permute-start = (f32[2,152,128]{2,1,0:T(8,128)}, f32[2,152,128]{2,1,0:T(8,128)S(1)}, u32[]{:S(2)}, u32[]{:S(2)}) collective-permute-start(f32[2,152,128]{2,1,0:T(8,128)} %get-tuple-element.28), channel_id=1, source_target_pairs={{0,16},{16,32},{32,48},{48,64},{64,80},{80,96},{96,112},{1,17},{17... | collective-permute-start | bytes 466952 | tf_op jit(solution)/shard_map/ppermute | solution.py:699
  10.0 7.6 %collective-permute-start.1 = (f32[2,152,128]{2,1,0:T(8,128)}, f32[2,152,128]{2,1,0:T(8,128)S(1)}, u32[]{:S(2)}, u32[]{:S(2)}) collective-permute-start(f32[2,152,128]{2,1,0:T(8,128)} %get-tuple-element.29), channel_id=1, source_target_pairs={{16,0},{32,16},{48,32},{64,48},{80,64},{96,80},{112,96},{17,1},{33... | collective-permute-start | bytes 466952 | tf_op jit(solution)/shard_map/ppermute | solution.py:699
  12.0 31.7 %collective-permute-start.2 = (f32[16,136,128]{2,1,0:T(8,128)}, f32[16,136,128]{2,1,0:T(8,128)S(1)}, u32[]{:S(2)}, u32[]{:S(2)}) collective-permute-start(f32[16,136,128]{2,1,0:T(8,128)} %get-tuple-element.32), channel_id=1, source_target_pairs={{0,16},{16,32},{32,48},{48,64},{64,80},{80,96},{96,112},{1,17},{17... | collective-permute-start | bytes 3342344 | tf_op jit(solution)/shard_map/ppermute | solution.py:699
  15.6 10.8 %copy-start.4 = (s32[256,1]{0,1:T(1,128)S(1)}, s32[256,1]{0,1:T(1,128)}, u32[]{:S(2)}) copy-start(s32[256,1]{0,1:T(1,128)} %param.14) | copy-start | bytes 3076
  15.6 11.0 %copy-start.6 = (f32[4,3]{1,0:T(4,128)S(1)}, f32[4,3]{1,0:T(4,128)}, u32[]{:S(2)}) copy-start(f32[4,3]{1,0:T(4,128)} %param.12) | copy-start | bytes 148
  15.6 28.0 %collective-permute-start.3 = (f32[16,136,128]{2,1,0:T(8,128)}, f32[16,136,128]{2,1,0:T(8,128)S(1)}, u32[]{:S(2)}, u32[]{:S(2)}) collective-permute-start(f32[16,136,128]{2,1,0:T(8,128)} %get-tuple-element.33), channel_id=1, source_target_pairs={{16,0},{32,16},{48,32},{64,48},{80,64},{96,80},{112,96},{17,1},{33... | collective-permute-start | bytes 3342344 | tf_op jit(solution)/shard_map/ppermute | solution.py:699
  17.6 16.3 %copy-start.7 = (s32[256]{0:T(256)S(1)}, s32[256]{0:T(256)}, u32[]{:S(2)}) copy-start(s32[256]{0:T(256)} %param.13) | copy-start | bytes 3076
  17.6 26.0 %copy-start = (s32[4,16,6]{1,0,2:T(4,128)S(1)}, s32[4,16,6]{1,0,2:T(4,128)}, u32[]{:S(2)}) copy-start(s32[4,16,6]{1,0,2:T(4,128)} %param.10) | copy-start | bytes 4612
  17.6 26.0 %copy-start.1 = (s32[4,16]{1,0:T(4,128)S(1)}, s32[4,16]{1,0:T(4,128)}, u32[]{:S(2)}) copy-start(s32[4,16]{1,0:T(4,128)} %refs_0_.1) | copy-start | bytes 772
  17.7 26.0 %copy-start.2 = (s32[4,16]{1,0:T(4,128)S(1)}, s32[4,16]{1,0:T(4,128)}, u32[]{:S(2)}) copy-start(s32[4,16]{1,0:T(4,128)} %refs_2_.1) | copy-start | bytes 772
  19.4 24.2 %collective-permute-start.4 = (f32[848,128]{1,0:T(8,128)}, f32[848,128]{1,0:T(8,128)S(1)}, u32[]{:S(2)}, u32[]{:S(2)}) collective-permute-start(f32[848,128]{1,0:T(8,128)} %pad_maximum_fusion), channel_id=1, source_target_pairs={{0,1},{1,2},{2,3},{3,4},{4,5},{5,6},{6,7},{7,8},{8,9},{9,10},{10,1... | collective-permute-start | bytes 1302536 | tf_op jit(solution)/shard_map/ppermute | solution.py:699
  21.5 22.1 %collective-permute-start.5 = (f32[848,128]{1,0:T(8,128)}, f32[848,128]{1,0:T(8,128)S(1)}, u32[]{:S(2)}, u32[]{:S(2)}) collective-permute-start(f32[848,128]{1,0:T(8,128)} %pad_maximum_fusion.1), channel_id=1, source_target_pairs={{1,0},{2,1},{3,2},{4,3},{5,4},{6,5},{7,6},{8,7},{9,8},{10,9},{11,1... | collective-permute-start | bytes 1302536 | tf_op jit(solution)/shard_map/ppermute | solution.py:699
  27.4 16.2 %all-to-all-start = ((f32[128,1,12]{2,1,0:T(1,128)}), f32[128,1,12]{2,1,0:T(1,128)S(1)}, u32[]{:S(2)}, u32[]{:S(2)}) async-start(f32[128,1,12]{2,1,0:T(1,128)} %broadcast_in_dim.8), calls=%async_computation | async-start | bytes 131072 | tf_op jit(solution)/shard_map/all_to_all | solution.py:725
  43.7 31.3 %copy-start.5 = (s32[512]{0:T(512)S(1)}, s32[512]{0:T(512)}, u32[]{:S(2)}) copy-start(s32[512]{0:T(512)} %param.15) | copy-start | bytes 6148
  70.7 15.8 %all-to-all-start.1 = ((f32[128,4,128]{2,1,0:T(4,128)}), f32[128,4,128]{2,1,0:T(4,128)S(1)}, u32[]{:S(2)}, u32[]{:S(2)}) async-start(f32[128,4,128]{2,1,0:T(4,128)} %bitcast.13), calls=%async_computation.1 | async-start | bytes 524288 | tf_op jit(solution)/shard_map/all_to_all | solution.py:737
  95.3 10.1 %collective-permute-start.8 = (f32[2,152,128]{2,1,0:T(8,128)S(1)}, f32[2,152,128]{2,1,0:T(8,128)S(1)}, u32[]{:S(2)}, u32[]{:S(2)}) collective-permute-start(f32[2,152,128]{2,1,0:T(8,128)S(1)} %get-tuple-element.40), channel_id=1, source_target_pairs={{0,16},{16,32},{32,48},{48,64},{64,80},{80,96},{96,112},{1,17},{17... | collective-permute-start | bytes 466952 | tf_op jit(solution)/shard_map/ppermute | solution.py:699
  98.0 7.5 %collective-permute-start.9 = (f32[2,152,128]{2,1,0:T(8,128)S(1)}, f32[2,152,128]{2,1,0:T(8,128)S(1)}, u32[]{:S(2)}, u32[]{:S(2)}) collective-permute-start(f32[2,152,128]{2,1,0:T(8,128)S(1)} %get-tuple-element.41), channel_id=1, source_target_pairs={{16,0},{32,16},{48,32},{64,48},{80,64},{96,80},{112,96},{17,1},{33... | collective-permute-start | bytes 466952 | tf_op jit(solution)/shard_map/ppermute | solution.py:699
  99.9 19.7 %collective-permute-start.6 = (f32[16,136,128]{2,1,0:T(8,128)}, f32[16,136,128]{2,1,0:T(8,128)S(1)}, u32[]{:S(2)}, u32[]{:S(2)}) collective-permute-start(f32[16,136,128]{2,1,0:T(8,128)} %get-tuple-element.37), channel_id=1, source_target_pairs={{0,16},{16,32},{32,48},{48,64},{64,80},{80,96},{96,112},{1,17},{17... | collective-permute-start | bytes 3342344 | tf_op jit(solution)/shard_map/ppermute | solution.py:699
  103.5 17.0 %collective-permute-start.7 = (f32[16,136,128]{2,1,0:T(8,128)}, f32[16,136,128]{2,1,0:T(8,128)S(1)}, u32[]{:S(2)}, u32[]{:S(2)}) collective-permute-start(f32[16,136,128]{2,1,0:T(8,128)} %get-tuple-element.38), channel_id=1, source_target_pairs={{16,0},{32,16},{48,32},{64,48},{80,64},{96,80},{112,96},{17,1},{33... | collective-permute-start | bytes 3342344 | tf_op jit(solution)/shard_map/ppermute | solution.py:699
  105.6 14.0 %collective-permute-start.10 = (f32[848,128]{1,0:T(8,128)S(1)}, f32[848,128]{1,0:T(8,128)S(1)}, u32[]{:S(2)}, u32[]{:S(2)}) collective-permute-start(f32[848,128]{1,0:T(8,128)S(1)} %pad_maximum_fusion.2), channel_id=1, source_target_pairs={{0,1},{1,2},{2,3},{3,4},{4,5},{5,6},{6,7},{7,8},{8,9},{9,10},{10,1... | collective-permute-start | bytes 1302536 | tf_op jit(solution)/shard_map/ppermute | solution.py:699
  106.0 13.6 %collective-permute-start.11 = (f32[848,128]{1,0:T(8,128)S(1)}, f32[848,128]{1,0:T(8,128)S(1)}, u32[]{:S(2)}, u32[]{:S(2)}) collective-permute-start(f32[848,128]{1,0:T(8,128)S(1)} %pad_maximum_fusion.3), channel_id=1, source_target_pairs={{1,0},{2,1},{3,2},{4,3},{5,4},{6,5},{7,6},{8,7},{9,8},{10,9},{11,1... | collective-permute-start | bytes 1302536 | tf_op jit(solution)/shard_map/ppermute | solution.py:699
